TPU v7x, 256 devices: a whole 4x4x8 slice. The times are simulated.
256 devices in a mesh: dp: 4 (over x), expert: 64 (over y, z, core).
Axes of the slice: x: 4, y: 4, z: 8, core: 2. Of those that a mesh axis runs over, the one named last changes fastest.
Arguments:
- tokens: bfloat16 [4096, 3584], P(('dp', 'expert')), may hold values from -6 to 6
- out_grad: bfloat16 [4096, 3584], P(('dp', 'expert')), may hold values from -6 to 6
- route_ids: int32 [4096, 8], P(('dp', 'expert')), may hold values from 0 to 127, all different within a row; in each aligned block of 16 rows (0 to 15, 16 to 31, ...) at most 2 rows name the same one
- route_probs: float32 [4096, 8], P(('dp', 'expert')), may hold values from 0.02 to 0.5
- w_gate: bfloat16 [128, 3584, 1024], P('expert', None, 'dp'), may hold values from -0.09375 to 0.09375
- w_up: bfloat16 [128, 3584, 1024], P('expert', None, 'dp'), may hold values from -0.09375 to 0.09375
- w_down: bfloat16 [128, 1024, 3584], P('expert', 'dp'), may hold values from -0.1875 to 0.1875
Outputs:
- in_grad: bfloat16 [4096, 3584], P(('dp', 'expert'))
Inputs may be any that keep to these rules, and one draw needn't show every extreme that they name: `route_ids`: the 8 ids of a token differ. Among the tokens of one device (aligned blocks of 16 rows) no expert is named more than 2 times, and in every draw some expert is named exactly 2 times there.
All inputs are finite; a program needn't handle non-finite values.
Results may differ from a plain program's by a relative error of at most 0.015.
Values may be sent and summed in bfloat16 or wider, within the bound.
No kernel may reach another device: no remote copies, remote signals or barrier semaphores. Data moves between devices by JAX's collectives and lax.ppermute only.
A program may use at most 128 MiB of HBM per device.

v0:
```python
import jax
import jax.numpy as jnp
from jax import lax
from jax.sharding import PartitionSpec as P

TOPK = 8


def slot_matches(flat_ids, experts, capacity):
    onehot = (flat_ids[:, None] == jnp.arange(experts, dtype=jnp.int32)[None, :]).astype(jnp.int32)
    earlier = jnp.cumsum(onehot, axis=0) - onehot
    slot_rank = jnp.sum(earlier * onehot, axis=1)
    slot_of = flat_ids * capacity + slot_rank
    return slot_of[None, :] == jnp.arange(experts * capacity, dtype=jnp.int32)[:, None]


def select_matrix(matches, tok_count):
    return jnp.sum(matches.reshape(matches.shape[0], tok_count, TOPK).astype(jnp.float32), axis=2)


def build_tiles(token_rows, grad_rows, matches, flat_probs):
    select = select_matrix(matches, token_rows.shape[0]).astype(jnp.bfloat16)
    slot_scale = jnp.sum(jnp.where(matches, flat_probs[None, :], 0.0), axis=1)
    x_rows = jnp.dot(select, token_rows, preferred_element_type=jnp.float32).astype(jnp.bfloat16)
    g_rows = (
        jnp.dot(select, grad_rows, preferred_element_type=jnp.float32) * slot_scale[:, None]
    ).astype(jnp.bfloat16)
    return jnp.stack([x_rows, g_rows])


def expert_grads(tiles, w_gate, w_up, w_down):
    x_rows = tiles[:, 0]
    g_rows = tiles[:, 1]
    gate_pre = jnp.einsum("nsecd,edh->nsech", x_rows, w_gate, preferred_element_type=jnp.float32)
    up_pre = jnp.einsum("nsecd,edh->nsech", x_rows, w_up, preferred_element_type=jnp.float32)
    hidden_grad = jnp.einsum("nsecd,ehd->nsech", g_rows, w_down, preferred_element_type=jnp.float32)
    sigmoid_a = jax.nn.sigmoid(gate_pre)
    gate_grad = (hidden_grad * up_pre * sigmoid_a * (1.0 + gate_pre * (1.0 - sigmoid_a))).astype(
        jnp.bfloat16
    )
    up_grad = (hidden_grad * gate_pre * sigmoid_a).astype(jnp.bfloat16)
    partial_value = jnp.einsum(
        "nsech,edh->nsecd", gate_grad, w_gate, preferred_element_type=jnp.float32
    )
    partial_value = partial_value + jnp.einsum(
        "nsech,edh->nsecd", up_grad, w_up, preferred_element_type=jnp.float32
    )
    return partial_value.astype(jnp.bfloat16)


def on_device(tokens, out_grad, route_ids, route_probs, w_gate, w_up, w_down):
    columns = lax.axis_size("expert")
    local_experts = w_gate.shape[0]
    experts = local_experts * columns
    tok_count, width = tokens.shape
    capacity = max(2, 2 * tok_count * TOPK // experts)
    slots = experts * capacity
    tile_shape = (2, columns, local_experts, capacity, width)
    own_matches = slot_matches(route_ids.reshape(-1), experts, capacity)
    tiles = build_tiles(tokens, out_grad, own_matches, route_probs.reshape(-1)).reshape(
        (1,) + tile_shape
    )
    received = lax.all_to_all(tiles, "expert", split_axis=2, concat_axis=2, tiled=True)
    partials = expert_grads(
        lax.all_gather(received, "dp", axis=0, tiled=True), w_gate, w_up, w_down
    )
    summed = lax.psum_scatter(
        partials.astype(jnp.float32).astype(jnp.bfloat16), "dp", scatter_dimension=0, tiled=True
    ).astype(jnp.float32)
    returned = lax.all_to_all(
        summed.astype(jnp.bfloat16), "expert", split_axis=1, concat_axis=1, tiled=True
    ).astype(summed.dtype)
    own_select = select_matrix(own_matches, tok_count)
    result = jnp.dot(own_select.T, returned.reshape(slots, width), precision=lax.Precision.HIGHEST)
    return result.astype(jnp.bfloat16)


def solution(mesh):
    placed = (
        P(("dp", "expert"), None),
        P(("dp", "expert"), None),
        P(("dp", "expert"), None),
        P(("dp", "expert"), None),
        P("expert", None, "dp"),
        P("expert", None, "dp"),
        P("expert", "dp", None),
    )
    return jax.shard_map(
        on_device, mesh=mesh, in_specs=placed, out_specs=P(("dp", "expert"), None), check_vma=False
    )
```

profile of v0, /device:TPU:1, one launch (start us, length us, event | category | flops | bytes accessed | tf_op | source)
XLA Modules:
  0.0 523.0 jit_solution(11787229914710495954)
XLA Ops:
  6.5 0.0 copy-start
  6.5 0.0 copy-start.4
  6.5 0.0 all-gather.2.cloned.1.call-start
  6.5 0.8 copy.26
  7.3 0.1 eq.35
  7.4 0.1 fusion.33
  7.5 0.2 reduce_window_sum.11
  7.7 0.2 select_reduce_fusion.1
  7.9 0.1 reduce_sum.34
  8.0 0.1 convert_reduce_fusion
  8.1 0.8 copy.28
  8.9 0.1 broadcast_in_dim.18
  9.0 0.1 select_reduce_fusion
  9.1 0.0 copy-done
  9.1 1.9 fusion.4
  11.0 3.9 stack.10
  14.9 0.0 copy-done.4
  14.9 1.9 convolution_convert_fusion
  16.8 4.7 stack.9
  21.6 6.4 %pad_maximum_fusion = bf16[1,2,64,2,2,3584]{5,4,0,3,1,2:T(2,128)(2,1)S(1)} fusion(bf16[1,1,64,2,2,3584]{5,4,0,3,1,2:T(2,128)(2,1)S(1)} %bitcast.88, bf16[1,1,64,2,2,3584]{5,4,0,3,1,2:T(2,128)(2,1)} %bitcast.89), kind=kLoop, calls=%fused_computation.11 | loop fusion | flops 1835008 | bytes 7340032 | tf_op jit(solution)/shard_map/stack | solution.py:28
  28.0 97.7 %all_to_all.10 = bf16[1,2,64,2,2,3584]{5,4,0,3,1,2:T(2,128)(2,1)S(1)} all-to-all(bf16[1,2,64,2,2,3584]{5,4,0,3,1,2:T(2,128)(2,1)S(1)} %pad_maximum_fusion), channel_id=1, replica_groups=mesh['dp'=4,'expert'=64] {'expert'}, dimensions={2} | all-to-all | bytes 7340032 | tf_op jit(solution)/shard_map/all_to_all | solution.py:63
  125.7 2.9 copy.31
  128.5 0.0 all-gather.2.cloned.1.call-update
  128.6 0.2 all-reduce.3.cloned.1.call-start
  128.8 135.5 %all-gather.2.cloned.1.call-done = bf16[4,2,64,2,2,3584]{5,2,4,0,3,1:T(8,128)(2,1)} async-done(((bf16[1,2,64,2,2,3584]{5,2,4,0,3,1:T(8,128)(2,1)}), bf16[4,2,64,2,2,3584]{5,2,4,0,3,1:T(8,128)(2,1)}) %all-gather.2.cloned.1.call-update) | async-done | bytes 14680080 | tf_op jit(solution)/shard_map/all_gather | solution.py:65
  264.3 0.0 copy-start.5
  264.3 6.3 %fusion.14 = f32[4,64,2,2,256]{4,1,3,0,2:T(8,128)S(1)} fusion(bf16[2,3584,256]{2,1,0:T(8,128)(2,1)} %param.11, bf16[4,2,64,2,2,3584]{5,2,4,0,3,1:T(8,128)(2,1)} %all-gather.2.cloned.1.call-done), kind=kOutput, calls=%fused_computation.19 | convolution fusion | flops 1879048192 | bytes 12058624 | tf_op jit(solution)/shard_map/nsecd,edh->nsech/dot_general | solution.py:34
  270.7 2.0 copy-done.5
  272.6 0.0 copy-start.3
  272.6 4.3 fusion.17
  276.9 0.0 copy-done.3
  276.9 0.0 copy-start.2
  276.9 5.5 %fusion.29 = bf16[4,64,2,2,256]{4,1,3,0,2:T(8,128)(2,1)S(1)} fusion(f32[4,64,2,2,256]{4,1,3,0,2:T(8,128)S(1)} %fusion.17, bf16[2,3584,256]{2,1,0:T(8,128)(2,1)S(1)} %copy-done.3, bf16[4,2,64,2,2,3584]{5,2,4,0,3,1:T(8,128)(2,1)} %all-gather.2.cloned.1.call-done, f32[4,64,2,2,256]{4,1,3,0,2:T(8,128)S(1)} %fusion.14), kind=kOutput, calls=%fused_computation.24 | convolution fusion | flops 1881669632 | bytes 13631488 | tf_op jit(solution)/shard_map/nsecd,edh->nsech/dot_general | solution.py:35
  282.4 0.0 copy-done.2
  282.4 7.3 %fusion.5 = f32[2,4,64,2,3584]{4,2,3,1,0:T(8,128)} fusion(bf16[4,64,2,2,256]{4,1,3,0,2:T(8,128)(2,1)S(1)} %fusion.29, bf16[2,3584,256]{2,1,0:T(8,128)(2,1)S(1)} %copy-done.2), kind=kOutput, calls=%fused_computation.12 | convolution fusion | flops 1879048192 | bytes 18874368 | tf_op jit(solution)/shard_map/nsech,edh->nsecd/dot_general | solution.py:42
  289.8 11.3 %fusion.1 = bf16[4,64,2,2,3584]{4,1,3,0,2:T(8,128)(2,1)} fusion(f32[2,4,64,2,3584]{4,2,3,1,0:T(8,128)} %fusion.5, bf16[2,3584,256]{2,1,0:T(8,128)(2,1)} %param.12, f32[4,64,2,2,256]{4,1,3,0,2:T(8,128)S(1)} %fusion.17, f32[4,64,2,2,256]{4,1,3,0,2:T(8,128)S(1)} %fusion.14), kind=kOutput, calls=%fused_computation.4 | convolution fusion | flops 1887961088 | bytes 27787264 | tf_op jit(solution)/shard_map/nsech,edh->nsecd/dot_general | solution.py:45
  301.1 0.0 copy-start.6
  301.1 0.0 all-reduce.3.cloned.1.call-update
  301.1 0.6 copy-done.6
  301.8 0.6 dynamic-slice
  302.4 148.9 %all-reduce.3.cloned.1.call-done = bf16[4,64,2,2,3584]{4,1,3,0,2:T(8,128)(2,1)} async-done(((bf16[4,64,2,2,3584]{4,1,3,0,2:T(8,128)(2,1)}), bf16[4,64,2,2,3584]{4,1,3,0,2:T(8,128)(2,1)}) %all-reduce.3.cloned.1.call-update) | async-done | bytes 7340048
  451.3 2.3 constant_dynamic-slice_fusion
  453.6 1.9 copy.32
  455.5 0.0 copy-start.1
  455.5 56.1 %all_to_all.11 = bf16[1,64,2,2,3584]{4,3,0,2,1:T(2,128)(2,1)S(1)} all-to-all(bf16[1,64,2,2,3584]{4,3,0,2,1:T(2,128)(2,1)S(1)} %copy.32), channel_id=1, replica_groups=mesh['dp'=4,'expert'=64] {'expert'}, dimensions={1} | all-to-all | bytes 3670016 | tf_op jit(solution)/shard_map/all_to_all | solution.py:70
  511.6 1.7 reshape.31
  513.2 3.0 convolution_convert_fusion.1
  516.2 0.0 copy-done.1
  (2 shorter events, 0.0 us)
Async XLA Ops:
  6.5 2.5 copy-start
  6.5 8.4 %copy-start.4 = (bf16[16,3584]{1,0:T(8,128)(2,1)S(1)}, bf16[16,3584]{1,0:T(8,128)(2,1)}, u32[]{:S(2)}) copy-start(bf16[16,3584]{1,0:T(8,128)(2,1)} %param.7) | copy-start | bytes 344068
  6.5 257.8 %all-gather.2.cloned.1.call-start = ((), (), s32[]{:S(2)}) async-start(), calls=%async_computation.2 | async-start | bytes 18350080 | tf_op jit(solution)/shard_map/all_gather | solution.py:65
  128.6 322.8 %all-reduce.3.cloned.1.call-start = ((), (), s32[]{:S(2)}) async-start(), calls=%async_computation.3 | async-start | bytes 14680064
  264.3 8.3 %copy-start.5 = (bf16[4,2,64,2,2,3584]{5,2,4,0,3,1:T(8,128)(2,1)S(1)}, bf16[4,2,64,2,2,3584]{5,2,4,0,3,1:T(8,128)(2,1)}, u32[]{:S(2)}) copy-start(bf16[4,2,64,2,2,3584]{5,2,4,0,3,1:T(8,128)(2,1)} %all-gather.2.cloned.1.call-done) | copy-start | bytes 44040196
  272.6 4.3 copy-start.3
  276.9 5.5 %copy-start.2 = (bf16[2,3584,256]{2,1,0:T(8,128)(2,1)S(1)}, bf16[2,3584,256]{2,1,0:T(8,128)(2,1)}, u32[]{:S(2)}) copy-start(bf16[2,3584,256]{2,1,0:T(8,128)(2,1)} %param.11) | copy-start | bytes 11010052
  301.1 0.7 copy-start.6
  455.5 60.7 %copy-start.1 = (bf16[16,3584]{1,0:T(8,128)(2,1)S(1)}, bf16[16,3584]{1,0:T(8,128)(2,1)}, u32[]{:S(2)}) copy-start(bf16[16,3584]{1,0:T(8,128)(2,1)} %param.8) | copy-start | bytes 344068
Sparse Core Ops, SparseCore 0:
  128.7 135.6 all-gather.1
  301.2 150.0 all-reduce.2
where the time goes:
time: 523 us
  waiting for transfers between devices  285 us (54%)
  blocking collectives  154 us (29%)
  matrix products  41.6 us (8%)
  local copies, waits for them, and re-layouts  22.3 us (4%)
  between operations  13.5 us (3%)
  other arithmetic  7.1 us (1%)
    unnamed x3, waiting for transfers between devices  149 us
    all_gather x1, waiting for transfers between devices, on_device(): lax.all_gather(received, 'dp', axis=0, tiled=True)  136 us
    all_to_all x1, blocking collectives, on_device(): lax.all_to_all(tiles, 'expert', split_axis=2, concat_axis=2, tiled=True)  97.7 us
    all_to_all x1, blocking collectives, on_device(): lax.all_to_all(summed.astype(jnp.bfloat16), 'expert', split_axis=1, conca...  56.1 us
    dot_general x1, matrix products, expert_grads(): jnp.einsum('nsech,edh->nsecd', up_grad, w_up, preferred_element_type=jnp....  11.3 us
  transfers between devices with their start and end apart: 2, of which 2 were waited for; matrix products, arithmetic and copies ran while one was open for 0% of the time, Pallas kernels for 0%

commit v1 on v0

v1 whole, which is shorter than its diff:
```python
import jax
import jax.numpy as jnp
from jax import lax
from jax.experimental import pallas as pl
from jax.experimental.pallas import tpu as pltpu
from jax.sharding import PartitionSpec as P

CAP = 2
LANES = 128
BLOCK = 256
CHUNKS = 2
NT = (((1,), (1,)), ((), ()))


def slot_table(ids, probs, experts):
    tok_count = ids.shape[0]
    named = ids.T[None, :, :] == jnp.arange(experts, dtype=jnp.int32)[:, None, None]
    mask = jnp.any(named, axis=1)
    scale = jnp.sum(jnp.where(named, probs.T[None, :, :], 0.0), axis=1)
    order = jnp.arange(tok_count, dtype=jnp.int32)
    before = (order[:, None] < order[None, :])[None, :, :]
    rank = jnp.sum((mask[:, :, None] & before).astype(jnp.int32), axis=1)
    slots = mask[:, None, :] & (rank[:, None, :] == jnp.arange(CAP, dtype=jnp.int32)[None, :, None])
    slot_scale = jnp.sum(jnp.where(slots, scale[:, None, :], 0.0), axis=2)
    return slots.reshape(experts * CAP, tok_count), slot_scale.reshape(experts * CAP)


def hidden_kernel(own_ref, right_ref, far_a_ref, far_b_ref, left_ref, w_ref, out_ref):
    width = w_ref.shape[2]
    half = own_ref.shape[0] // 2
    for e in range(2):
        rows = pl.ds(e * half, half)
        far = (far_a_ref, far_b_ref)[e]
        g = jnp.concatenate(
            [own_ref[rows, :width], right_ref[rows, :width], far[:, :width], left_ref[rows, :width]], axis=0
        )
        out_ref[e] = lax.dot_general(g, w_ref[e], NT, preferred_element_type=jnp.float32)


def hidden_grads(own, right, far_a, far_b, left, w_down):
    local_experts, units, width = w_down.shape
    rows = own.shape[0] // 2 * 4
    return pl.pallas_call(
        hidden_kernel,
        out_shape=jax.ShapeDtypeStruct((local_experts, rows, units), jnp.float32),
        in_specs=[pl.BlockSpec(memory_space=pltpu.VMEM)] * 6,
        out_specs=pl.BlockSpec(memory_space=pltpu.VMEM),
        cost_estimate=pl.CostEstimate(
            flops=2 * local_experts * rows * units * width, bytes_accessed=12 << 20, transcendentals=0
        ),
        name="hidden_grads",
    )(own, right, far_a, far_b, left, w_down)


def act_kernel(me_ref, x_ref, sel_ref, gate_ref, up_ref, hidden_ref, out_ref, picked):
    step = pl.program_id(0)
    blocks = pl.num_programs(0) // 4
    group, block = step // blocks, step % blocks
    rows = lax.dot_general(
        sel_ref[0], x_ref[...], (((1,), (0,)), ((), ())), preferred_element_type=jnp.float32
    ).astype(jnp.bfloat16)
    part = rows.shape[0] // 4
    for slot in range(4):
        at = pl.multiple_of(group * (blocks * part * CAP) + (slot % CAP) * (blocks * part) + block * part, 16)
        picked[slot // CAP, pl.ds(at, part), :] = rows[slot * part : (slot + 1) * part]

    @pl.when(step == pl.num_programs(0) - 1)
    def _():
        units = gate_ref.shape[2]
        for e in range(2):
            x = picked[e]
            gate_pre = jnp.dot(x, gate_ref[e], preferred_element_type=jnp.float32)
            up_pre = jnp.dot(x, up_ref[e], preferred_element_type=jnp.float32)
            hidden = hidden_ref[e]
            s = jax.nn.sigmoid(gate_pre)
            out_ref[e, :, :units] = (hidden * up_pre * s * (1.0 + gate_pre * (1.0 - s))).astype(jnp.bfloat16)
            out_ref[e, :, units:] = (hidden * gate_pre * s).astype(jnp.bfloat16)


def act_grads(me, x_all, sel, w_gate, w_up, hidden):
    local_experts, width, units = w_gate.shape
    steps, part, block = sel.shape
    rows = hidden.shape[1]
    blocks = steps // 4
    whole = lambda i, me: (0, 0, 0)
    return pl.pallas_call(
        act_kernel,
        out_shape=jax.ShapeDtypeStruct((local_experts, rows, 2 * units), jnp.bfloat16),
        grid_spec=pltpu.PrefetchScalarGridSpec(
            num_scalar_prefetch=1,
            grid=(steps,),
            in_specs=[
                pl.BlockSpec((block, width), lambda i, me: (lax.rem(me[0] + i // blocks, 4) * blocks + i % blocks, 0)),
                pl.BlockSpec((1, part, block), lambda i, me: (i, 0, 0)),
                pl.BlockSpec((local_experts, width, units), whole),
                pl.BlockSpec((local_experts, width, units), whole),
                pl.BlockSpec((local_experts, rows, units), whole),
            ],
            out_specs=pl.BlockSpec((local_experts, rows, 2 * units), whole),
            scratch_shapes=[pltpu.VMEM((local_experts, rows, width), jnp.bfloat16)],
        ),
        compiler_params=pltpu.CompilerParams(dimension_semantics=("arbitrary",)),
        cost_estimate=pl.CostEstimate(
            flops=2 * local_experts * rows * 2 * units * width + 2 * steps * part * block * width,
            bytes_accessed=40 << 20,
            transcendentals=local_experts * rows * units,
        ),
        name="act_grads",
    )(me, x_all, sel, w_gate, w_up, hidden)


def out_kernel(me_ref, h_ref, gate_ref, up_ref, out_ref):
    units = gate_ref.shape[2]
    for e in range(2):
        value = lax.dot_general(h_ref[e, :, :units], gate_ref[e], NT, preferred_element_type=jnp.float32)
        value = value + lax.dot_general(h_ref[e, :, units:], up_ref[e], NT, preferred_element_type=jnp.float32)
        value = value.astype(jnp.bfloat16)
        part = value.shape[0] // 4
        for r in range(4):
            out_ref[lax.rem(me_ref[0] + r, 4), e * part : (e + 1) * part, :] = value[r * part : (r + 1) * part]


def out_rows(me, h, w_gate, w_up, chunk, chunks, cols):
    local_experts, rows, _ = h.shape
    _, width, units = w_gate.shape
    per = width // chunks // cols
    first = chunk * per
    w_spec = pl.BlockSpec((local_experts, cols, units), lambda n, me: (0, first + n, 0))
    return pl.pallas_call(
        out_kernel,
        out_shape=jax.ShapeDtypeStruct((4, local_experts * rows // 4, width // chunks), jnp.bfloat16),
        grid_spec=pltpu.PrefetchScalarGridSpec(
            num_scalar_prefetch=1,
            grid=(per,),
            in_specs=[
                pl.BlockSpec((local_experts, rows, 2 * units), lambda n, me: (0, 0, 0)),
                w_spec,
                w_spec,
            ],
            out_specs=pl.BlockSpec((4, local_experts * rows // 4, cols), lambda n, me: (0, 0, n)),
        ),
        compiler_params=pltpu.CompilerParams(dimension_semantics=("arbitrary",)),
        cost_estimate=pl.CostEstimate(
            flops=2 * local_experts * rows * 2 * units * width // chunks, bytes_accessed=8 << 20, transcendentals=0
        ),
        name="out_rows",
    )(me, h, w_gate, w_up)


def on_device(tokens, out_grad, route_ids, route_probs, w_gate, w_up, w_down):
    columns = lax.axis_size("expert")
    local_experts = w_gate.shape[0]
    experts = local_experts * columns
    tok_count, width = tokens.shape
    slots = experts * CAP
    per_dest = local_experts * CAP
    me = lax.axis_index("dp").astype(jnp.int32).reshape(1)

    with jax.named_scope("gather_tokens"):
        x_all = lax.all_gather(tokens, ("dp", "expert"), axis=0, tiled=True)

    with jax.named_scope("build_slots"):
        table, slot_scale = slot_table(route_ids, route_probs, experts)
        select = table.astype(jnp.bfloat16)
        picked = jnp.dot(select, out_grad, preferred_element_type=jnp.float32)
        g_rows = (picked * slot_scale[:, None]).astype(jnp.bfloat16)
        which = jnp.sum(jnp.where(table, jnp.arange(1, tok_count + 1, dtype=jnp.int32)[None, :], 0), axis=1) - 1
        tag = jnp.broadcast_to(which.astype(jnp.bfloat16)[:, None], (slots, LANES))
        tiles = jnp.concatenate([g_rows, tag], axis=1).reshape(columns, per_dest, width + LANES)

    with jax.named_scope("send_slots"):
        got = lax.all_to_all(tiles, "expert", split_axis=0, concat_axis=0, tiled=True)
        own = got.transpose(1, 0, 2).reshape(slots, width + LANES)

    with jax.named_scope("ring"):
        up_ring = [(i, (i + 1) % 4) for i in range(4)]
        down_ring = [(i, (i + 3) % 4) for i in range(4)]
        half = slots // 2
        a, b = own[:half], own[half:]
        left_a = lax.ppermute(a, "dp", up_ring)
        right_b = lax.ppermute(b, "dp", down_ring)
        left_b = lax.ppermute(b, "dp", up_ring)
        right_a = lax.ppermute(a, "dp", down_ring)
        far_a = lax.ppermute(left_a, "dp", up_ring)
        far_b = lax.ppermute(right_b, "dp", down_ring)
        left = jnp.concatenate([left_a, left_b], axis=0)
        right = jnp.concatenate([right_a, right_b], axis=0)

    with jax.named_scope("token_choice"):
        tags = jnp.stack(
            [
                own[:, width],
                right[:, width],
                jnp.concatenate([far_a[:, width], far_b[:, width]]),
                left[:, width],
            ]
        )
        sources = BLOCK // tok_count
        blocks = columns // sources
        tags = tags.reshape(4, per_dest, blocks, sources).transpose(0, 2, 1, 3)
        target = tags.astype(jnp.int32) + jnp.where(
            tags < 0, -BLOCK, tok_count * jnp.arange(sources, dtype=jnp.int32)
        )
        target = target.reshape(4 * blocks, per_dest * sources)
        sel = (target[:, :, None] == jnp.arange(BLOCK, dtype=jnp.int32)).astype(jnp.bfloat16)

    hidden = hidden_grads(own, right, far_a, far_b, left, w_down)
    h = act_grads(me, x_all, sel, w_gate, w_up, hidden)

    results = []
    for chunk in range(CHUNKS):
        cols = width // CHUNKS
        partials = out_rows(me, h, w_gate, w_up, chunk, CHUNKS, 256)
        with jax.named_scope("sum_blocks"):
            summed = lax.psum_scatter(
                partials.reshape(4 * slots, cols), "dp", scatter_dimension=0, tiled=True
            )
        with jax.named_scope("return_slots"):
            back = summed.reshape(per_dest, columns, cols).transpose(1, 0, 2)
            returned = lax.all_to_all(back, "expert", split_axis=0, concat_axis=0, tiled=True)
        with jax.named_scope("combine"):
            results.append(
                lax.dot_general(
                    select, returned.reshape(slots, cols), (((0,), (0,)), ((), ())),
                    preferred_element_type=jnp.float32,
                ).astype(jnp.bfloat16)
            )
    return jnp.concatenate(results, axis=1)


def solution(mesh):
    placed = (
        P(("dp", "expert"), None),
        P(("dp", "expert"), None),
        P(("dp", "expert"), None),
        P(("dp", "expert"), None),
        P("expert", None, "dp"),
        P("expert", None, "dp"),
        P("expert", "dp", None),
    )
    return jax.shard_map(
        on_device, mesh=mesh, in_specs=placed, out_specs=P(("dp", "expert"), None), check_vma=False
    )
```

time: 523 us -> 372 us (0.71)
  waiting for transfers between devices: 285 us -> 186 us
  blocking collectives: 154 us -> 64.2 us
  Pallas kernels: 0 us -> 48.6 us
  matrix products: 41.6 us -> 1.22 us
  starting transfers between devices: 0.22 us -> 28.2 us
    unnamed x3, waiting for transfers between devices: 149 us -> 0.74 us
    all_gather x1, waiting for transfers between devices: 136 us -> 3.74 us  [on_device(): x_all = lax.all_gather(tokens, ('dp', 'expert'), axis=0, tiled=True)]
    all_to_all x2 -> x1, blocking collectives: 154 us -> 64.2 us  [on_device(): lax.all_to_all(tiles, 'expert', split_axis=0, concat_axis=0, tiled=True)]
    ppermute x0 -> x6, waiting for transfers between devices: none -> 87.8 us  [the longest x1 34.9 us: on_device(): far_b = lax.ppermute(right_b, 'dp', down_ring)]
    reduce_scatter x0 -> x2, waiting for transfers between devices: none -> 69 us  [on_device(): lax.psum_scatter(partials.reshape(4 * slots, cols), 'dp', scatter_dimensi...]
    pallas_call x0 -> x4, Pallas kernels: none -> 48.6 us  [the longest x1 24.9 us: act_grads(): pl.pallas_call(act_kernel, out_shape=jax.ShapeDtypeStruct((local_experts,...]
    dot_general x8 -> x3, matrix products: 41.6 us -> 1.22 us  [the longest x1 0.67 us: on_device(): picked = jnp.dot(select, out_grad, preferred_element_type=jnp.float32)]
    all_to_all x0 -> x2, waiting for transfers between devices: none -> 25.2 us  [on_device(): lax.all_to_all(back, 'expert', split_axis=0, concat_axis=0, tiled=True)]
  transfers between devices with their start and end apart: 2 -> 11, of which waited for: 2 -> 7; matrix products, arithmetic and copies ran while one was open for 0% -> 7% of each run, Pallas kernels for 0% -> 4%
where the time goes in v1:
time: 372 us; the launch traced here: 371 us
  waiting for transfers between devices  186 us (50%)
  blocking collectives  64.2 us (17%)
  Pallas kernels  48.6 us (13%)
  starting transfers between devices  28.2 us (8%)
  local copies, waits for them, and re-layouts  22.7 us (6%)
  between operations  13.4 us (4%)
  other arithmetic  6.02 us (2%)
    reduce_scatter x2, waiting for transfers between devices, on_device(): lax.psum_scatter(partials.reshape(4 * slots, cols), 'dp', scatter_dimensi...  69 us
    all_to_all x1, blocking collectives, on_device(): lax.all_to_all(tiles, 'expert', split_axis=0, concat_axis=0, tiled=True)  64.2 us
    ppermute x1, waiting for transfers between devices, on_device(): far_b = lax.ppermute(right_b, 'dp', down_ring)  34.9 us
    ppermute x1, waiting for transfers between devices, on_device(): right_a = lax.ppermute(a, 'dp', down_ring)  33 us
    all_to_all x2, waiting for transfers between devices, on_device(): lax.all_to_all(back, 'expert', split_axis=0, concat_axis=0, tiled=True)  25.2 us
    pallas_call x1, Pallas kernels, act_grads(): pl.pallas_call(act_kernel, out_shape=jax.ShapeDtypeStruct((local_experts,...  24.9 us
    all_to_all x2, starting transfers between devices, on_device(): lax.all_to_all(back, 'expert', split_axis=0, concat_axis=0, tiled=True)  21.3 us
    ppermute x1, waiting for transfers between devices, on_device(): left_a = lax.ppermute(a, 'dp', up_ring)  19.9 us
  transfers between devices with their start and end apart: 11, of which 7 were waited for; matrix products, arithmetic and copies ran while one was open for 7% of the time, Pallas kernels for 4%

profile of v1, /device:TPU:1, one launch (start us, length us, event | category | flops | bytes accessed | tf_op | source)
XLA Modules:
  0.0 370.8 jit_solution(8333964873352219718)
XLA Ops:
  6.5 0.7 all-gather.2.cloned.1.call-update
  7.3 0.8 fusion.5
  8.4 0.8 select_reduce_fusion.2
  9.3 0.3 select_reduce_fusion.1
  9.6 0.1 mul.13
  9.9 0.1 eq.72
  10.1 2.2 select_reduce_fusion
  12.3 0.1 convert_element_type.33
  12.5 0.7 fusion
  13.5 1.5 reshape.147
  15.0 64.2 %all_to_all.15 = bf16[64,4,3712]{2,1,0:T(4,128)(2,1)S(1)} all-to-all(bf16[64,4,3712]{2,1,0:T(4,128)(2,1)} %reshape.147), channel_id=1, replica_groups=mesh['dp'=4,'expert'=64] {'expert'}, dimensions={0} | all-to-all | bytes 3801088 | tf_op jit(solution)/shard_map/send_slots/all_to_all | solution.py:172
  79.2 1.3 fusion.6
  80.6 1.1 copy.25
  81.6 1.3 collective-permute-start.2
  82.9 1.1 copy.26
  84.0 1.4 collective-permute-start.1
  85.4 1.3 collective-permute-start
  86.8 0.2 copy.24
  87.0 1.3 copy-done.2
  88.6 19.9 %collective-permute-done.2 = bf16[128,3712]{1,0:T(8,128)(2,1)} collective-permute-done((bf16[128,3712]{1,0:T(8,128)(2,1)}, bf16[128,3712]{1,0:T(8,128)(2,1)}, u32[]{:S(2)}, u32[]{:S(2)}) %collective-permute-start.2) | collective-permute-done | bytes 950304 | tf_op jit(solution)/shard_map/ring/ppermute | solution.py:180
  108.4 2.7 collective-permute-start.4
  111.1 1.3 constant_dynamic-update-slice_fusion.3
  112.3 33.0 %collective-permute-done = bf16[128,3712]{1,0:T(8,128)(2,1)} collective-permute-done((bf16[128,3712]{1,0:T(8,128)(2,1)}, bf16[128,3712]{1,0:T(8,128)(2,1)}, u32[]{:S(2)}, u32[]{:S(2)}) %collective-permute-start) | collective-permute-done | bytes 950304 | tf_op jit(solution)/shard_map/ring/ppermute | solution.py:183
  145.4 1.4 constant_dynamic-update-slice_fusion.1
  146.8 1.4 constant_dynamic-update-slice_fusion.right_ref
  148.2 1.2 copy-done.4
  149.7 1.3 constant_dynamic-update-slice_fusion.2.left_ref
  151.2 34.9 %collective-permute-done.4.far_b_ref = bf16[128,3712]{1,0:T(8,128)(2,1)} collective-permute-done((bf16[128,3712]{1,0:T(8,128)(2,1)}, bf16[128,3712]{1,0:T(8,128)(2,1)}, u32[]{:S(2)}, u32[]{:S(2)}) %collective-permute-start.4) | collective-permute-done | bytes 950304 | tf_op jit(solution)/shard_map/ring/ppermute | solution.py:185
  186.1 0.9 slice_reduce_fusion.3
  187.4 0.6 copy-done.5
  188.0 7.8 %hidden_grads.1.hidden_ref = f32[2,512,256]{2,1,0:T(8,128)} custom-call(bf16[256,3712]{1,0:T(8,128)(2,1)} %bitcast.28, bf16[256,3712]{1,0:T(8,128)(2,1)} %copy-done.4, bf16[128,3712]{1,0:T(8,128)(2,1)} %copy-done.5, bf16[128,3712]{1,0:T(8,128)(2,1)} %collective-permute-done.4.far_b_ref, bf16[256,3712]{1,0:T(8,128)(2,1)} %copy-done.3, bf16[2,256,3584]{2,1,0:T(8,128)(2,1)} %w_ref.1), custom_call_target="tpu_custom_call" | custom-call | flops 1879048192 | bytes 12582912 | tf_op jit(solution)/shard_map/hidden_grads/pallas_call | solution.py:43
  195.8 1.0 fusion.1.sel_ref
  196.7 3.7 %all-gather.2.cloned.1.call-done.x_ref = bf16[4096,3584]{1,0:T(8,128)(2,1)} async-done(((bf16[16,3584]{1,0:T(8,128)(2,1)}), bf16[4096,3584]{1,0:T(8,128)(2,1)}) %all-gather.2.cloned.1.call-update) | async-done | bytes 29360144 | tf_op jit(solution)/shard_map/gather_tokens/all_gather | solution.py:160
  200.5 24.9 %act_grads.1.h_ref = bf16[2,512,512]{2,1,0:T(8,128)(2,1)} custom-call(s32[1]{0:T(128)} %bitcast.1.me_ref, bf16[4096,3584]{1,0:T(8,128)(2,1)} %all-gather.2.cloned.1.call-done.x_ref, bf16[16,64,256]{2,1,0:T(8,128)(2,1)} %fusion.1.sel_ref, bf16[2,3584,256]{2,1,0:T(8,128)(2,1)} %gate_ref.5, bf16[2,3584,256]{2,1,0:T(8,128)(2,1)} %up_ref.5, ...), custom_call_target="tpu_custom_call" | custom-call | flops 5637144576 | bytes 41943040 | tf_op jit(solution)/shard_map/act_grads/pallas_call | solution.py:86
  225.3 8.0 %out_rows.2 = bf16[4,256,1792]{2,1,0:T(8,128)(2,1)} custom-call(s32[1]{0:T(128)} %bitcast.1.me_ref, bf16[2,512,512]{2,1,0:T(8,128)(2,1)} %act_grads.1.h_ref, bf16[2,3584,256]{2,1,0:T(8,128)(2,1)} %gate_ref.5, bf16[2,3584,256]{2,1,0:T(8,128)(2,1)} %up_ref.5), custom_call_target="tpu_custom_call" | custom-call | flops 1879048192 | bytes 8388608 | tf_op jit(solution)/shard_map/out_rows/pallas_call | solution.py:129
  233.4 8.0 %out_rows.3 = bf16[4,256,1792]{2,1,0:T(8,128)(2,1)} custom-call(s32[1]{0:T(128)} %bitcast.1.me_ref, bf16[2,512,512]{2,1,0:T(8,128)(2,1)} %act_grads.1.h_ref, bf16[2,3584,256]{2,1,0:T(8,128)(2,1)} %gate_ref.5, bf16[2,3584,256]{2,1,0:T(8,128)(2,1)} %up_ref.5), custom_call_target="tpu_custom_call" | custom-call | flops 1879048192 | bytes 8388608 | tf_op jit(solution)/shard_map/out_rows/pallas_call | solution.py:129
  241.4 35.1 %reduce-scatter.3.cloned.1.call-done = bf16[256,1792]{1,0:T(8,128)(2,1)} async-done(((bf16[1024,1792]{1,0:T(8,128)(2,1)}), bf16[256,1792]{1,0:T(8,128)(2,1)}) %reduce-scatter.3.cloned.1.call-update) | async-done | bytes 917520 | tf_op jit(solution)/shard_map/sum_blocks/reduce_scatter | solution.py:215
  276.5 2.8 copy.28
  279.3 10.6 %all-to-all-start.1 = ((bf16[64,4,1792]{2,1,0:T(4,128)(2,1)}), bf16[64,4,1792]{2,1,0:T(4,128)(2,1)S(1)}, u32[]{:S(2)}, u32[]{:S(2)}) async-start(bf16[64,4,1792]{2,1,0:T(4,128)(2,1)} %copy.28), calls=%async_computation.2 | async-start | bytes 1835008 | tf_op jit(solution)/shard_map/return_slots/all_to_all | solution.py:220
  290.0 34.0 %reduce-scatter.5.cloned.1.call-done = bf16[256,1792]{1,0:T(8,128)(2,1)} async-done(((bf16[1024,1792]{1,0:T(8,128)(2,1)}), bf16[256,1792]{1,0:T(8,128)(2,1)}) %reduce-scatter.5.cloned.1.call-update) | async-done | bytes 917520 | tf_op jit(solution)/shard_map/sum_blocks/reduce_scatter | solution.py:215
  323.9 2.8 copy.29
  326.7 10.6 %all-to-all-start.2 = ((bf16[64,4,1792]{2,1,0:T(4,128)(2,1)}), bf16[64,4,1792]{2,1,0:T(4,128)(2,1)S(1)}, u32[]{:S(2)}, u32[]{:S(2)}) async-start(bf16[64,4,1792]{2,1,0:T(4,128)(2,1)} %copy.29), calls=%async_computation.4 | async-start | bytes 1835008 | tf_op jit(solution)/shard_map/return_slots/all_to_all | solution.py:220
  337.5 0.2 reshape.151
  337.7 0.3 convolution_convert_fusion.1
  338.0 25.2 %all-to-all-done.2 = bf16[64,4,1792]{2,1,0:T(4,128)(2,1)S(1)} async-done(((bf16[64,4,1792]{2,1,0:T(4,128)(2,1)}), bf16[64,4,1792]{2,1,0:T(4,128)(2,1)S(1)}, u32[]{:S(2)}, u32[]{:S(2)}) %all-to-all-start.2) | async-done | bytes 917536 | tf_op jit(solution)/shard_map/return_slots/all_to_all | solution.py:220
  363.1 0.2 reshape.154
  363.4 0.3 convolution_convert_fusion
  363.6 0.7 pad_maximum_fusion.1
  (51 shorter events, 2.2 us)
Async XLA Ops:
  6.5 6.0 %copy-start = (bf16[16,3584]{1,0:T(8,128)(2,1)S(1)}, bf16[16,3584]{1,0:T(8,128)(2,1)}, u32[]{:S(2)}) copy-start(bf16[16,3584]{1,0:T(8,128)(2,1)} %param.8) | copy-start | bytes 344068
  6.5 193.9 %all-gather.2.cloned.1.call-start = ((), (), s32[]{:S(2)}) async-start(), calls=%async_computation.5 | async-start | bytes 29474816 | tf_op jit(solution)/shard_map/gather_tokens/all_gather | solution.py:160
  7.3 269.2 %reduce-scatter.3.cloned.1.call-start = ((), (), s32[]{:S(2)}) async-start(), calls=%async_computation.6 | async-start | bytes 4587520 | tf_op jit(solution)/shard_map/sum_blocks/reduce_scatter | solution.py:215
  81.6 26.8 %collective-permute-start.2 = (bf16[128,3712]{1,0:T(8,128)(2,1)}, bf16[128,3712]{1,0:T(8,128)(2,1)}, u32[]{:S(2)}, u32[]{:S(2)}) collective-permute-start(bf16[128,3712]{1,0:T(8,128)(2,1)} %bitcast.6), channel_id=1, source_target_pairs={{0,64},{64,128},{128,192},{192,0},{1,65},{65,129},{129,193},{193,1... | collective-permute-start | bytes 2850824 | tf_op jit(solution)/shard_map/ring/ppermute | solution.py:180
  84.0 24.5 %collective-permute-start.1 = (bf16[128,3712]{1,0:T(8,128)(2,1)}, bf16[128,3712]{1,0:T(8,128)(2,1)}, u32[]{:S(2)}, u32[]{:S(2)}) collective-permute-start(bf16[128,3712]{1,0:T(8,128)(2,1)} %bitcast.7), channel_id=1, source_target_pairs={{0,192},{64,0},{128,64},{192,128},{1,193},{65,1},{129,65},{193,129... | collective-permute-start | bytes 2850824 | tf_op jit(solution)/shard_map/ring/ppermute | solution.py:181
  85.4 60.0 %collective-permute-start = (bf16[128,3712]{1,0:T(8,128)(2,1)}, bf16[128,3712]{1,0:T(8,128)(2,1)}, u32[]{:S(2)}, u32[]{:S(2)}) collective-permute-start(bf16[128,3712]{1,0:T(8,128)(2,1)} %bitcast.6), channel_id=1, source_target_pairs={{0,192},{64,0},{128,64},{192,128},{1,193},{65,1},{129,65},{193,129... | collective-permute-start | bytes 2850824 | tf_op jit(solution)/shard_map/ring/ppermute | solution.py:183
  86.7 62.9 %collective-permute-start.5 = (bf16[128,3712]{1,0:T(8,128)(2,1)}, bf16[128,3712]{1,0:T(8,128)(2,1)}, u32[]{:S(2)}, u32[]{:S(2)}) collective-permute-start(bf16[128,3712]{1,0:T(8,128)(2,1)} %bitcast.7), channel_id=1, source_target_pairs={{0,64},{64,128},{128,192},{192,0},{1,65},{65,129},{129,193},{193,1... | collective-permute-start | bytes 2850824 | tf_op jit(solution)/shard_map/ring/ppermute | solution.py:182
  87.0 1.3 copy-start.2
  108.4 78.6 %collective-permute-start.3 = (bf16[128,3712]{1,0:T(8,128)(2,1)}, bf16[128,3712]{1,0:T(8,128)(2,1)S(1)}, u32[]{:S(2)}, u32[]{:S(2)}) collective-permute-start(bf16[128,3712]{1,0:T(8,128)(2,1)} %collective-permute-done.2), channel_id=1, source_target_pairs={{0,64},{64,128},{128,192},{192,0},{1,65},{65,129},{129,193},{193,1... | collective-permute-start | bytes 2850824 | tf_op jit(solution)/shard_map/ring/ppermute | solution.py:184
  108.4 77.7 %collective-permute-start.4 = (bf16[128,3712]{1,0:T(8,128)(2,1)}, bf16[128,3712]{1,0:T(8,128)(2,1)}, u32[]{:S(2)}, u32[]{:S(2)}) collective-permute-start(bf16[128,3712]{1,0:T(8,128)(2,1)} %collective-permute-done.1), channel_id=1, source_target_pairs={{0,192},{64,0},{128,64},{192,128},{1,193},{65,1},{129,65},{193,129... | collective-permute-start | bytes 2850824 | tf_op jit(solution)/shard_map/ring/ppermute | solution.py:185
  148.2 1.3 copy-start.4
  151.0 36.4 %copy-start.3 = (bf16[256,3712]{1,0:T(8,128)(2,1)}, bf16[256,3712]{1,0:T(8,128)(2,1)S(1)}, u32[]{:S(2)}) copy-start(bf16[256,3712]{1,0:T(8,128)(2,1)S(1)} %constant_dynamic-update-slice_fusion.2.left_ref) | copy-start | bytes 5701636
  187.0 1.0 copy-start.5
  233.3 90.6 %reduce-scatter.5.cloned.1.call-start = ((), (), s32[]{:S(2)}) async-start(), calls=%async_computation.7 | async-start | bytes 4587520 | tf_op jit(solution)/shard_map/sum_blocks/reduce_scatter | solution.py:215
  279.3 47.4 %all-to-all-start.1 = ((bf16[64,4,1792]{2,1,0:T(4,128)(2,1)}), bf16[64,4,1792]{2,1,0:T(4,128)(2,1)S(1)}, u32[]{:S(2)}, u32[]{:S(2)}) async-start(bf16[64,4,1792]{2,1,0:T(4,128)(2,1)} %copy.28), calls=%async_computation.2 | async-start | bytes 1835008 | tf_op jit(solution)/shard_map/return_slots/all_to_all | solution.py:220
  326.7 36.4 %all-to-all-start.2 = ((bf16[64,4,1792]{2,1,0:T(4,128)(2,1)}), bf16[64,4,1792]{2,1,0:T(4,128)(2,1)S(1)}, u32[]{:S(2)}, u32[]{:S(2)}) async-start(bf16[64,4,1792]{2,1,0:T(4,128)(2,1)} %copy.29), calls=%async_computation.4 | async-start | bytes 1835008 | tf_op jit(solution)/shard_map/return_slots/all_to_all | solution.py:220
  337.5 26.8 %copy-start.1 = (bf16[16,3584]{1,0:T(8,128)(2,1)S(1)}, bf16[16,3584]{1,0:T(8,128)(2,1)}, u32[]{:S(2)}) copy-start(bf16[16,3584]{1,0:T(8,128)(2,1)} %param.8) | copy-start | bytes 344068
Sparse Core Ops, SparseCore 0:
  10.9 189.4 all-gather.1
  233.4 43.0 reduce-scatter.2
  279.1 44.8 reduce-scatter.4

commit v2 on v1

v2 whole, which is shorter than its diff:
```python
import jax
import jax.numpy as jnp
from jax import lax
from jax.experimental import pallas as pl
from jax.experimental.pallas import tpu as pltpu
from jax.sharding import PartitionSpec as P

CAP = 2
LANES = 128
BLOCK = 256
CHUNKS = 2
HEAD = 2048
STEP = 512
NT = (((1,), (1,)), ((), ()))


def slot_table(ids, probs, experts):
    tok_count = ids.shape[0]
    named = ids.T[None, :, :] == jnp.arange(experts, dtype=jnp.int32)[:, None, None]
    mask = jnp.any(named, axis=1)
    scale = jnp.sum(jnp.where(named, probs.T[None, :, :], 0.0), axis=1)
    order = jnp.arange(tok_count, dtype=jnp.int32)
    before = (order[:, None] < order[None, :])[None, :, :]
    rank = jnp.sum((mask[:, :, None] & before).astype(jnp.int32), axis=1)
    slots = mask[:, None, :] & (rank[:, None, :] == jnp.arange(CAP, dtype=jnp.int32)[None, :, None])
    slot_scale = jnp.sum(jnp.where(slots, scale[:, None, :], 0.0), axis=2)
    return slots.reshape(experts * CAP, tok_count), slot_scale.reshape(experts * CAP)


def head_kernel(me_ref, x_ref, sel_ref, gate_ref, up_ref, out_ref, picked):
    step = pl.program_id(0)
    blocks = pl.num_programs(0) // 4
    group, block = lax.rem(step // blocks + 4 - me_ref[0], 4), step % blocks
    x = x_ref[...].reshape(-1, x_ref.shape[3])
    rows = jnp.dot(sel_ref[0], x, preferred_element_type=jnp.float32).astype(jnp.bfloat16)
    part = rows.shape[0] // 4
    for slot in range(4):
        at = pl.multiple_of(group * (blocks * part * CAP) + (slot % CAP) * (blocks * part) + block * part, 16)
        picked[slot // CAP, pl.ds(at, part), :] = rows[slot * part : (slot + 1) * part]

    @pl.when(step == pl.num_programs(0) - 1)
    def _():
        units = gate_ref.shape[2]
        for e in range(2):
            out_ref[e, :, :units] = jnp.dot(picked[e], gate_ref[e], preferred_element_type=jnp.float32)
            out_ref[e, :, units:] = jnp.dot(picked[e], up_ref[e], preferred_element_type=jnp.float32)


def head_products(me, x_all, sel, w_gate, w_up):
    columns, groups, tok_count, head = x_all.shape
    local_experts, _, units = w_gate.shape
    steps, part, block = sel.shape
    rows = columns * groups * CAP
    blocks = steps // groups
    w_spec = pl.BlockSpec((local_experts, head, units), lambda i, me: (0, 0, 0))
    return pl.pallas_call(
        head_kernel,
        out_shape=jax.ShapeDtypeStruct((local_experts, rows, 2 * units), jnp.float32),
        grid_spec=pltpu.PrefetchScalarGridSpec(
            num_scalar_prefetch=1,
            grid=(steps,),
            in_specs=[
                pl.BlockSpec((columns // blocks, 1, tok_count, head), lambda i, me: (i % blocks, i // blocks, 0, 0)),
                pl.BlockSpec((1, part, block), lambda i, me: (i, 0, 0)),
                w_spec,
                w_spec,
            ],
            out_specs=pl.BlockSpec((local_experts, rows, 2 * units), lambda i, me: (0, 0, 0)),
            scratch_shapes=[pltpu.VMEM((local_experts, rows, head), jnp.bfloat16)],
        ),
        compiler_params=pltpu.CompilerParams(dimension_semantics=("arbitrary",)),
        cost_estimate=pl.CostEstimate(
            flops=2 * local_experts * rows * 2 * units * head + 2 * steps * part * block * head,
            bytes_accessed=25 << 20,
            transcendentals=0,
        ),
        name="head_products",
    )(me, x_all, sel, w_gate, w_up)


def late_kernel(first, own_ref, right_ref, far_ref, left_ref, head_ref, down_ref, gate_ref, up_ref, out_ref, hidden, pre):
    step = pl.program_id(0)
    units = gate_ref.shape[2]

    @pl.when(step == 0)
    def _():
        hidden[...] = jnp.zeros_like(hidden)
        pre[...] = head_ref[0]

    rows = jnp.concatenate([own_ref[...], right_ref[...], far_ref[...], left_ref[...]], axis=0)

    @pl.when(step < first)
    def _():
        hidden[...] += lax.dot_general(rows, down_ref[0], NT, preferred_element_type=jnp.float32)

    @pl.when(step >= first)
    def _():
        pre[:, :units] += jnp.dot(rows, gate_ref[0], preferred_element_type=jnp.float32)
        pre[:, units:] += jnp.dot(rows, up_ref[0], preferred_element_type=jnp.float32)

    @pl.when(step == pl.num_programs(0) - 1)
    def _():
        gate_pre, up_pre, grad = pre[:, :units], pre[:, units:], hidden[...]
        s = jax.nn.sigmoid(gate_pre)
        out_ref[:, :units] = (grad * up_pre * s * (1.0 + gate_pre * (1.0 - s))).astype(jnp.bfloat16)
        out_ref[:, units:] = (grad * gate_pre * s).astype(jnp.bfloat16)


def late_grads(e, own, right, far, left, head_pre, w_down, w_gate, w_up, head):
    _, width, units = w_gate.shape
    rows = 4 * own.shape[0]
    first, steps, skip = width // STEP, (2 * width - head) // STEP, head // STEP
    slot_spec = pl.BlockSpec((own.shape[0], STEP), lambda k: (0, k))
    w_spec = pl.BlockSpec((1, STEP, units), lambda k: (e, skip + jnp.maximum(k - first, 0), 0))
    return pl.pallas_call(
        lambda *refs: late_kernel(first, *refs),
        out_shape=jax.ShapeDtypeStruct((rows, 2 * units), jnp.bfloat16),
        grid=(steps,),
        in_specs=[
            slot_spec,
            slot_spec,
            slot_spec,
            slot_spec,
            pl.BlockSpec((1, rows, 2 * units), lambda k: (e, 0, 0)),
            pl.BlockSpec((1, units, STEP), lambda k: (e, 0, jnp.minimum(k, first - 1))),
            w_spec,
            w_spec,
        ],
        out_specs=pl.BlockSpec((rows, 2 * units), lambda k: (0, 0)),
        scratch_shapes=[pltpu.VMEM((rows, units), jnp.float32), pltpu.VMEM((rows, 2 * units), jnp.float32)],
        compiler_params=pltpu.CompilerParams(dimension_semantics=("arbitrary",)),
        cost_estimate=pl.CostEstimate(
            flops=2 * rows * units * (3 * width - 2 * head), bytes_accessed=10 << 20, transcendentals=rows * units
        ),
        name="late_grads",
    )(own, right, far, left, head_pre, w_down, w_gate, w_up)


def out_kernel(me_ref, h0_ref, h1_ref, gate_ref, up_ref, out_ref):
    units = gate_ref.shape[2]
    for e, h_ref in enumerate((h0_ref, h1_ref)):
        value = lax.dot_general(h_ref[:, :units], gate_ref[e], NT, preferred_element_type=jnp.float32)
        value = value + lax.dot_general(h_ref[:, units:], up_ref[e], NT, preferred_element_type=jnp.float32)
        value = value.astype(jnp.bfloat16)
        part = value.shape[0] // 4
        for r in range(4):
            out_ref[lax.rem(me_ref[0] + r, 4), e * part : (e + 1) * part, :] = value[r * part : (r + 1) * part]


def out_rows(me, h, w_gate, w_up, chunk, chunks, cols):
    rows = h[0].shape[0]
    local_experts, width, units = w_gate.shape
    h_spec = pl.BlockSpec((rows, 2 * units), lambda n, me: (0, 0))
    per = width // chunks // cols
    first = chunk * per
    w_spec = pl.BlockSpec((local_experts, cols, units), lambda n, me: (0, first + n, 0))
    return pl.pallas_call(
        out_kernel,
        out_shape=jax.ShapeDtypeStruct((4, local_experts * rows // 4, width // chunks), jnp.bfloat16),
        grid_spec=pltpu.PrefetchScalarGridSpec(
            num_scalar_prefetch=1,
            grid=(per,),
            in_specs=[
                h_spec,
                h_spec,
                w_spec,
                w_spec,
            ],
            out_specs=pl.BlockSpec((4, local_experts * rows // 4, cols), lambda n, me: (0, 0, n)),
        ),
        compiler_params=pltpu.CompilerParams(dimension_semantics=("arbitrary",)),
        cost_estimate=pl.CostEstimate(
            flops=2 * local_experts * rows * 2 * units * width // chunks, bytes_accessed=8 << 20, transcendentals=0
        ),
        name="out_rows",
    )(me, *h, w_gate, w_up)


def on_device(tokens, out_grad, route_ids, route_probs, w_gate, w_up, w_down):
    columns = lax.axis_size("expert")
    local_experts = w_gate.shape[0]
    experts = local_experts * columns
    tok_count, width = tokens.shape
    slots = experts * CAP
    per_dest = local_experts * CAP
    me = lax.axis_index("dp").astype(jnp.int32).reshape(1)

    with jax.named_scope("gather_tokens"):
        near = lax.all_gather(tokens[:, :HEAD], "dp", axis=0, tiled=True)
        x_all = lax.all_gather(near, "expert", axis=0, tiled=True).reshape(columns, 4, tok_count, HEAD)

    with jax.named_scope("build_slots"):
        table, slot_scale = slot_table(route_ids, route_probs, experts)
        select = table.astype(jnp.bfloat16)
        which = jnp.sum(jnp.where(table, jnp.arange(1, tok_count + 1, dtype=jnp.int32)[None, :], 0), axis=1) - 1
        tag = which.astype(jnp.bfloat16).reshape(columns, local_experts, CAP)
        tiles = []
        for e in range(2):
            choose = select.reshape(columns, local_experts, CAP, tok_count)[:, e].reshape(columns * CAP, tok_count)
            scale = slot_scale.reshape(columns, local_experts, CAP)[:, e].reshape(columns * CAP, 1)
            g_rows = (jnp.dot(choose, out_grad, preferred_element_type=jnp.float32) * scale).astype(jnp.bfloat16)
            x_rows = jnp.dot(choose, tokens[:, HEAD:], preferred_element_type=jnp.float32).astype(jnp.bfloat16)
            parts = [g_rows, x_rows]
            if e == 0:
                both = jnp.broadcast_to(tag.transpose(0, 2, 1)[:, :, :, None], (columns, CAP, 2, LANES // 2))
                parts.append(both.reshape(columns * CAP, LANES))
            tiles.append(jnp.concatenate(parts, axis=1).reshape(columns, CAP, -1))

    up_ring = [(i, (i + 1) % 4) for i in range(4)]
    down_ring = [(i, (i + 3) % 4) for i in range(4)]
    sent = 2 * width - HEAD
    half = columns * CAP

    def send(tile):
        return lax.all_to_all(tile, "expert", split_axis=0, concat_axis=0, tiled=True)

    def by_slot(got):
        return got.transpose(1, 0, 2).reshape(half, -1)

    with jax.named_scope("send_first"):
        got = by_slot(send(tiles[0]))
        a, own_tags = got[:, :sent], got[:, sent:]
        own_tags = own_tags.reshape(CAP, columns, 2, LANES // 2)[:, :, :, 0].transpose(2, 0, 1)
        tags = lax.all_gather(own_tags.reshape(2, half), "dp", axis=0, tiled=True)
    with jax.named_scope("ring_first"):
        left_a = lax.ppermute(a, "dp", up_ring)
        right_a = lax.ppermute(a, "dp", down_ring)
    with jax.named_scope("send_second"):
        second, _ = lax.optimization_barrier((tiles[1], a))
        got, left_a, right_a = lax.optimization_barrier((send(second), left_a, right_a))
        b = by_slot(got)
    with jax.named_scope("ring_far"):
        far_a = lax.ppermute(left_a, "dp", up_ring)
    with jax.named_scope("ring_second"):
        right_b = lax.ppermute(b, "dp", down_ring)
        left_b = lax.ppermute(b, "dp", up_ring)
        far_b = lax.ppermute(right_b, "dp", down_ring)

    with jax.named_scope("token_choice"):
        sources = BLOCK // tok_count
        blocks = columns // sources
        tags = tags.reshape(4, per_dest, blocks, sources).transpose(0, 2, 1, 3)
        target = tags.astype(jnp.int32) + jnp.where(
            tags < 0, -BLOCK, tok_count * jnp.arange(sources, dtype=jnp.int32)
        )
        target = target.reshape(4 * blocks, per_dest * sources)
        sel = (target[:, :, None] == jnp.arange(BLOCK, dtype=jnp.int32)).astype(jnp.bfloat16)

    head_pre = head_products(me, x_all, sel, w_gate, w_up)
    h = (
        late_grads(0, a, right_a, far_a, left_a, head_pre, w_down, w_gate, w_up, HEAD),
        late_grads(1, b, right_b, far_b, left_b, head_pre, w_down, w_gate, w_up, HEAD),
    )

    results = []
    for chunk in range(CHUNKS):
        cols = width // CHUNKS
        partials = out_rows(me, h, w_gate, w_up, chunk, CHUNKS, 256)
        with jax.named_scope("sum_blocks"):
            summed = lax.psum_scatter(
                partials.reshape(4 * slots, cols), "dp", scatter_dimension=0, tiled=True
            )
        with jax.named_scope("return_slots"):
            back = summed.reshape(per_dest, columns, cols).transpose(1, 0, 2)
            returned = lax.all_to_all(back, "expert", split_axis=0, concat_axis=0, tiled=True)
        with jax.named_scope("combine"):
            results.append(
                lax.dot_general(
                    select, returned.reshape(slots, cols), (((0,), (0,)), ((), ())),
                    preferred_element_type=jnp.float32,
                ).astype(jnp.bfloat16)
            )
    return jnp.concatenate(results, axis=1)


def solution(mesh):
    placed = (
        P(("dp", "expert"), None),
        P(("dp", "expert"), None),
        P(("dp", "expert"), None),
        P(("dp", "expert"), None),
        P("expert", None, "dp"),
        P("expert", None, "dp"),
        P("expert", "dp", None),
    )
    return jax.shard_map(
        on_device, mesh=mesh, in_specs=placed, out_specs=P(("dp", "expert"), None), check_vma=False
    )
```

time: 372 us -> 397 us (1.067)
  waiting for transfers between devices: 186 us -> 208 us
  starting transfers between devices: 28.2 us -> 50.1 us
  blocking collectives: 64.2 us -> 43.2 us
  local copies, waits for them, and re-layouts: 22.7 us -> 15.4 us
  Pallas kernels: 48.6 us -> 55.3 us
    all_to_all x1 -> x0, blocking collectives: 64.2 us -> none  [on_device(): lax.all_to_all(tiles, 'expert', split_axis=0, concat_axis=0, tiled=True)]
    all_to_all x0 -> x2, waiting for transfers between devices: none -> 55 us  [send(): lax.all_to_all(tile, 'expert', split_axis=0, concat_axis=0, tiled=True)]
    all_gather x0 -> x2, blocking collectives: none -> 43.2 us  [the longest x1 31.4 us: on_device(): tags = lax.all_gather(own_tags.reshape(2, half), 'dp', axis=0, tiled=True)]
    ppermute x1, waiting for transfers between devices: 34.9 us -> 0.01 us  [on_device(): far_b = lax.ppermute(right_b, 'dp', down_ring)]
    ppermute x1, waiting for transfers between devices: 0.01 us -> 28.1 us  [on_device(): right_b = lax.ppermute(b, 'dp', down_ring)]
    all_to_all x0 -> x2, starting transfers between devices: none -> 20.6 us  [send(): lax.all_to_all(tile, 'expert', split_axis=0, concat_axis=0, tiled=True)]
    ppermute x1, waiting for transfers between devices: 19.9 us -> 2.12 us  [on_device(): left_a = lax.ppermute(a, 'dp', up_ring)]
    pallas_call x2 -> x3, Pallas kernels: 32.6 us -> 39.4 us  [the longest x2 20.9 us: late_grads(): pl.pallas_call(lambda *refs: late_kernel(first, *refs), out_shape=jax.Sha...]
  transfers between devices with their start and end apart: 11 -> 13, of which waited for: 7 -> 8; matrix products, arithmetic and copies ran while one was open for 7% -> 6% of each run, Pallas kernels for 4% -> 9%
where the time goes in v2:
time: 397 us; the launch traced here: 396 us
  waiting for transfers between devices  208 us (52%)
  Pallas kernels  55.3 us (14%)
  starting transfers between devices  50.1 us (13%)
  blocking collectives  43.2 us (11%)
  local copies, waits for them, and re-layouts  15.4 us (4%)
  between operations  13.4 us (3%)
  other arithmetic  8.77 us (2%)
    reduce_scatter x2, waiting for transfers between devices, on_device(): lax.psum_scatter(partials.reshape(4 * slots, cols), 'dp', scatter_dimensi...  69.5 us
    all_to_all x2, waiting for transfers between devices, send(): lax.all_to_all(tile, 'expert', split_axis=0, concat_axis=0, tiled=True)  55 us
    all_gather x1, blocking collectives, on_device(): tags = lax.all_gather(own_tags.reshape(2, half), 'dp', axis=0, tiled=True)  31.4 us
    ppermute x1, waiting for transfers between devices, on_device(): right_b = lax.ppermute(b, 'dp', down_ring)  28.1 us
    ppermute x1, waiting for transfers between devices, on_device(): right_a = lax.ppermute(a, 'dp', down_ring)  27.6 us
    all_to_all x2, waiting for transfers between devices, on_device(): lax.all_to_all(back, 'expert', split_axis=0, concat_axis=0, tiled=True)  25.2 us
    all_to_all x2, starting transfers between devices, on_device(): lax.all_to_all(back, 'expert', split_axis=0, concat_axis=0, tiled=True)  21.3 us
    pallas_call x2, Pallas kernels, late_grads(): pl.pallas_call(lambda *refs: late_kernel(first, *refs), out_shape=jax.Sha...  20.9 us
  transfers between devices with their start and end apart: 13, of which 8 were waited for; matrix products, arithmetic and copies ran while one was open for 6% of the time, Pallas kernels for 9%

profile of v2, /device:TPU:1, one launch (start us, length us, event | category | flops | bytes accessed | tf_op | source)
XLA Modules:
  0.0 395.5 jit_solution(7202186672997119504)
XLA Ops:
  6.5 0.9 slice.34
  7.5 11.8 %all_gather.9 = bf16[64,2048]{1,0:T(8,128)(2,1)} all-gather(bf16[16,2048]{1,0:T(8,128)(2,1)S(1)} %slice.34), channel_id=1, replica_groups=mesh['dp'=4,'expert'=64] {'dp'}, dimensions={0}, use_global_device_ids=true | all-gather | bytes 327680 | tf_op jit(solution)/shard_map/gather_tokens/all_gather | solution.py:189
  19.3 0.8 fusion.3
  20.5 0.8 select_reduce_fusion.2
  21.4 0.3 select_reduce_fusion.1
  21.7 0.2 slice_reduce_fusion
  22.0 2.2 select_reduce_fusion
  24.3 0.5 copy.90
  24.8 0.2 broadcast_in_dim.69
  25.4 0.2 convolution_convert_fusion.1
  25.7 0.1 concatenate.17
  25.8 0.4 fusion
  26.2 0.3 concatenate.16
  26.5 2.6 pad_maximum_fusion
  29.1 14.7 %all-to-all-start = ((bf16[64,2,5248]{2,1,0:T(2,128)(2,1)}), bf16[64,2,5248]{2,1,0:T(2,128)(2,1)S(1)}, u32[]{:S(2)}, u32[]{:S(2)}) async-start(bf16[64,2,5248]{2,1,0:T(2,128)(2,1)} %pad_maximum_fusion), calls=%async_computation | async-start | bytes 2686976 | tf_op jit(solution)/shard_map/send_first/all_to_all | solution.py:215
  44.0 0.2 convolution_convert_fusion
  44.3 0.4 fusion.1
  44.8 1.4 reshape.167
  46.1 39.8 %all-to-all-done = bf16[64,2,5248]{2,1,0:T(2,128)(2,1)S(1)} async-done(((bf16[64,2,5248]{2,1,0:T(2,128)(2,1)}), bf16[64,2,5248]{2,1,0:T(2,128)(2,1)S(1)}, u32[]{:S(2)}, u32[]{:S(2)}) %all-to-all-start) | async-done | bytes 1343520 | tf_op jit(solution)/shard_map/send_first/all_to_all | solution.py:215
  86.2 5.9 %all-to-all-start.1 = ((bf16[64,2,5120]{2,1,0:T(2,128)(2,1)}), bf16[64,2,5120]{2,1,0:T(2,128)(2,1)}, u32[]{:S(2)}, u32[]{:S(2)}) async-start(bf16[64,2,5120]{2,1,0:T(2,128)(2,1)} %reshape.167), calls=%async_computation.1 | async-start | bytes 2621440 | tf_op jit(solution)/shard_map/send_second/all_to_all | solution.py:215
  92.2 2.5 collective-permute-start.1
  94.7 27.6 %collective-permute-done.1.refs_1_ = bf16[128,5120]{1,0:T(8,128)(2,1)S(1)} collective-permute-done((bf16[128,5120]{1,0:T(8,128)(2,1)S(1)}, bf16[128,5120]{1,0:T(8,128)(2,1)S(1)}, u32[]{:S(2)}, u32[]{:S(2)}) %collective-permute-start.1) | collective-permute-done | bytes 1310752 | tf_op jit(solution)/shard_map/ring_first/ppermute | solution.py:227
  122.3 1.1 copy-done.3
  123.3 2.1 collective-permute-done.refs_3_
  125.5 15.2 %all-to-all-done.1 = bf16[64,2,5120]{2,1,0:T(2,128)(2,1)} async-done(((bf16[64,2,5120]{2,1,0:T(2,128)(2,1)}), bf16[64,2,5120]{2,1,0:T(2,128)(2,1)}, u32[]{:S(2)}, u32[]{:S(2)}) %all-to-all-start.1) | async-done | bytes 1310752 | tf_op jit(solution)/shard_map/send_second/all_to_all | solution.py:215
  140.6 2.7 copy.79
  143.3 2.4 collective-permute-start.3
  145.8 28.1 %collective-permute-done.3.refs_1_ = bf16[128,5120]{1,0:T(8,128)(2,1)S(1)} collective-permute-done((bf16[128,5120]{1,0:T(8,128)(2,1)}, bf16[128,5120]{1,0:T(8,128)(2,1)S(1)}, u32[]{:S(2)}, u32[]{:S(2)}) %collective-permute-start.3) | collective-permute-done | bytes 1310752 | tf_op jit(solution)/shard_map/ring_second/ppermute | solution.py:235
  173.8 3.3 collective-permute-start.4
  177.4 31.4 %all-gather = bf16[4,2,128]{2,1,0:T(2,128)(2,1)S(1)} all-gather(bf16[1,2,128]{2,1,0:T(2,128)(2,1)S(1)} %reshape.179), channel_id=1, replica_groups=mesh['dp'=4,'expert'=64] {'dp'}, dimensions={0}, use_global_device_ids=true | all-gather | bytes 2560 | tf_op jit(solution)/shard_map/send_first/all_gather | solution.py:224
  209.2 1.0 fusion.2.sel_ref
  210.2 18.5 %head_products.1.refs_4_ = f32[2,512,512]{2,1,0:T(8,128)} custom-call(s32[1]{0:T(128)} %bitcast.1.me_ref, bf16[64,4,16,2048]{3,2,1,0:T(8,128)(2,1)} %bitcast.42, bf16[16,64,256]{2,1,0:T(8,128)(2,1)} %fusion.2.sel_ref, bf16[2,3584,256]{2,1,0:T(8,128)(2,1)} %gate_ref.5, bf16[2,3584,256]{2,1,0:T(8,128)(2,1)} %up_ref.5), custom_call_target="tpu_custom_call" | custom-call | flops 3221225472 | bytes 26214400 | tf_op jit(solution)/shard_map/head_products/pallas_call | solution.py:56
  228.7 10.4 %late_grads.3.h1_ref = bf16[512,512]{1,0:T(8,128)(2,1)} custom-call(bf16[128,5120]{1,0:T(8,128)(2,1)} %bitcast.13.refs_0_, bf16[128,5120]{1,0:T(8,128)(2,1)} %copy-done.4, bf16[128,5120]{1,0:T(8,128)(2,1)} %collective-permute-done.4.refs_2_, bf16[128,5120]{1,0:T(8,128)(2,1)} %collective-permute-done.5.refs_3_, f32[2,512,512]{2,1,0:T(8,128)} %head_products.1.refs_4_, ...), custom_call_target="tpu_custom_call" | custom-call | flops 1744830464 | bytes 10485760 | tf_op jit(solution)/shard_map/late_grads/pallas_call | solution.py:115
  239.1 10.5 %late_grads.2.h0_ref = bf16[512,512]{1,0:T(8,128)(2,1)} custom-call(bf16[128,5120]{1,0:T(8,128)(2,1)} %copy-done.2, bf16[128,5120]{1,0:T(8,128)(2,1)} %copy-done.3, bf16[128,5120]{1,0:T(8,128)(2,1)} %collective-permute-done.2.refs_2_, bf16[128,5120]{1,0:T(8,128)(2,1)} %collective-permute-done.refs_3_, f32[2,512,512]{2,1,0:T(8,128)} %head_products.1.refs_4_, ...), custom_call_target="tpu_custom_call" | custom-call | flops 1744830464 | bytes 10485760 | tf_op jit(solution)/shard_map/late_grads/pallas_call | solution.py:115
  249.6 8.0 %out_rows.3 = bf16[4,256,1792]{2,1,0:T(8,128)(2,1)} custom-call(s32[1]{0:T(128)} %bitcast.1.me_ref, bf16[512,512]{1,0:T(8,128)(2,1)} %late_grads.2.h0_ref, bf16[512,512]{1,0:T(8,128)(2,1)} %late_grads.3.h1_ref, bf16[2,3584,256]{2,1,0:T(8,128)(2,1)} %gate_ref.5, bf16[2,3584,256]{2,1,0:T(8,128)(2,1)} %up_ref.5), custom_call_target="tpu_custom_call" | custom-call | flops 1879048192 | bytes 8388608 | tf_op jit(solution)/shard_map/out_rows/pallas_call | solution.py:157
  257.6 8.0 %out_rows.2 = bf16[4,256,1792]{2,1,0:T(8,128)(2,1)} custom-call(s32[1]{0:T(128)} %bitcast.1.me_ref, bf16[512,512]{1,0:T(8,128)(2,1)} %late_grads.2.h0_ref, bf16[512,512]{1,0:T(8,128)(2,1)} %late_grads.3.h1_ref, bf16[2,3584,256]{2,1,0:T(8,128)(2,1)} %gate_ref.5, bf16[2,3584,256]{2,1,0:T(8,128)(2,1)} %up_ref.5), custom_call_target="tpu_custom_call" | custom-call | flops 1879048192 | bytes 8388608 | tf_op jit(solution)/shard_map/out_rows/pallas_call | solution.py:157
  265.6 35.5 %reduce-scatter.5.cloned.1.call-done = bf16[256,1792]{1,0:T(8,128)(2,1)} async-done(((bf16[1024,1792]{1,0:T(8,128)(2,1)}), bf16[256,1792]{1,0:T(8,128)(2,1)}) %reduce-scatter.5.cloned.1.call-update) | async-done | bytes 917520 | tf_op jit(solution)/shard_map/sum_blocks/reduce_scatter | solution.py:260
  301.2 2.8 copy.81
  304.0 10.6 %all-to-all-start.3 = ((bf16[64,4,1792]{2,1,0:T(4,128)(2,1)}), bf16[64,4,1792]{2,1,0:T(4,128)(2,1)S(1)}, u32[]{:S(2)}, u32[]{:S(2)}) async-start(bf16[64,4,1792]{2,1,0:T(4,128)(2,1)} %copy.81), calls=%async_computation.5 | async-start | bytes 1835008 | tf_op jit(solution)/shard_map/return_slots/all_to_all | solution.py:265
  314.6 34.0 %reduce-scatter.3.cloned.1.call-done = bf16[256,1792]{1,0:T(8,128)(2,1)} async-done(((bf16[1024,1792]{1,0:T(8,128)(2,1)}), bf16[256,1792]{1,0:T(8,128)(2,1)}) %reduce-scatter.3.cloned.1.call-update) | async-done | bytes 917520 | tf_op jit(solution)/shard_map/sum_blocks/reduce_scatter | solution.py:260
  348.6 2.8 copy.80
  351.4 10.6 %all-to-all-start.2 = ((bf16[64,4,1792]{2,1,0:T(4,128)(2,1)}), bf16[64,4,1792]{2,1,0:T(4,128)(2,1)S(1)}, u32[]{:S(2)}, u32[]{:S(2)}) async-start(bf16[64,4,1792]{2,1,0:T(4,128)(2,1)} %copy.80), calls=%async_computation.3 | async-start | bytes 1835008 | tf_op jit(solution)/shard_map/return_slots/all_to_all | solution.py:265
  362.2 0.2 reshape.177
  362.4 0.3 convolution_convert_fusion.2
  362.7 25.2 %all-to-all-done.2 = bf16[64,4,1792]{2,1,0:T(4,128)(2,1)S(1)} async-done(((bf16[64,4,1792]{2,1,0:T(4,128)(2,1)}), bf16[64,4,1792]{2,1,0:T(4,128)(2,1)S(1)}, u32[]{:S(2)}, u32[]{:S(2)}) %all-to-all-start.2) | async-done | bytes 917536 | tf_op jit(solution)/shard_map/return_slots/all_to_all | solution.py:265
  387.8 0.2 reshape.174
  388.0 0.3 convolution_convert_fusion.3
  388.3 0.7 pad_maximum_fusion.2
  (59 shorter events, 2.4 us)
Async XLA Ops:
  6.5 19.3 %copy-start = (bf16[16,3584]{1,0:T(8,128)(2,1)S(1)}, bf16[16,3584]{1,0:T(8,128)(2,1)}, u32[]{:S(2)}) copy-start(bf16[16,3584]{1,0:T(8,128)(2,1)} %param.8) | copy-start | bytes 344068
  6.5 18.9 %copy-start.5 = (bf16[16,3584]{1,0:T(8,128)(2,1)S(1)}, bf16[16,3584]{1,0:T(8,128)(2,1)}, u32[]{:S(2)}) copy-start(bf16[16,3584]{1,0:T(8,128)(2,1)} %param.7) | copy-start | bytes 344068
  6.5 203.7 %all-gather.3.cloned.1.call-start = ((), (), s32[]{:S(2)}) async-start(), calls=%async_computation.6 | async-start | bytes 17039360 | tf_op jit(solution)/shard_map/gather_tokens/all_gather | solution.py:190
  29.1 56.8 %all-to-all-start = ((bf16[64,2,5248]{2,1,0:T(2,128)(2,1)}), bf16[64,2,5248]{2,1,0:T(2,128)(2,1)S(1)}, u32[]{:S(2)}, u32[]{:S(2)}) async-start(bf16[64,2,5248]{2,1,0:T(2,128)(2,1)} %pad_maximum_fusion), calls=%async_computation | async-start | bytes 2686976 | tf_op jit(solution)/shard_map/send_first/all_to_all | solution.py:215
  86.2 57.1 %copy-start.2 = (bf16[128,5120]{1,0:T(8,128)(2,1)}, bf16[128,5120]{1,0:T(8,128)(2,1)S(1)}, u32[]{:S(2)}) copy-start(bf16[128,5120]{1,0:T(8,128)(2,1)S(1)} %slice.39.refs_0_) | copy-start | bytes 3932164
  86.2 54.4 %all-to-all-start.1 = ((bf16[64,2,5120]{2,1,0:T(2,128)(2,1)}), bf16[64,2,5120]{2,1,0:T(2,128)(2,1)}, u32[]{:S(2)}, u32[]{:S(2)}) async-start(bf16[64,2,5120]{2,1,0:T(2,128)(2,1)} %reshape.167), calls=%async_computation.1 | async-start | bytes 2621440 | tf_op jit(solution)/shard_map/send_second/all_to_all | solution.py:215
  92.1 209.1 %reduce-scatter.5.cloned.1.call-start = ((), (), s32[]{:S(2)}) async-start(), calls=%async_computation.8 | async-start | bytes 4587520 | tf_op jit(solution)/shard_map/sum_blocks/reduce_scatter | solution.py:260
  92.2 30.1 %collective-permute-start.1 = (bf16[128,5120]{1,0:T(8,128)(2,1)S(1)}, bf16[128,5120]{1,0:T(8,128)(2,1)S(1)}, u32[]{:S(2)}, u32[]{:S(2)}) collective-permute-start(bf16[128,5120]{1,0:T(8,128)(2,1)S(1)} %slice.39.refs_0_), channel_id=1, source_target_pairs={{0,192},{64,0},{128,64},{192,128},{1,193},{65,1},{129,65},{193,129... | collective-permute-start | bytes 3932168 | tf_op jit(solution)/shard_map/ring_first/ppermute | solution.py:227
  94.7 30.8 %collective-permute-start = (bf16[128,5120]{1,0:T(8,128)(2,1)S(1)}, bf16[128,5120]{1,0:T(8,128)(2,1)}, u32[]{:S(2)}, u32[]{:S(2)}) collective-permute-start(bf16[128,5120]{1,0:T(8,128)(2,1)S(1)} %slice.39.refs_0_), channel_id=1, source_target_pairs={{0,64},{64,128},{128,192},{192,0},{1,65},{65,129},{129,193},{193,1... | collective-permute-start | bytes 3932168 | tf_op jit(solution)/shard_map/ring_first/ppermute | solution.py:226
  122.3 1.1 copy-start.3
  143.3 30.5 %collective-permute-start.3 = (bf16[128,5120]{1,0:T(8,128)(2,1)}, bf16[128,5120]{1,0:T(8,128)(2,1)S(1)}, u32[]{:S(2)}, u32[]{:S(2)}) collective-permute-start(bf16[128,5120]{1,0:T(8,128)(2,1)} %bitcast.13.refs_0_), channel_id=1, source_target_pairs={{0,192},{64,0},{128,64},{192,128},{1,193},{65,1},{129,65},{193,129... | collective-permute-start | bytes 3932168 | tf_op jit(solution)/shard_map/ring_second/ppermute | solution.py:235
  145.8 83.0 %collective-permute-start.5 = (bf16[128,5120]{1,0:T(8,128)(2,1)}, bf16[128,5120]{1,0:T(8,128)(2,1)}, u32[]{:S(2)}, u32[]{:S(2)}) collective-permute-start(bf16[128,5120]{1,0:T(8,128)(2,1)} %bitcast.13.refs_0_), channel_id=1, source_target_pairs={{0,64},{64,128},{128,192},{192,0},{1,65},{65,129},{129,193},{193,1... | collective-permute-start | bytes 3932168 | tf_op jit(solution)/shard_map/ring_second/ppermute | solution.py:236
  173.8 54.9 %copy-start.4 = (bf16[128,5120]{1,0:T(8,128)(2,1)}, bf16[128,5120]{1,0:T(8,128)(2,1)S(1)}, u32[]{:S(2)}) copy-start(bf16[128,5120]{1,0:T(8,128)(2,1)S(1)} %collective-permute-done.3.refs_1_) | copy-start | bytes 3932164
  173.8 54.9 %collective-permute-start.4 = (bf16[128,5120]{1,0:T(8,128)(2,1)S(1)}, bf16[128,5120]{1,0:T(8,128)(2,1)}, u32[]{:S(2)}, u32[]{:S(2)}) collective-permute-start(bf16[128,5120]{1,0:T(8,128)(2,1)S(1)} %collective-permute-done.3.refs_1_), channel_id=1, source_target_pairs={{0,192},{64,0},{128,64},{192,128},{1,193},{65,1},{129,65},{193,129... | collective-permute-start | bytes 3932168 | tf_op jit(solution)/shard_map/ring_second/ppermute | solution.py:237
  177.1 62.0 %collective-permute-start.2 = (bf16[128,5120]{1,0:T(8,128)(2,1)}, bf16[128,5120]{1,0:T(8,128)(2,1)}, u32[]{:S(2)}, u32[]{:S(2)}) collective-permute-start(bf16[128,5120]{1,0:T(8,128)(2,1)} %collective-permute-done.refs_3_), channel_id=1, source_target_pairs={{0,64},{64,128},{128,192},{192,0},{1,65},{65,129},{129,193},{193,1... | collective-permute-start | bytes 3932168 | tf_op jit(solution)/shard_map/ring_far/ppermute | solution.py:233
  257.6 91.0 %reduce-scatter.3.cloned.1.call-start = ((), (), s32[]{:S(2)}) async-start(), calls=%async_computation.7 | async-start | bytes 4587520 | tf_op jit(solution)/shard_map/sum_blocks/reduce_scatter | solution.py:260
  304.0 47.5 %all-to-all-start.3 = ((bf16[64,4,1792]{2,1,0:T(4,128)(2,1)}), bf16[64,4,1792]{2,1,0:T(4,128)(2,1)S(1)}, u32[]{:S(2)}, u32[]{:S(2)}) async-start(bf16[64,4,1792]{2,1,0:T(4,128)(2,1)} %copy.81), calls=%async_computation.5 | async-start | bytes 1835008 | tf_op jit(solution)/shard_map/return_slots/all_to_all | solution.py:265
  351.4 36.4 %all-to-all-start.2 = ((bf16[64,4,1792]{2,1,0:T(4,128)(2,1)}), bf16[64,4,1792]{2,1,0:T(4,128)(2,1)S(1)}, u32[]{:S(2)}, u32[]{:S(2)}) async-start(bf16[64,4,1792]{2,1,0:T(4,128)(2,1)} %copy.80), calls=%async_computation.3 | async-start | bytes 1835008 | tf_op jit(solution)/shard_map/return_slots/all_to_all | solution.py:265
  362.2 26.8 %copy-start.1 = (bf16[16,3584]{1,0:T(8,128)(2,1)S(1)}, bf16[16,3584]{1,0:T(8,128)(2,1)}, u32[]{:S(2)}) copy-start(bf16[16,3584]{1,0:T(8,128)(2,1)} %param.8) | copy-start | bytes 344068
Sparse Core Ops, SparseCore 0:
  19.4 140.7 all-gather.2
  257.7 43.4 reduce-scatter.4
  303.7 44.8 reduce-scatter.2

commit v3 on v2

v3 whole, which is shorter than its diff:
```python
import jax
import jax.numpy as jnp
from jax import lax
from jax.experimental import pallas as pl
from jax.experimental.pallas import tpu as pltpu
from jax.sharding import PartitionSpec as P

CAP = 2
LANES = 128
BLOCK = 256
CHUNKS = 2
HEAD = 1792
STEP = 512
TAIL_STEP = 256
NT = (((1,), (1,)), ((), ()))


def slot_table(ids, probs, experts):
    tok_count = ids.shape[0]
    named = ids.T[None, :, :] == jnp.arange(experts, dtype=jnp.int32)[:, None, None]
    mask = jnp.any(named, axis=1)
    scale = jnp.sum(jnp.where(named, probs.T[None, :, :], 0.0), axis=1)
    order = jnp.arange(tok_count, dtype=jnp.int32)
    before = (order[:, None] < order[None, :])[None, :, :]
    rank = jnp.sum((mask[:, :, None] & before).astype(jnp.int32), axis=1)
    slots = mask[:, None, :] & (rank[:, None, :] == jnp.arange(CAP, dtype=jnp.int32)[None, :, None])
    slot_scale = jnp.sum(jnp.where(slots, scale[:, None, :], 0.0), axis=2)
    return slots.reshape(experts * CAP, tok_count), slot_scale.reshape(experts * CAP)


def head_kernel(first_ref, x_ref, gate_ref, up_ref, out_ref, picked):
    group = pl.program_id(0)
    head = gate_ref.shape[1]
    columns, _, tok_count, _ = x_ref.shape
    sources = BLOCK // tok_count
    from_tok = lax.broadcasted_iota(jnp.int32, (BLOCK, BLOCK), 0)
    to_tok = lax.broadcasted_iota(jnp.int32, (BLOCK, BLOCK), 1)
    earlier = ((from_tok // tok_count == to_tok // tok_count) & (from_tok < to_tok)).astype(jnp.bfloat16)
    ones = jnp.ones((sources, LANES), jnp.bfloat16)
    mine = lax.broadcasted_iota(jnp.int32, (sources, BLOCK), 0) == (
        lax.broadcasted_iota(jnp.int32, (sources, BLOCK), 1) // tok_count
    )
    for block in range(columns // sources):
        part = pl.ds(block * sources, sources)
        ids = x_ref[part, :, :, head:].reshape(BLOCK, LANES).astype(jnp.float32)
        picks = []
        for e in range(2):
            named = (ids == (first_ref[0] + e).astype(jnp.float32)).astype(jnp.bfloat16)
            mask = lax.dot_general(ones, named, NT, preferred_element_type=jnp.float32)
            rank = jnp.dot(mask.astype(jnp.bfloat16), earlier, preferred_element_type=jnp.float32)
            for c in range(CAP):
                chosen = mine & (mask > 0.5) & (jnp.abs(rank - c) < 0.5)
                picks.append(jnp.where(chosen, 1.0, 0.0).astype(jnp.bfloat16))
        x = x_ref[part, :, :, :head].reshape(BLOCK, head)
        rows = jnp.dot(jnp.concatenate(picks, axis=0), x, preferred_element_type=jnp.float32).astype(jnp.bfloat16)
        for slot in range(4):
            at = pl.multiple_of((group * CAP + slot % CAP) * columns + block * sources, 16)
            picked[slot // CAP, pl.ds(at, sources), :] = rows[slot * sources : (slot + 1) * sources]

    @pl.when(group == pl.num_programs(0) - 1)
    def _():
        units = gate_ref.shape[2]
        for e in range(2):
            out_ref[e, :, :units] = jnp.dot(picked[e], gate_ref[e], preferred_element_type=jnp.float32)
            out_ref[e, :, units:] = jnp.dot(picked[e], up_ref[e], preferred_element_type=jnp.float32)


def head_products(first, x_all, w_gate, w_up):
    columns, groups, tok_count, wide = x_all.shape
    head = wide - LANES
    local_experts, _, units = w_gate.shape
    rows = columns * groups * CAP
    w_spec = pl.BlockSpec((local_experts, head, units), lambda i, first: (0, 0, 0))
    return pl.pallas_call(
        head_kernel,
        out_shape=jax.ShapeDtypeStruct((local_experts, rows, 2 * units), jnp.float32),
        grid_spec=pltpu.PrefetchScalarGridSpec(
            num_scalar_prefetch=1,
            grid=(groups,),
            in_specs=[
                pl.BlockSpec((columns, 1, tok_count, wide), lambda i, first: (0, i, 0, 0)),
                w_spec,
                w_spec,
            ],
            out_specs=pl.BlockSpec((local_experts, rows, 2 * units), lambda i, first: (0, 0, 0)),
            scratch_shapes=[pltpu.VMEM((local_experts, rows, head), jnp.bfloat16)],
        ),
        compiler_params=pltpu.CompilerParams(dimension_semantics=("arbitrary",)),
        cost_estimate=pl.CostEstimate(
            flops=2 * local_experts * rows * 2 * units * head + rows * BLOCK * head,
            bytes_accessed=20 << 20,
            transcendentals=0,
        ),
        name="head_products",
    )(first, x_all, w_gate, w_up)


def hidden_kernel(own_ref, right_ref, far_ref, left_ref, down_ref, out_ref):
    @pl.when(pl.program_id(0) == 0)
    def _():
        out_ref[...] = jnp.zeros_like(out_ref)

    rows = jnp.concatenate([own_ref[...], right_ref[...], far_ref[...], left_ref[...]], axis=0)
    out_ref[...] += lax.dot_general(rows, down_ref[0], NT, preferred_element_type=jnp.float32)


def hidden_grads(e, parts, w_down):
    _, units, _ = w_down.shape
    count, wide = parts[0].shape
    slot_spec = pl.BlockSpec((count, STEP), lambda k: (0, k))
    return pl.pallas_call(
        hidden_kernel,
        out_shape=jax.ShapeDtypeStruct((4 * count, units), jnp.float32),
        grid=(wide // STEP,),
        in_specs=[slot_spec] * 4 + [pl.BlockSpec((1, units, STEP), lambda k: (e, 0, k))],
        out_specs=pl.BlockSpec((4 * count, units), lambda k: (0, 0)),
        compiler_params=pltpu.CompilerParams(dimension_semantics=("arbitrary",)),
        cost_estimate=pl.CostEstimate(flops=8 * count * units * wide, bytes_accessed=5 << 20, transcendentals=0),
        name="hidden_grads",
    )(*parts, w_down)


def late_kernel(own_ref, right_ref, far_ref, left_ref, hidden_ref, head_ref, gate_ref, up_ref, out_ref, pre):
    step = pl.program_id(0)
    units = gate_ref.shape[2]

    @pl.when(step == 0)
    def _():
        pre[...] = head_ref[0]

    rows = jnp.concatenate([own_ref[...], right_ref[...], far_ref[...], left_ref[...]], axis=0)
    pre[:, :units] += jnp.dot(rows, gate_ref[0], preferred_element_type=jnp.float32)
    pre[:, units:] += jnp.dot(rows, up_ref[0], preferred_element_type=jnp.float32)

    @pl.when(step == pl.num_programs(0) - 1)
    def _():
        gate_pre, up_pre, grad = pre[:, :units], pre[:, units:], hidden_ref[...]
        s = jax.nn.sigmoid(gate_pre)
        out_ref[:, :units] = (grad * up_pre * s * (1.0 + gate_pre * (1.0 - s))).astype(jnp.bfloat16)
        out_ref[:, units:] = (grad * gate_pre * s).astype(jnp.bfloat16)


def late_grads(e, parts, hidden, head_pre, w_gate, w_up):
    _, width, units = w_gate.shape
    count, wide = parts[0].shape
    rows = 4 * count
    slot_spec = pl.BlockSpec((count, TAIL_STEP), lambda k: (0, k))
    w_spec = pl.BlockSpec((1, TAIL_STEP, units), lambda k: (e, HEAD // TAIL_STEP + k, 0))
    return pl.pallas_call(
        late_kernel,
        out_shape=jax.ShapeDtypeStruct((rows, 2 * units), jnp.bfloat16),
        grid=(wide // TAIL_STEP,),
        in_specs=[slot_spec] * 4
        + [
            pl.BlockSpec((rows, units), lambda k: (0, 0)),
            pl.BlockSpec((1, rows, 2 * units), lambda k: (e, 0, 0)),
            w_spec,
            w_spec,
        ],
        out_specs=pl.BlockSpec((rows, 2 * units), lambda k: (0, 0)),
        scratch_shapes=[pltpu.VMEM((rows, 2 * units), jnp.float32)],
        compiler_params=pltpu.CompilerParams(dimension_semantics=("arbitrary",)),
        cost_estimate=pl.CostEstimate(
            flops=4 * rows * units * wide, bytes_accessed=6 << 20, transcendentals=rows * units
        ),
        name="late_grads",
    )(*parts, hidden, head_pre, w_gate, w_up)


def out_kernel(me_ref, h0_ref, h1_ref, gate_ref, up_ref, out_ref):
    units = gate_ref.shape[2]
    for e, h_ref in enumerate((h0_ref, h1_ref)):
        value = lax.dot_general(h_ref[:, :units], gate_ref[e], NT, preferred_element_type=jnp.float32)
        value = value + lax.dot_general(h_ref[:, units:], up_ref[e], NT, preferred_element_type=jnp.float32)
        value = value.astype(jnp.bfloat16)
        part = value.shape[0] // 4
        for r in range(4):
            out_ref[lax.rem(me_ref[0] + r, 4), e * part : (e + 1) * part, :] = value[r * part : (r + 1) * part]


def out_rows(me, h, w_gate, w_up, chunk, chunks, cols):
    rows = h[0].shape[0]
    local_experts, width, units = w_gate.shape
    h_spec = pl.BlockSpec((rows, 2 * units), lambda n, me: (0, 0))
    per = width // chunks // cols
    first = chunk * per
    w_spec = pl.BlockSpec((local_experts, cols, units), lambda n, me: (0, first + n, 0))
    return pl.pallas_call(
        out_kernel,
        out_shape=jax.ShapeDtypeStruct((4, local_experts * rows // 4, width // chunks), jnp.bfloat16),
        grid_spec=pltpu.PrefetchScalarGridSpec(
            num_scalar_prefetch=1,
            grid=(per,),
            in_specs=[
                h_spec,
                h_spec,
                w_spec,
                w_spec,
            ],
            out_specs=pl.BlockSpec((4, local_experts * rows // 4, cols), lambda n, me: (0, 0, n)),
        ),
        compiler_params=pltpu.CompilerParams(dimension_semantics=("arbitrary",)),
        cost_estimate=pl.CostEstimate(
            flops=2 * local_experts * rows * 2 * units * width // chunks, bytes_accessed=8 << 20, transcendentals=0
        ),
        name="out_rows",
    )(me, *h, w_gate, w_up)


def on_device(tokens, out_grad, route_ids, route_probs, w_gate, w_up, w_down):
    columns = lax.axis_size("expert")
    local_experts = w_gate.shape[0]
    experts = local_experts * columns
    tok_count, width = tokens.shape
    slots = experts * CAP
    per_dest = local_experts * CAP
    me = lax.axis_index("dp").astype(jnp.int32).reshape(1)
    first = (lax.axis_index("expert").astype(jnp.int32) * local_experts).reshape(1)

    up_ring = [(i, (i + 1) % 4) for i in range(4)]
    down_ring = [(i, (i + 3) % 4) for i in range(4)]
    far_ring = [(i, (i + 2) % 4) for i in range(4)]

    def forward(parts, upward):
        return lax.ppermute(parts[3], "dp", up_ring) if upward else lax.ppermute(parts[1], "dp", down_ring)

    with jax.named_scope("gather_tokens"):
        ids = jnp.pad(route_ids.astype(jnp.bfloat16), ((0, 0), (0, LANES - route_ids.shape[1])), constant_values=-1)
        mine = jnp.concatenate([tokens[:, :HEAD], ids], axis=1)
        near = jnp.concatenate([mine] + [lax.ppermute(mine, "dp", ring) for ring in (down_ring, far_ring, up_ring)])
        x_all = lax.all_gather(near, "expert", axis=0, tiled=True).reshape(columns, 4, tok_count, HEAD + LANES)

    with jax.named_scope("build_slots"):
        table, slot_scale = slot_table(route_ids, route_probs, experts)
        select = table.astype(jnp.bfloat16)
        tiles = {}
        for e in range(2):
            choose = select.reshape(columns, local_experts, CAP, tok_count)[:, e].reshape(columns * CAP, tok_count)
            scale = slot_scale.reshape(columns, local_experts, CAP)[:, e].reshape(columns * CAP, 1)
            g_rows = jnp.dot(choose, out_grad, preferred_element_type=jnp.float32) * scale
            x_rows = jnp.dot(choose, tokens[:, HEAD:], preferred_element_type=jnp.float32)
            tiles["g", e] = g_rows.astype(jnp.bfloat16).reshape(columns, CAP, -1)
            tiles["x", e] = x_rows.astype(jnp.bfloat16).reshape(columns, CAP, -1)

    order = (("x", 0), ("g", 0), ("g", 1), ("x", 1))
    upward = (False, True, False, True)
    sent = {}
    for n, name in enumerate(order):
        tile = tiles[name]
        last = sent[order[n - 1]] if n else None
        with jax.named_scope("send_slots"):
            if n:
                tile, _ = lax.optimization_barrier((tile, last[0]))
            got = lax.all_to_all(tile, "expert", split_axis=0, concat_axis=0, tiled=True)
            if n == len(order) - 1:
                head_pre = head_products(first, x_all, w_gate, w_up)
                got, last[1], last[3], head_pre = lax.optimization_barrier((got, last[1], last[3], head_pre))
            elif n == 2:
                early = sent[order[0]]
                got, last[1], last[3], early[2] = lax.optimization_barrier((got, last[1], last[3], early[2]))
            elif n:
                got, last[1], last[3] = lax.optimization_barrier((got, last[1], last[3]))
            own = got.transpose(1, 0, 2).reshape(columns * CAP, -1)
        with jax.named_scope("ring"):
            if n:
                last[2] = forward(last, upward[n - 1])
            right = lax.ppermute(own, "dp", down_ring)
            left = lax.ppermute(own, "dp", up_ring)
            sent[name] = [own, right, None, left]

    hidden = hidden_grads(0, sent["g", 0], w_down)
    h = [late_grads(0, sent["x", 0], hidden, head_pre, w_gate, w_up)]
    with jax.named_scope("ring"):
        final = sent["x", 1]
        final[2] = forward(final, upward[3])
    hidden = hidden_grads(1, sent["g", 1], w_down)
    h.append(late_grads(1, final, hidden, head_pre, w_gate, w_up))

    results = []
    for chunk in range(CHUNKS):
        cols = width // CHUNKS
        partials = out_rows(me, h, w_gate, w_up, chunk, CHUNKS, 256)
        with jax.named_scope("sum_blocks"):
            summed = lax.psum_scatter(
                partials.reshape(4 * slots, cols), "dp", scatter_dimension=0, tiled=True
            )
        with jax.named_scope("return_slots"):
            back = summed.reshape(per_dest, columns, cols).transpose(1, 0, 2)
            returned = lax.all_to_all(back, "expert", split_axis=0, concat_axis=0, tiled=True)
        with jax.named_scope("combine"):
            results.append(
                lax.dot_general(
                    select, returned.reshape(slots, cols), (((0,), (0,)), ((), ())),
                    preferred_element_type=jnp.float32,
                ).astype(jnp.bfloat16)
            )
    return jnp.concatenate(results, axis=1)


def solution(mesh):
    placed = (
        P(("dp", "expert"), None),
        P(("dp", "expert"), None),
        P(("dp", "expert"), None),
        P(("dp", "expert"), None),
        P("expert", None, "dp"),
        P("expert", None, "dp"),
        P("expert", "dp", None),
    )
    return jax.shard_map(
        on_device, mesh=mesh, in_specs=placed, out_specs=P(("dp", "expert"), None), check_vma=False
    )
```

time: 397 us -> 364 us (0.917)
  blocking collectives: 43.2 us -> 0 us
  starting transfers between devices: 50.1 us -> 77.5 us
  waiting for transfers between devices: 208 us -> 191 us
  other arithmetic: 8.77 us -> 3.53 us
    all_gather x2 -> x0, blocking collectives: 43.2 us -> none  [the longest x1 31.4 us: on_device(): tags = lax.all_gather(own_tags.reshape(2, half), 'dp', axis=0, tiled=True)]
    all_to_all x2 -> x4, waiting for transfers between devices: 55 us -> 38.1 us  [on_device(): lax.all_to_all(tile, 'expert', split_axis=0, concat_axis=0, tiled=True)]
    all_to_all x2 -> x4, starting transfers between devices: 20.6 us -> 36.4 us  [on_device(): lax.all_to_all(tile, 'expert', split_axis=0, concat_axis=0, tiled=True)]
    ppermute x6 -> x15, starting transfers between devices: 8.21 us -> 19.5 us  [the longest x4 10.7 us: on_device(): right = lax.ppermute(own, 'dp', down_ring)]
    pallas_call x2 -> x4, Pallas kernels: 20.9 us -> 28.8 us  [the longest x2 14.7 us: late_grads(): pl.pallas_call(late_kernel, out_shape=jax.ShapeDtypeStruct((rows, 2 * uni...]
    pallas_call x1, Pallas kernels: 18.5 us -> 14.1 us  [head_products(): pl.pallas_call(head_kernel, out_shape=jax.ShapeDtypeStruct((local_experts...]
    ppermute x6 -> x15, waiting for transfers between devices: 57.8 us -> 56.6 us  [the longest x2 27.7 us: forward(): lax.ppermute(parts[1], 'dp', down_ring)]
  transfers between devices with their start and end apart: 13 -> 24, of which waited for: 8 -> 12; matrix products, arithmetic and copies ran while one was open for 6% -> 4% of each run, Pallas kernels for 9% -> 12%
where the time goes in v3:
time: 364 us; the launch traced here: 362 us
  waiting for transfers between devices  191 us (52%)
  starting transfers between devices  77.5 us (21%)
  Pallas kernels  58.8 us (16%)
  local copies, waits for them, and re-layouts  15.6 us (4%)
  between operations  13.5 us (4%)
    reduce_scatter x2, waiting for transfers between devices, on_device(): lax.psum_scatter(partials.reshape(4 * slots, cols), 'dp', scatter_dimensi...  70.8 us
    all_to_all x4, waiting for transfers between devices, on_device(): lax.all_to_all(tile, 'expert', split_axis=0, concat_axis=0, tiled=True)  38.1 us
    all_to_all x4, starting transfers between devices, on_device(): lax.all_to_all(tile, 'expert', split_axis=0, concat_axis=0, tiled=True)  36.4 us
    ppermute x2, waiting for transfers between devices, forward(): lax.ppermute(parts[1], 'dp', down_ring)  27.7 us
    ppermute x4, waiting for transfers between devices, on_device(): left = lax.ppermute(own, 'dp', up_ring)  26.7 us
    all_to_all x2, waiting for transfers between devices, on_device(): lax.all_to_all(back, 'expert', split_axis=0, concat_axis=0, tiled=True)  25.2 us
    all_to_all x2, starting transfers between devices, on_device(): lax.all_to_all(back, 'expert', split_axis=0, concat_axis=0, tiled=True)  21.3 us
    pallas_call x2, Pallas kernels, out_rows(): pl.pallas_call(out_kernel, out_shape=jax.ShapeDtypeStruct((4, local_exper...  15.9 us
  transfers between devices with their start and end apart: 24, of which 12 were waited for; matrix products, arithmetic and copies ran while one was open for 4% of the time, Pallas kernels for 12%

profile of v3, /device:TPU:1, one launch (start us, length us, event | category | flops | bytes accessed | tf_op | source)
XLA Modules:
  0.0 362.3 jit_solution(16298253139817575485)
XLA Ops:
  6.5 0.8 convert_element_type.32
  7.4 0.8 slice.24
  8.2 2.1 collective-permute-start.10
  10.4 2.5 collective-permute-start.9
  12.8 1.2 collective-permute-start.8
  14.0 1.3 collective-permute-done.9
  15.2 0.9 collective-permute-done.8
  16.2 0.7 pad_maximum_fusion
  16.9 0.8 fusion.2
  18.4 1.1 convolution_convert_fusion.1
  19.5 1.0 reshape.142
  20.4 13.7 %all-to-all-start = ((bf16[64,2,1792]{2,1,0:T(2,128)(2,1)}), bf16[64,2,1792]{2,1,0:T(2,128)(2,1)S(1)}, u32[]{:S(2)}, u32[]{:S(2)}) async-start(bf16[64,2,1792]{2,1,0:T(2,128)(2,1)} %reshape.142), calls=%async_computation | async-start | bytes 917504 | tf_op jit(solution)/shard_map/send_slots/all_to_all | solution.py:254
  35.4 1.3 reshape.145
  36.7 17.8 %all-to-all-done = bf16[64,2,1792]{2,1,0:T(2,128)(2,1)S(1)} async-done(((bf16[64,2,1792]{2,1,0:T(2,128)(2,1)}), bf16[64,2,1792]{2,1,0:T(2,128)(2,1)S(1)}, u32[]{:S(2)}, u32[]{:S(2)}) %all-to-all-start) | async-done | bytes 458784 | tf_op jit(solution)/shard_map/send_slots/all_to_all | solution.py:254
  54.5 6.4 %all-to-all-start.1 = ((bf16[64,2,3584]{2,1,0:T(2,128)(2,1)}), bf16[64,2,3584]{2,1,0:T(2,128)(2,1)S(1)}, u32[]{:S(2)}, u32[]{:S(2)}) async-start(bf16[64,2,3584]{2,1,0:T(2,128)(2,1)} %reshape.145), calls=%async_computation.1 | async-start | bytes 1835008 | tf_op jit(solution)/shard_map/send_slots/all_to_all | solution.py:254
  61.0 2.7 collective-permute-start
  64.2 1.3 reshape.146
  65.5 8.3 %collective-permute-done.1.left_ref = bf16[128,1792]{1,0:T(8,128)(2,1)S(1)} collective-permute-done((bf16[128,1792]{1,0:T(8,128)(2,1)S(1)}, bf16[128,1792]{1,0:T(8,128)(2,1)S(1)}, u32[]{:S(2)}, u32[]{:S(2)}) %collective-permute-start.1) | collective-permute-done | bytes 458784 | tf_op jit(solution)/shard_map/ring/ppermute | solution.py:268
  73.8 15.4 %all-to-all-done.1 = bf16[64,2,3584]{2,1,0:T(2,128)(2,1)S(1)} async-done(((bf16[64,2,3584]{2,1,0:T(2,128)(2,1)}), bf16[64,2,3584]{2,1,0:T(2,128)(2,1)S(1)}, u32[]{:S(2)}, u32[]{:S(2)}) %all-to-all-start.1) | async-done | bytes 917536 | tf_op jit(solution)/shard_map/send_slots/all_to_all | solution.py:254
  89.4 6.7 %all-to-all-start.2 = ((bf16[64,2,3584]{2,1,0:T(2,128)(2,1)}), bf16[64,2,3584]{2,1,0:T(2,128)(2,1)S(1)}, u32[]{:S(2)}, u32[]{:S(2)}) async-start(bf16[64,2,3584]{2,1,0:T(2,128)(2,1)} %reshape.146), calls=%async_computation.2 | async-start | bytes 1835008 | tf_op jit(solution)/shard_map/send_slots/all_to_all | solution.py:254
  96.2 2.7 collective-permute-start.2
  98.9 1.1 collective-permute-start.4
  100.0 27.7 %collective-permute-done.4.far_ref = bf16[128,1792]{1,0:T(8,128)(2,1)S(1)} collective-permute-done((bf16[128,1792]{1,0:T(8,128)(2,1)S(1)}, bf16[128,1792]{1,0:T(8,128)(2,1)S(1)}, u32[]{:S(2)}, u32[]{:S(2)}) %collective-permute-start.4) | collective-permute-done | bytes 458784 | tf_op jit(solution)/shard_map/ring/ppermute | solution.py:225
  127.7 0.9 copy-done.5
  128.6 3.2 all-to-all-done.2
  132.1 2.7 collective-permute-start.6
  135.0 1.0 reshape.148
  136.0 9.5 %all-to-all-start.3 = ((bf16[64,2,1792]{2,1,0:T(2,128)(2,1)}), bf16[64,2,1792]{2,1,0:T(2,128)(2,1)S(1)}, u32[]{:S(2)}, u32[]{:S(2)}) async-start(bf16[64,2,1792]{2,1,0:T(2,128)(2,1)} %reshape.148), calls=%async_computation.3 | async-start | bytes 917504 | tf_op jit(solution)/shard_map/send_slots/all_to_all | solution.py:254
  145.8 14.1 %head_products.1.head_ref = f32[2,512,512]{2,1,0:T(8,128)} custom-call(s32[1]{0:T(128)} %bitcast.11.first_ref, bf16[64,4,16,1920]{3,2,1,0:T(8,128)(2,1)} %bitcast.37, bf16[2,3584,256]{2,1,0:T(8,128)(2,1)} %gate_ref.9, bf16[2,3584,256]{2,1,0:T(8,128)(2,1)} %up_ref.9), custom_call_target="tpu_custom_call" | custom-call | flops 2113929216 | bytes 20971520 | tf_op jit(solution)/shard_map/send_slots/head_products/pallas_call | solution.py:74
  159.8 1.7 all-to-all-done.3
  161.5 1.7 collective-permute-start.14
  163.3 2.7 collective-permute-start.11
  166.0 18.3 %collective-permute-done.12.left_ref = bf16[128,1792]{1,0:T(8,128)(2,1)S(1)} collective-permute-done((bf16[128,1792]{1,0:T(8,128)(2,1)S(1)}, bf16[128,1792]{1,0:T(8,128)(2,1)S(1)}, u32[]{:S(2)}, u32[]{:S(2)}) %collective-permute-start.12) | collective-permute-done | bytes 458784 | tf_op jit(solution)/shard_map/ring/ppermute | solution.py:268
  184.3 1.0 copy-done.7
  185.3 7.0 %hidden_grads.2.hidden_ref = f32[512,256]{1,0:T(8,128)} custom-call(bf16[128,3584]{1,0:T(8,128)(2,1)} %bitcast.44, bf16[128,3584]{1,0:T(8,128)(2,1)} %collective-permute-done.2.right_ref, bf16[128,3584]{1,0:T(8,128)(2,1)} %copy-done.7, bf16[128,3584]{1,0:T(8,128)(2,1)} %copy-done.5, bf16[2,256,3584]{2,1,0:T(8,128)(2,1)} %down_ref.3), custom_call_target="tpu_custom_call" | custom-call | flops 939524096 | bytes 5242880 | tf_op jit(solution)/shard_map/hidden_grads/pallas_call | solution.py:111
  192.3 7.4 %late_grads.2.h0_ref = bf16[512,512]{1,0:T(8,128)(2,1)} custom-call(bf16[128,1792]{1,0:T(8,128)(2,1)} %bitcast.52, bf16[128,1792]{1,0:T(8,128)(2,1)} %copy-done.9, bf16[128,1792]{1,0:T(8,128)(2,1)} %copy-done.10, bf16[128,1792]{1,0:T(8,128)(2,1)} %copy-done.8, f32[512,256]{1,0:T(8,128)} %hidden_grads.2.hidden_ref, f32[2,512,512]{2,1,0:T(8,128)} %head_products.1.head_ref, ...), custom_call_target="tpu_custom_call" | custom-call | flops 939524096 | bytes 6291456 | tf_op jit(solution)/shard_map/late_grads/pallas_call | solution.py:149
  199.7 7.0 %hidden_grads.3.hidden_ref = f32[512,256]{1,0:T(8,128)} custom-call(bf16[128,3584]{1,0:T(8,128)(2,1)} %bitcast.47, bf16[128,3584]{1,0:T(8,128)(2,1)} %collective-permute-done.6.right_ref, bf16[128,3584]{1,0:T(8,128)(2,1)} %collective-permute-done.14.far_ref, bf16[128,3584]{1,0:T(8,128)(2,1)} %collective-permute-done.7.left_ref, bf16[2,256,3584]{2,1,0:T(8,128)(2,1)} %down_ref.3), custom_call_target="tpu_custom_call" | custom-call | flops 939524096 | bytes 5242880 | tf_op jit(solution)/shard_map/hidden_grads/pallas_call | solution.py:111
  206.8 0.8 copy-done.12
  207.6 7.4 %late_grads.3.h1_ref = bf16[512,512]{1,0:T(8,128)(2,1)} custom-call(bf16[128,1792]{1,0:T(8,128)(2,1)} %bitcast.55, bf16[128,1792]{1,0:T(8,128)(2,1)} %copy-done.12, bf16[128,1792]{1,0:T(8,128)(2,1)} %collective-permute-done.13.far_ref, bf16[128,1792]{1,0:T(8,128)(2,1)} %copy-done.11, f32[512,256]{1,0:T(8,128)} %hidden_grads.3.hidden_ref, ...), custom_call_target="tpu_custom_call" | custom-call | flops 939524096 | bytes 6291456 | tf_op jit(solution)/shard_map/late_grads/pallas_call | solution.py:149
  214.9 7.9 %out_rows.3 = bf16[4,256,1792]{2,1,0:T(8,128)(2,1)} custom-call(s32[1]{0:T(128)} %bitcast.1.me_ref, bf16[512,512]{1,0:T(8,128)(2,1)} %late_grads.2.h0_ref, bf16[512,512]{1,0:T(8,128)(2,1)} %late_grads.3.h1_ref, bf16[2,3584,256]{2,1,0:T(8,128)(2,1)} %gate_ref.9, bf16[2,3584,256]{2,1,0:T(8,128)(2,1)} %up_ref.9), custom_call_target="tpu_custom_call" | custom-call | flops 1879048192 | bytes 8388608 | tf_op jit(solution)/shard_map/out_rows/pallas_call | solution.py:188
  223.1 7.9 %out_rows.2 = bf16[4,256,1792]{2,1,0:T(8,128)(2,1)} custom-call(s32[1]{0:T(128)} %bitcast.1.me_ref, bf16[512,512]{1,0:T(8,128)(2,1)} %late_grads.2.h0_ref, bf16[512,512]{1,0:T(8,128)(2,1)} %late_grads.3.h1_ref, bf16[2,3584,256]{2,1,0:T(8,128)(2,1)} %gate_ref.9, bf16[2,3584,256]{2,1,0:T(8,128)(2,1)} %up_ref.9), custom_call_target="tpu_custom_call" | custom-call | flops 1879048192 | bytes 8388608 | tf_op jit(solution)/shard_map/out_rows/pallas_call | solution.py:188
  231.1 36.8 %reduce-scatter.5.cloned.1.call-done = bf16[256,1792]{1,0:T(8,128)(2,1)} async-done(((bf16[1024,1792]{1,0:T(8,128)(2,1)}), bf16[256,1792]{1,0:T(8,128)(2,1)}) %reduce-scatter.5.cloned.1.call-update) | async-done | bytes 917520 | tf_op jit(solution)/shard_map/sum_blocks/reduce_scatter | solution.py:284
  268.0 2.8 copy.60
  270.8 10.6 %all-to-all-start.5 = ((bf16[64,4,1792]{2,1,0:T(4,128)(2,1)}), bf16[64,4,1792]{2,1,0:T(4,128)(2,1)S(1)}, u32[]{:S(2)}, u32[]{:S(2)}) async-start(bf16[64,4,1792]{2,1,0:T(4,128)(2,1)} %copy.60), calls=%async_computation.7 | async-start | bytes 1835008 | tf_op jit(solution)/shard_map/return_slots/all_to_all | solution.py:289
  281.4 34.0 %reduce-scatter.3.cloned.1.call-done = bf16[256,1792]{1,0:T(8,128)(2,1)} async-done(((bf16[1024,1792]{1,0:T(8,128)(2,1)}), bf16[256,1792]{1,0:T(8,128)(2,1)}) %reduce-scatter.3.cloned.1.call-update) | async-done | bytes 917520 | tf_op jit(solution)/shard_map/sum_blocks/reduce_scatter | solution.py:284
  315.4 2.8 copy.59
  318.2 10.6 %all-to-all-start.4 = ((bf16[64,4,1792]{2,1,0:T(4,128)(2,1)}), bf16[64,4,1792]{2,1,0:T(4,128)(2,1)S(1)}, u32[]{:S(2)}, u32[]{:S(2)}) async-start(bf16[64,4,1792]{2,1,0:T(4,128)(2,1)} %copy.59), calls=%async_computation.5 | async-start | bytes 1835008 | tf_op jit(solution)/shard_map/return_slots/all_to_all | solution.py:289
  329.4 25.2 %all-to-all-done.4 = bf16[64,4,1792]{2,1,0:T(4,128)(2,1)S(1)} async-done(((bf16[64,4,1792]{2,1,0:T(4,128)(2,1)}), bf16[64,4,1792]{2,1,0:T(4,128)(2,1)S(1)}, u32[]{:S(2)}, u32[]{:S(2)}) %all-to-all-start.4) | async-done | bytes 917536 | tf_op jit(solution)/shard_map/return_slots/all_to_all | solution.py:289
  (86 shorter events, 5.5 us)
Async XLA Ops:
  6.5 28.4 %copy-start = (bf16[16,3584]{1,0:T(8,128)(2,1)S(1)}, bf16[16,3584]{1,0:T(8,128)(2,1)}, u32[]{:S(2)}) copy-start(bf16[16,3584]{1,0:T(8,128)(2,1)} %param.8) | copy-start | bytes 344068
  6.5 27.6 %copy-start.14 = (s32[16,8]{0,1:T(8,128)S(1)}, s32[16,8]{0,1:T(8,128)}, u32[]{:S(2)}) copy-start(s32[16,8]{0,1:T(8,128)} %param.9) | copy-start | bytes 1540
  6.5 27.6 %copy-start.15 = (f32[16,8]{0,1:T(8,128)S(1)}, f32[16,8]{0,1:T(8,128)}, u32[]{:S(2)}) copy-start(f32[16,8]{0,1:T(8,128)} %param.10) | copy-start | bytes 1540
  6.5 139.2 %all-gather.2.cloned.1.call-start = ((), (), s32[]{:S(2)}) async-start(), calls=%async_computation.8 | async-start | bytes 15974400 | tf_op jit(solution)/shard_map/gather_tokens/all_gather | solution.py:231
  8.2 5.7 %collective-permute-start.10 = (bf16[16,1920]{1,0:T(8,128)(2,1)S(1)}, bf16[16,1920]{1,0:T(8,128)(2,1)S(1)}, u32[]{:S(2)}, u32[]{:S(2)}) collective-permute-start(bf16[16,1920]{1,0:T(8,128)(2,1)S(1)} %pad_maximum_fusion.2), channel_id=1, source_target_pairs={{0,64},{64,128},{128,192},{192,0},{1,65},{65,129},{129,193},{193,1... | collective-permute-start | bytes 184328 | tf_op jit(solution)/shard_map/gather_tokens/ppermute | solution.py:230
  10.4 4.9 %collective-permute-start.9 = (bf16[16,1920]{1,0:T(8,128)(2,1)S(1)}, bf16[16,1920]{1,0:T(8,128)(2,1)S(1)}, u32[]{:S(2)}, u32[]{:S(2)}) collective-permute-start(bf16[16,1920]{1,0:T(8,128)(2,1)S(1)} %pad_maximum_fusion.2), channel_id=1, source_target_pairs={{0,128},{64,192},{128,0},{192,64},{1,129},{65,193},{129,1},{193,65... | collective-permute-start | bytes 184328 | tf_op jit(solution)/shard_map/gather_tokens/ppermute | solution.py:230
  12.8 3.4 collective-permute-start.8
  20.4 34.0 %all-to-all-start = ((bf16[64,2,1792]{2,1,0:T(2,128)(2,1)}), bf16[64,2,1792]{2,1,0:T(2,128)(2,1)S(1)}, u32[]{:S(2)}, u32[]{:S(2)}) async-start(bf16[64,2,1792]{2,1,0:T(2,128)(2,1)} %reshape.142), calls=%async_computation | async-start | bytes 917504 | tf_op jit(solution)/shard_map/send_slots/all_to_all | solution.py:254
  54.5 11.0 %copy-start.3 = (bf16[2,64,1792]{2,1,0:T(8,128)(2,1)}, bf16[2,64,1792]{2,1,0:T(8,128)(2,1)S(1)}, u32[]{:S(2)}) copy-start(bf16[2,64,1792]{2,1,0:T(8,128)(2,1)S(1)} %copy.50) | copy-start | bytes 1376260
  54.5 34.7 %all-to-all-start.1 = ((bf16[64,2,3584]{2,1,0:T(2,128)(2,1)}), bf16[64,2,3584]{2,1,0:T(2,128)(2,1)S(1)}, u32[]{:S(2)}, u32[]{:S(2)}) async-start(bf16[64,2,3584]{2,1,0:T(2,128)(2,1)} %reshape.145), calls=%async_computation.1 | async-start | bytes 1835008 | tf_op jit(solution)/shard_map/send_slots/all_to_all | solution.py:254
  60.9 12.9 %collective-permute-start.1 = (bf16[128,1792]{1,0:T(8,128)(2,1)S(1)}, bf16[128,1792]{1,0:T(8,128)(2,1)S(1)}, u32[]{:S(2)}, u32[]{:S(2)}) collective-permute-start(bf16[128,1792]{1,0:T(8,128)(2,1)S(1)} %bitcast.50), channel_id=1, source_target_pairs={{0,64},{64,128},{128,192},{192,0},{1,65},{65,129},{129,193},{193,1... | collective-permute-start | bytes 1376264 | tf_op jit(solution)/shard_map/ring/ppermute | solution.py:268
  61.0 12.8 %collective-permute-start = (bf16[128,1792]{1,0:T(8,128)(2,1)S(1)}, bf16[128,1792]{1,0:T(8,128)(2,1)S(1)}, u32[]{:S(2)}, u32[]{:S(2)}) collective-permute-start(bf16[128,1792]{1,0:T(8,128)(2,1)S(1)} %bitcast.51), channel_id=1, source_target_pairs={{0,192},{64,0},{128,64},{192,128},{1,193},{65,1},{129,65},{193,129... | collective-permute-start | bytes 1376264 | tf_op jit(solution)/shard_map/ring/ppermute | solution.py:267
  73.8 58.0 %copy-start.8 = (bf16[128,1792]{1,0:T(8,128)(2,1)}, bf16[128,1792]{1,0:T(8,128)(2,1)S(1)}, u32[]{:S(2)}) copy-start(bf16[128,1792]{1,0:T(8,128)(2,1)S(1)} %collective-permute-done.1.left_ref) | copy-start | bytes 1376260
  73.8 58.0 %copy-start.9 = (bf16[128,1792]{1,0:T(8,128)(2,1)}, bf16[128,1792]{1,0:T(8,128)(2,1)S(1)}, u32[]{:S(2)}) copy-start(bf16[128,1792]{1,0:T(8,128)(2,1)S(1)} %collective-permute-done.right_ref) | copy-start | bytes 1376260
  89.4 45.6 %copy-start.1 = (bf16[2,64,3584]{2,1,0:T(8,128)(2,1)}, bf16[2,64,3584]{2,1,0:T(8,128)(2,1)S(1)}, u32[]{:S(2)}) copy-start(bf16[2,64,3584]{2,1,0:T(8,128)(2,1)S(1)} %copy.55) | copy-start | bytes 2752516
  89.4 45.4 %copy-start.13 = (bf16[16,3584]{1,0:T(8,128)(2,1)S(1)}, bf16[16,3584]{1,0:T(8,128)(2,1)}, u32[]{:S(2)}) copy-start(bf16[16,3584]{1,0:T(8,128)(2,1)} %param.7) | copy-start | bytes 344068
  89.4 42.5 %all-to-all-start.2 = ((bf16[64,2,3584]{2,1,0:T(2,128)(2,1)}), bf16[64,2,3584]{2,1,0:T(2,128)(2,1)S(1)}, u32[]{:S(2)}, u32[]{:S(2)}) async-start(bf16[64,2,3584]{2,1,0:T(2,128)(2,1)} %reshape.146), calls=%async_computation.2 | async-start | bytes 1835008 | tf_op jit(solution)/shard_map/send_slots/all_to_all | solution.py:254
  96.1 31.6 %collective-permute-start.3 = (bf16[128,3584]{1,0:T(8,128)(2,1)S(1)}, bf16[128,3584]{1,0:T(8,128)(2,1)S(1)}, u32[]{:S(2)}, u32[]{:S(2)}) collective-permute-start(bf16[128,3584]{1,0:T(8,128)(2,1)S(1)} %bitcast.42), channel_id=1, source_target_pairs={{0,64},{64,128},{128,192},{192,0},{1,65},{65,129},{129,193},{193,1... | collective-permute-start | bytes 2752520 | tf_op jit(solution)/shard_map/ring/ppermute | solution.py:268
  96.2 32.4 %collective-permute-start.2 = (bf16[128,3584]{1,0:T(8,128)(2,1)S(1)}, bf16[128,3584]{1,0:T(8,128)(2,1)}, u32[]{:S(2)}, u32[]{:S(2)}) collective-permute-start(bf16[128,3584]{1,0:T(8,128)(2,1)S(1)} %bitcast.43), channel_id=1, source_target_pairs={{0,192},{64,0},{128,64},{192,128},{1,193},{65,1},{129,65},{193,129... | collective-permute-start | bytes 2752520 | tf_op jit(solution)/shard_map/ring/ppermute | solution.py:267
  98.9 28.8 %collective-permute-start.4 = (bf16[128,1792]{1,0:T(8,128)(2,1)S(1)}, bf16[128,1792]{1,0:T(8,128)(2,1)S(1)}, u32[]{:S(2)}, u32[]{:S(2)}) collective-permute-start(bf16[128,1792]{1,0:T(8,128)(2,1)S(1)} %collective-permute-done.right_ref), channel_id=1, source_target_pairs={{0,192},{64,0},{128,64},{192,128},{1,193},{65,1},{129,65},{193,129... | collective-permute-start | bytes 1376264 | tf_op jit(solution)/shard_map/ring/ppermute | solution.py:225
  127.7 4.2 %copy-start.10 = (bf16[128,1792]{1,0:T(8,128)(2,1)}, bf16[128,1792]{1,0:T(8,128)(2,1)S(1)}, u32[]{:S(2)}) copy-start(bf16[128,1792]{1,0:T(8,128)(2,1)S(1)} %collective-permute-done.4.far_ref) | copy-start | bytes 1376260
  127.7 1.0 copy-start.5
  132.0 27.8 %copy-start.2 = (bf16[2,64,3584]{2,1,0:T(8,128)(2,1)}, bf16[2,64,3584]{2,1,0:T(8,128)(2,1)S(1)}, u32[]{:S(2)}) copy-start(bf16[2,64,3584]{2,1,0:T(8,128)(2,1)S(1)} %copy.56) | copy-start | bytes 2752516
  132.0 13.6 %copy-start.6 = (bf16[128,3584]{1,0:T(8,128)(2,1)S(1)}, bf16[128,3584]{1,0:T(8,128)(2,1)}, u32[]{:S(2)}) copy-start(bf16[128,3584]{1,0:T(8,128)(2,1)} %copy-done.5) | copy-start | bytes 2752516
  132.0 29.5 %collective-permute-start.7 = (bf16[128,3584]{1,0:T(8,128)(2,1)S(1)}, bf16[128,3584]{1,0:T(8,128)(2,1)}, u32[]{:S(2)}, u32[]{:S(2)}) collective-permute-start(bf16[128,3584]{1,0:T(8,128)(2,1)S(1)} %bitcast.45), channel_id=1, source_target_pairs={{0,64},{64,128},{128,192},{192,0},{1,65},{65,129},{129,193},{193,1... | collective-permute-start | bytes 2752520 | tf_op jit(solution)/shard_map/ring/ppermute | solution.py:268
  132.1 29.4 %collective-permute-start.6 = (bf16[128,3584]{1,0:T(8,128)(2,1)S(1)}, bf16[128,3584]{1,0:T(8,128)(2,1)}, u32[]{:S(2)}, u32[]{:S(2)}) collective-permute-start(bf16[128,3584]{1,0:T(8,128)(2,1)S(1)} %bitcast.46), channel_id=1, source_target_pairs={{0,192},{64,0},{128,64},{192,128},{1,193},{65,1},{129,65},{193,129... | collective-permute-start | bytes 2752520 | tf_op jit(solution)/shard_map/ring/ppermute | solution.py:267
  136.0 25.5 %all-to-all-start.3 = ((bf16[64,2,1792]{2,1,0:T(2,128)(2,1)}), bf16[64,2,1792]{2,1,0:T(2,128)(2,1)S(1)}, u32[]{:S(2)}, u32[]{:S(2)}) async-start(bf16[64,2,1792]{2,1,0:T(2,128)(2,1)} %reshape.148), calls=%async_computation.3 | async-start | bytes 917504 | tf_op jit(solution)/shard_map/send_slots/all_to_all | solution.py:254
  145.6 122.4 %reduce-scatter.5.cloned.1.call-start = ((), (), s32[]{:S(2)}) async-start(), calls=%async_computation.10 | async-start | bytes 4587520 | tf_op jit(solution)/shard_map/sum_blocks/reduce_scatter | solution.py:284
  145.6 38.7 %collective-permute-start.5 = (bf16[128,3584]{1,0:T(8,128)(2,1)S(1)}, bf16[128,3584]{1,0:T(8,128)(2,1)S(1)}, u32[]{:S(2)}, u32[]{:S(2)}) collective-permute-start(bf16[128,3584]{1,0:T(8,128)(2,1)S(1)} %copy-done.6), channel_id=1, source_target_pairs={{0,64},{64,128},{128,192},{192,0},{1,65},{65,129},{129,193},{193,1... | collective-permute-start | bytes 2752520 | tf_op jit(solution)/shard_map/ring/ppermute | solution.py:225
  161.5 38.2 %collective-permute-start.14 = (bf16[128,3584]{1,0:T(8,128)(2,1)}, bf16[128,3584]{1,0:T(8,128)(2,1)}, u32[]{:S(2)}, u32[]{:S(2)}) collective-permute-start(bf16[128,3584]{1,0:T(8,128)(2,1)} %collective-permute-done.6.right_ref), channel_id=1, source_target_pairs={{0,192},{64,0},{128,64},{192,128},{1,193},{65,1},{129,65},{193,129... | collective-permute-start | bytes 2752520 | tf_op jit(solution)/shard_map/ring/ppermute | solution.py:225
  163.2 29.1 %copy-start.4 = (bf16[2,64,1792]{2,1,0:T(8,128)(2,1)}, bf16[2,64,1792]{2,1,0:T(8,128)(2,1)S(1)}, u32[]{:S(2)}) copy-start(bf16[2,64,1792]{2,1,0:T(8,128)(2,1)S(1)} %copy.58) | copy-start | bytes 1376260
  163.2 21.1 %collective-permute-start.12 = (bf16[128,1792]{1,0:T(8,128)(2,1)S(1)}, bf16[128,1792]{1,0:T(8,128)(2,1)S(1)}, u32[]{:S(2)}, u32[]{:S(2)}) collective-permute-start(bf16[128,1792]{1,0:T(8,128)(2,1)S(1)} %bitcast.53), channel_id=1, source_target_pairs={{0,64},{64,128},{128,192},{192,0},{1,65},{65,129},{129,193},{193,1... | collective-permute-start | bytes 1376264 | tf_op jit(solution)/shard_map/ring/ppermute | solution.py:268
  163.3 43.5 %collective-permute-start.11 = (bf16[128,1792]{1,0:T(8,128)(2,1)S(1)}, bf16[128,1792]{1,0:T(8,128)(2,1)S(1)}, u32[]{:S(2)}, u32[]{:S(2)}) collective-permute-start(bf16[128,1792]{1,0:T(8,128)(2,1)S(1)} %bitcast.54), channel_id=1, source_target_pairs={{0,192},{64,0},{128,64},{192,128},{1,193},{65,1},{129,65},{193,129... | collective-permute-start | bytes 1376264 | tf_op jit(solution)/shard_map/ring/ppermute | solution.py:267
  184.3 15.4 %copy-start.11 = (bf16[128,1792]{1,0:T(8,128)(2,1)}, bf16[128,1792]{1,0:T(8,128)(2,1)S(1)}, u32[]{:S(2)}) copy-start(bf16[128,1792]{1,0:T(8,128)(2,1)S(1)} %collective-permute-done.12.left_ref) | copy-start | bytes 1376260
  184.3 22.5 %collective-permute-start.13 = (bf16[128,1792]{1,0:T(8,128)(2,1)S(1)}, bf16[128,1792]{1,0:T(8,128)(2,1)}, u32[]{:S(2)}, u32[]{:S(2)}) collective-permute-start(bf16[128,1792]{1,0:T(8,128)(2,1)S(1)} %collective-permute-done.12.left_ref), channel_id=1, source_target_pairs={{0,64},{64,128},{128,192},{192,0},{1,65},{65,129},{129,193},{193,1... | collective-permute-start | bytes 1376264 | tf_op jit(solution)/shard_map/ring/ppermute | solution.py:225
  184.3 1.0 copy-start.7
  206.8 0.8 copy-start.12
  222.9 92.5 %reduce-scatter.3.cloned.1.call-start = ((), (), s32[]{:S(2)}) async-start(), calls=%async_computation.9 | async-start | bytes 4587520 | tf_op jit(solution)/shard_map/sum_blocks/reduce_scatter | solution.py:284
  270.8 47.4 %all-to-all-start.5 = ((bf16[64,4,1792]{2,1,0:T(4,128)(2,1)}), bf16[64,4,1792]{2,1,0:T(4,128)(2,1)S(1)}, u32[]{:S(2)}, u32[]{:S(2)}) async-start(bf16[64,4,1792]{2,1,0:T(4,128)(2,1)} %copy.60), calls=%async_computation.7 | async-start | bytes 1835008 | tf_op jit(solution)/shard_map/return_slots/all_to_all | solution.py:289
  318.2 36.4 %all-to-all-start.4 = ((bf16[64,4,1792]{2,1,0:T(4,128)(2,1)}), bf16[64,4,1792]{2,1,0:T(4,128)(2,1)S(1)}, u32[]{:S(2)}, u32[]{:S(2)}) async-start(bf16[64,4,1792]{2,1,0:T(4,128)(2,1)} %copy.59), calls=%async_computation.5 | async-start | bytes 1835008 | tf_op jit(solution)/shard_map/return_slots/all_to_all | solution.py:289
Sparse Core Ops, SparseCore 0:
  17.1 128.1 all-gather.1
  223.0 44.9 reduce-scatter.4
  270.5 44.8 reduce-scatter.2

commit v4 on v3

--- a/solution.py
+++ b/solution.py
@@ -8,10 +8,11 @@
 CAP = 2
 LANES = 128
 BLOCK = 256
-CHUNKS = 2
 HEAD = 1792
-STEP = 512
-TAIL_STEP = 256
+STEP = 1792
+TAIL_STEP = 896
+OUT_STEP = 512
+OUT_SPLIT = 1536
 NT = (((1,), (1,)), ((), ()))
 
 
@@ -167,44 +168,42 @@
     )(*parts, hidden, head_pre, w_gate, w_up)
 
 
-def out_kernel(me_ref, h0_ref, h1_ref, gate_ref, up_ref, out_ref):
+def out_kernel(h0_ref, h1_ref, gate_ref, up_ref, *out_refs):
     units = gate_ref.shape[2]
     for e, h_ref in enumerate((h0_ref, h1_ref)):
         value = lax.dot_general(h_ref[:, :units], gate_ref[e], NT, preferred_element_type=jnp.float32)
         value = value + lax.dot_general(h_ref[:, units:], up_ref[e], NT, preferred_element_type=jnp.float32)
         value = value.astype(jnp.bfloat16)
         part = value.shape[0] // 4
-        for r in range(4):
-            out_ref[lax.rem(me_ref[0] + r, 4), e * part : (e + 1) * part, :] = value[r * part : (r + 1) * part]
-
-
-def out_rows(me, h, w_gate, w_up, chunk, chunks, cols):
+        for r, out_ref in enumerate(out_refs):
+            out_ref[e * part : (e + 1) * part, :] = value[r * part : (r + 1) * part]
+
+
+def out_rows(h, w_gate, w_up, start, stop):
     rows = h[0].shape[0]
     local_experts, width, units = w_gate.shape
-    h_spec = pl.BlockSpec((rows, 2 * units), lambda n, me: (0, 0))
-    per = width // chunks // cols
-    first = chunk * per
-    w_spec = pl.BlockSpec((local_experts, cols, units), lambda n, me: (0, first + n, 0))
+    count = local_experts * rows // 4
+    h_spec = pl.BlockSpec((rows, 2 * units), lambda n: (0, 0))
+    w_spec = pl.BlockSpec((local_experts, OUT_STEP, units), lambda n: (0, start // OUT_STEP + n, 0))
     return pl.pallas_call(
         out_kernel,
-        out_shape=jax.ShapeDtypeStruct((4, local_experts * rows // 4, width // chunks), jnp.bfloat16),
-        grid_spec=pltpu.PrefetchScalarGridSpec(
-            num_scalar_prefetch=1,
-            grid=(per,),
-            in_specs=[
-                h_spec,
-                h_spec,
-                w_spec,
-                w_spec,
-            ],
-            out_specs=pl.BlockSpec((4, local_experts * rows // 4, cols), lambda n, me: (0, 0, n)),
-        ),
+        out_shape=[jax.ShapeDtypeStruct((count, stop - start), jnp.bfloat16)] * 4,
+        grid=((stop - start) // OUT_STEP,),
+        in_specs=[h_spec, h_spec, w_spec, w_spec],
+        out_specs=[pl.BlockSpec((count, OUT_STEP), lambda n: (0, n))] * 4,
         compiler_params=pltpu.CompilerParams(dimension_semantics=("arbitrary",)),
         cost_estimate=pl.CostEstimate(
-            flops=2 * local_experts * rows * 2 * units * width // chunks, bytes_accessed=8 << 20, transcendentals=0
+            flops=2 * local_experts * rows * 2 * units * (stop - start), bytes_accessed=8 << 20, transcendentals=0
         ),
         name="out_rows",
-    )(me, *h, w_gate, w_up)
+    )(*h, w_gate, w_up)
+
+
+def total(*terms):
+    value = terms[0].astype(jnp.float32)
+    for term in terms[1:]:
+        value = value + term.astype(jnp.float32)
+    return value.astype(jnp.bfloat16)
 
 
 def on_device(tokens, out_grad, route_ids, route_probs, w_gate, w_up, w_down):
@@ -214,7 +213,6 @@
     tok_count, width = tokens.shape
     slots = experts * CAP
     per_dest = local_experts * CAP
-    me = lax.axis_index("dp").astype(jnp.int32).reshape(1)
     first = (lax.axis_index("expert").astype(jnp.int32) * local_experts).reshape(1)
 
     up_ring = [(i, (i + 1) % 4) for i in range(4)]
@@ -269,22 +267,33 @@
             sent[name] = [own, right, None, left]
 
     hidden = hidden_grads(0, sent["g", 0], w_down)
-    h = [late_grads(0, sent["x", 0], hidden, head_pre, w_gate, w_up)]
     with jax.named_scope("ring"):
         final = sent["x", 1]
+        final[1], final[3], hidden = lax.optimization_barrier((final[1], final[3], hidden))
         final[2] = forward(final, upward[3])
+    h = [late_grads(0, sent["x", 0], hidden, head_pre, w_gate, w_up)]
     hidden = hidden_grads(1, sent["g", 1], w_down)
     h.append(late_grads(1, final, hidden, head_pre, w_gate, w_up))
 
+    own_a, right_a, far_a, left_a = out_rows(h, w_gate, w_up, 0, OUT_SPLIT)
+    own_b, right_b, far_b, left_b = out_rows(h, w_gate, w_up, OUT_SPLIT, width)
+    with jax.named_scope("sum_blocks"):
+        from_far = lax.ppermute(far_a, "dp", up_ring)
+        from_right_a = lax.ppermute(left_a, "dp", down_ring)
+        from_left_a = lax.ppermute(total(right_a, from_far), "dp", up_ring)
+        far_b, from_right_a = lax.optimization_barrier((far_b, from_right_a))
+        from_far = lax.ppermute(far_b, "dp", down_ring)
+        right_b, from_left_a = lax.optimization_barrier((right_b, from_left_a))
+        from_left_b = lax.ppermute(right_b, "dp", up_ring)
+        left_b = total(left_b, from_far)
+        left_b, from_left_a = lax.optimization_barrier((left_b, from_left_a))
+        from_right_b = lax.ppermute(left_b, "dp", down_ring)
+
     results = []
-    for chunk in range(CHUNKS):
-        cols = width // CHUNKS
-        partials = out_rows(me, h, w_gate, w_up, chunk, CHUNKS, 256)
-        with jax.named_scope("sum_blocks"):
-            summed = lax.psum_scatter(
-                partials.reshape(4 * slots, cols), "dp", scatter_dimension=0, tiled=True
-            )
+    for terms in ((own_a, from_left_a, from_right_a), (own_b, from_left_b, from_right_b)):
         with jax.named_scope("return_slots"):
+            summed = total(*terms)
+            cols = summed.shape[1]
             back = summed.reshape(per_dest, columns, cols).transpose(1, 0, 2)
             returned = lax.all_to_all(back, "expert", split_axis=0, concat_axis=0, tiled=True)
         with jax.named_scope("combine"):

time: 364 us -> 341 us (0.937)
  Pallas kernels: 58.8 us -> 43.7 us
  waiting for transfers between devices: 191 us -> 179 us
  starting transfers between devices: 77.5 us -> 81.7 us
    reduce_scatter x2 -> x0, waiting for transfers between devices: 70.8 us -> none  [on_device(): lax.psum_scatter(partials.reshape(4 * slots, cols), 'dp', scatter_dimensi...]
    ppermute x0 -> x6, waiting for transfers between devices: none -> 33.3 us  [the longest x1 16.9 us: on_device(): from_left_a = lax.ppermute(total(right_a, from_far), 'dp', up_ring)]
    all_to_all x2, waiting for transfers between devices: 25.2 us -> 42.9 us  [on_device(): lax.all_to_all(back, 'expert', split_axis=0, concat_axis=0, tiled=True)]
    ppermute x4, waiting for transfers between devices: 26.7 us -> 14 us  [on_device(): left = lax.ppermute(own, 'dp', up_ring)]
    ppermute x2, waiting for transfers between devices: 0.01 us -> 12.2 us  [forward(): lax.ppermute(parts[3], 'dp', up_ring)]
    ppermute x4, waiting for transfers between devices: 0.01 us -> 8.64 us  [on_device(): right = lax.ppermute(own, 'dp', down_ring)]
    ppermute x0 -> x6, starting transfers between devices: none -> 7.2 us  [the longest x1 3.37 us: on_device(): from_right_b = lax.ppermute(left_b, 'dp', down_ring)]
    pallas_call x2, Pallas kernels: 14.1 us -> 8.08 us  [hidden_grads(): pl.pallas_call(hidden_kernel, out_shape=jax.ShapeDtypeStruct((4 * count,...]
  transfers between devices with their start and end apart: 24 -> 28, of which waited for: 12 -> 19; matrix products, arithmetic and copies ran while one was open for 4% -> 5% of each run, Pallas kernels for 12% -> 10%
where the time goes in v4:
time: 341 us; the launch traced here: 340 us
  waiting for transfers between devices  179 us (52%)
  starting transfers between devices  81.7 us (24%)
  Pallas kernels  43.7 us (13%)
  between operations  13.9 us (4%)
  local copies, waits for them, and re-layouts  12.3 us (4%)
  other arithmetic  6.47 us (2%)
    all_to_all x2, waiting for transfers between devices, on_device(): lax.all_to_all(back, 'expert', split_axis=0, concat_axis=0, tiled=True)  42.9 us
    all_to_all x4, waiting for transfers between devices, on_device(): lax.all_to_all(tile, 'expert', split_axis=0, concat_axis=0, tiled=True)  38.3 us
    all_to_all x4, starting transfers between devices, on_device(): lax.all_to_all(tile, 'expert', split_axis=0, concat_axis=0, tiled=True)  36.3 us
    ppermute x2, waiting for transfers between devices, forward(): lax.ppermute(parts[1], 'dp', down_ring)  27.7 us
    all_to_all x2, starting transfers between devices, on_device(): lax.all_to_all(back, 'expert', split_axis=0, concat_axis=0, tiled=True)  18.7 us
    ppermute x1, waiting for transfers between devices, on_device(): from_left_a = lax.ppermute(total(right_a, from_far), 'dp', up_ring)  16.9 us
    pallas_call x1, Pallas kernels, head_products(): pl.pallas_call(head_kernel, out_shape=jax.ShapeDtypeStruct((local_experts...  14.1 us
    ppermute x4, waiting for transfers between devices, on_device(): left = lax.ppermute(own, 'dp', up_ring)  14 us
  transfers between devices with their start and end apart: 28, of which 19 were waited for; matrix products, arithmetic and copies ran while one was open for 5% of the time, Pallas kernels for 10%

profile of v4, /device:TPU:1, one launch (start us, length us, event | category | flops | bytes accessed | tf_op | source)
XLA Modules:
  0.0 340.0 jit_solution(13856139194344143695)
XLA Ops:
  8.2 2.1 collective-permute-start.9
  10.3 2.5 collective-permute-start.8
  12.8 1.2 collective-permute-start.7
  13.9 1.3 collective-permute-done.8
  20.4 13.7 %all-to-all-start = ((bf16[64,2,1792]{2,1,0:T(2,128)(2,1)}), bf16[64,2,1792]{2,1,0:T(2,128)(2,1)S(1)}, u32[]{:S(2)}, u32[]{:S(2)}) async-start(bf16[64,2,1792]{2,1,0:T(2,128)(2,1)} %reshape.132), calls=%async_computation | async-start | bytes 917504 | tf_op jit(solution)/shard_map/send_slots/all_to_all | solution.py:252
  35.3 1.3 reshape.135
  36.6 17.9 %all-to-all-done = bf16[64,2,1792]{2,1,0:T(2,128)(2,1)S(1)} async-done(((bf16[64,2,1792]{2,1,0:T(2,128)(2,1)}), bf16[64,2,1792]{2,1,0:T(2,128)(2,1)S(1)}, u32[]{:S(2)}, u32[]{:S(2)}) %all-to-all-start) | async-done | bytes 458784 | tf_op jit(solution)/shard_map/send_slots/all_to_all | solution.py:252
  54.6 6.3 %all-to-all-start.1 = ((bf16[64,2,3584]{2,1,0:T(2,128)(2,1)}), bf16[64,2,3584]{2,1,0:T(2,128)(2,1)S(1)}, u32[]{:S(2)}, u32[]{:S(2)}) async-start(bf16[64,2,3584]{2,1,0:T(2,128)(2,1)} %reshape.135), calls=%async_computation.1 | async-start | bytes 1835008 | tf_op jit(solution)/shard_map/send_slots/all_to_all | solution.py:252
  61.0 2.7 collective-permute-start
  64.2 1.3 reshape.136
  65.5 8.3 %collective-permute-done.1.left_ref = bf16[128,1792]{1,0:T(8,128)(2,1)S(1)} collective-permute-done((bf16[128,1792]{1,0:T(8,128)(2,1)S(1)}, bf16[128,1792]{1,0:T(8,128)(2,1)S(1)}, u32[]{:S(2)}, u32[]{:S(2)}) %collective-permute-start.1) | collective-permute-done | bytes 458784 | tf_op jit(solution)/shard_map/ring/ppermute | solution.py:266
  73.8 15.6 %all-to-all-done.1 = bf16[64,2,3584]{2,1,0:T(2,128)(2,1)S(1)} async-done(((bf16[64,2,3584]{2,1,0:T(2,128)(2,1)}), bf16[64,2,3584]{2,1,0:T(2,128)(2,1)S(1)}, u32[]{:S(2)}, u32[]{:S(2)}) %all-to-all-start.1) | async-done | bytes 917536 | tf_op jit(solution)/shard_map/send_slots/all_to_all | solution.py:252
  89.5 6.8 %all-to-all-start.2 = ((bf16[64,2,3584]{2,1,0:T(2,128)(2,1)}), bf16[64,2,3584]{2,1,0:T(2,128)(2,1)S(1)}, u32[]{:S(2)}, u32[]{:S(2)}) async-start(bf16[64,2,3584]{2,1,0:T(2,128)(2,1)} %reshape.136), calls=%async_computation.2 | async-start | bytes 1835008 | tf_op jit(solution)/shard_map/send_slots/all_to_all | solution.py:252
  96.4 2.7 collective-permute-start.2
  99.0 1.2 collective-permute-start.4
  100.2 27.7 %collective-permute-done.4.far_ref = bf16[128,1792]{1,0:T(8,128)(2,1)S(1)} collective-permute-done((bf16[128,1792]{1,0:T(8,128)(2,1)S(1)}, bf16[128,1792]{1,0:T(8,128)(2,1)S(1)}, u32[]{:S(2)}, u32[]{:S(2)}) %collective-permute-start.4) | collective-permute-done | bytes 458784 | tf_op jit(solution)/shard_map/ring/ppermute | solution.py:223
  128.8 3.2 all-to-all-done.2
  132.2 2.7 collective-permute-start.5
  136.1 9.5 %all-to-all-start.3 = ((bf16[64,2,1792]{2,1,0:T(2,128)(2,1)}), bf16[64,2,1792]{2,1,0:T(2,128)(2,1)S(1)}, u32[]{:S(2)}, u32[]{:S(2)}) async-start(bf16[64,2,1792]{2,1,0:T(2,128)(2,1)} %reshape.138), calls=%async_computation.3 | async-start | bytes 917504 | tf_op jit(solution)/shard_map/send_slots/all_to_all | solution.py:252
  145.7 14.1 %head_products.1.head_ref = f32[2,512,512]{2,1,0:T(8,128)} custom-call(s32[1]{0:T(128)} %bitcast.10.first_ref, bf16[64,4,16,1920]{3,2,1,0:T(8,128)(2,1)} %bitcast.36, bf16[2,3584,256]{2,1,0:T(8,128)(2,1)} %gate_ref.9, bf16[2,3584,256]{2,1,0:T(8,128)(2,1)} %up_ref.9), custom_call_target="tpu_custom_call" | custom-call | flops 2113929216 | bytes 20971520 | tf_op jit(solution)/shard_map/send_slots/head_products/pallas_call | solution.py:75
  159.8 1.7 all-to-all-done.3
  161.5 1.7 collective-permute-start.14
  163.3 2.7 collective-permute-start.10
  166.0 8.8 %collective-permute-done.12.far_ref = bf16[128,3584]{1,0:T(8,128)(2,1)} collective-permute-done((bf16[128,3584]{1,0:T(8,128)(2,1)S(1)}, bf16[128,3584]{1,0:T(8,128)(2,1)}, u32[]{:S(2)}, u32[]{:S(2)}) %collective-permute-start.12) | collective-permute-done | bytes 917536 | tf_op jit(solution)/shard_map/ring/ppermute | solution.py:223
  174.8 4.0 %hidden_grads.2.hidden_ref = f32[512,256]{1,0:T(8,128)} custom-call(bf16[128,3584]{1,0:T(8,128)(2,1)} %bitcast.42, bf16[128,3584]{1,0:T(8,128)(2,1)} %collective-permute-done.2.right_ref, bf16[128,3584]{1,0:T(8,128)(2,1)} %collective-permute-done.12.far_ref, bf16[128,3584]{1,0:T(8,128)(2,1)} %copy-done.8, bf16[2,256,3584]{2,1,0:T(8,128)(2,1)} %down_ref.3), custom_call_target="tpu_custom_call" | custom-call | flops 939524096 | bytes 5242880 | tf_op jit(solution)/shard_map/hidden_grads/pallas_call | solution.py:112
  178.8 5.7 %collective-permute-done.11.left_ref = bf16[128,1792]{1,0:T(8,128)(2,1)S(1)} collective-permute-done((bf16[128,1792]{1,0:T(8,128)(2,1)S(1)}, bf16[128,1792]{1,0:T(8,128)(2,1)S(1)}, u32[]{:S(2)}, u32[]{:S(2)}) %collective-permute-start.11) | collective-permute-done | bytes 458784 | tf_op jit(solution)/shard_map/ring/ppermute | solution.py:266
  184.5 8.6 %collective-permute-done.10.right_ref = bf16[128,1792]{1,0:T(8,128)(2,1)S(1)} collective-permute-done((bf16[128,1792]{1,0:T(8,128)(2,1)S(1)}, bf16[128,1792]{1,0:T(8,128)(2,1)S(1)}, u32[]{:S(2)}, u32[]{:S(2)}) %collective-permute-start.10) | collective-permute-done | bytes 458784 | tf_op jit(solution)/shard_map/ring/ppermute | solution.py:265
  193.1 5.0 %late_grads.2.h0_ref = bf16[512,512]{1,0:T(8,128)(2,1)} custom-call(bf16[128,1792]{1,0:T(8,128)(2,1)} %bitcast.51, bf16[128,1792]{1,0:T(8,128)(2,1)} %copy-done.13, bf16[128,1792]{1,0:T(8,128)(2,1)} %copy-done.14, bf16[128,1792]{1,0:T(8,128)(2,1)} %copy-done.12, f32[512,256]{1,0:T(8,128)} %hidden_grads.2.hidden_ref, f32[2,512,512]{2,1,0:T(8,128)} %head_products.1.head_ref, ...), custom_call_target="tpu_custom_call" | custom-call | flops 939524096 | bytes 6291456 | tf_op jit(solution)/shard_map/late_grads/pallas_call | solution.py:150
  198.1 4.0 %hidden_grads.3.hidden_ref = f32[512,256]{1,0:T(8,128)} custom-call(bf16[128,3584]{1,0:T(8,128)(2,1)} %bitcast.45, bf16[128,3584]{1,0:T(8,128)(2,1)} %collective-permute-done.5.right_ref, bf16[128,3584]{1,0:T(8,128)(2,1)} %collective-permute-done.14.far_ref, bf16[128,3584]{1,0:T(8,128)(2,1)} %collective-permute-done.6.left_ref, bf16[2,256,3584]{2,1,0:T(8,128)(2,1)} %down_ref.3), custom_call_target="tpu_custom_call" | custom-call | flops 939524096 | bytes 5242880 | tf_op jit(solution)/shard_map/hidden_grads/pallas_call | solution.py:112
  202.2 3.4 %collective-permute-done.13.far_ref = bf16[128,1792]{1,0:T(8,128)(2,1)S(1)} collective-permute-done((bf16[128,1792]{1,0:T(8,128)(2,1)S(1)}, bf16[128,1792]{1,0:T(8,128)(2,1)S(1)}, u32[]{:S(2)}, u32[]{:S(2)}) %collective-permute-start.13) | collective-permute-done | bytes 458784 | tf_op jit(solution)/shard_map/ring/ppermute | solution.py:223
  206.3 4.9 %late_grads.3.h1_ref = bf16[512,512]{1,0:T(8,128)(2,1)} custom-call(bf16[128,1792]{1,0:T(8,128)(2,1)} %bitcast.54, bf16[128,1792]{1,0:T(8,128)(2,1)} %copy-done.16, bf16[128,1792]{1,0:T(8,128)(2,1)} %copy-done.17, bf16[128,1792]{1,0:T(8,128)(2,1)} %copy-done.15, f32[512,256]{1,0:T(8,128)} %hidden_grads.3.hidden_ref, f32[2,512,512]{2,1,0:T(8,128)} %head_products.1.head_ref, ...), custom_call_target="tpu_custom_call" | custom-call | flops 939524096 | bytes 6291456 | tf_op jit(solution)/shard_map/late_grads/pallas_call | solution.py:150
  211.2 5.4 %out_rows.2 = (bf16[256,1536]{1,0:T(8,128)(2,1)}, bf16[256,1536]{1,0:T(8,128)(2,1)}, bf16[256,1536]{1,0:T(8,128)(2,1)}, bf16[256,1536]{1,0:T(8,128)(2,1)}) custom-call(bf16[512,512]{1,0:T(8,128)(2,1)} %late_grads.2.h0_ref, bf16[512,512]{1,0:T(8,128)(2,1)} %late_grads.3.h1_ref, bf16[2,3584,256]{2,1,0:T(8,128)(2,1)} %gate_ref.9, bf16[2,3584,256]{2,1,0:T(8,128)(2,1)} %up_ref.9), custom_call_target="tpu_custom_call" | custom-call | flops 1610612736 | bytes 8388608 | tf_op jit(solution)/shard_map/out_rows/pallas_call | solution.py:188
  216.7 1.3 collective-permute-start.15
  218.1 6.3 %out_rows.3 = (bf16[256,2048]{1,0:T(8,128)(2,1)}, bf16[256,2048]{1,0:T(8,128)(2,1)}, bf16[256,2048]{1,0:T(8,128)(2,1)}, bf16[256,2048]{1,0:T(8,128)(2,1)}) custom-call(bf16[512,512]{1,0:T(8,128)(2,1)} %late_grads.2.h0_ref, bf16[512,512]{1,0:T(8,128)(2,1)} %late_grads.3.h1_ref, bf16[2,3584,256]{2,1,0:T(8,128)(2,1)} %gate_ref.9, bf16[2,3584,256]{2,1,0:T(8,128)(2,1)} %up_ref.9), custom_call_target="tpu_custom_call" | custom-call | flops 2147483648 | bytes 8388608 | tf_op jit(solution)/shard_map/out_rows/pallas_call | solution.py:188
  224.4 9.6 %collective-permute-done.15 = bf16[256,1536]{1,0:T(8,128)(2,1)S(1)} collective-permute-done((bf16[256,1536]{1,0:T(8,128)(2,1)}, bf16[256,1536]{1,0:T(8,128)(2,1)S(1)}, u32[]{:S(2)}, u32[]{:S(2)}) %collective-permute-start.15) | collective-permute-done | bytes 786464 | tf_op jit(solution)/shard_map/sum_blocks/ppermute | solution.py:282
  234.0 2.3 collective-permute-start.16
  236.6 16.9 %collective-permute-done.18 = bf16[256,1536]{1,0:T(8,128)(2,1)S(1)} collective-permute-done((bf16[256,1536]{1,0:T(8,128)(2,1)S(1)}, bf16[256,1536]{1,0:T(8,128)(2,1)S(1)}, u32[]{:S(2)}, u32[]{:S(2)}) %collective-permute-start.18) | collective-permute-done | bytes 786464 | tf_op jit(solution)/shard_map/sum_blocks/ppermute | solution.py:283
  253.5 2.5 collective-permute-done.16
  256.5 3.4 collective-permute-start.20
  260.2 1.5 copy.72
  261.7 12.5 %all-to-all-start.4 = ((bf16[64,4,1536]{2,1,0:T(4,128)(2,1)}), bf16[64,4,1536]{2,1,0:T(4,128)(2,1)S(1)}, u32[]{:S(2)}, u32[]{:S(2)}) async-start(bf16[64,4,1536]{2,1,0:T(4,128)(2,1)} %bitcast.35), calls=%async_computation.4 | async-start | bytes 1572864 | tf_op jit(solution)/shard_map/return_slots/all_to_all | solution.py:298
  274.2 1.4 collective-permute-done.19
  275.5 2.9 collective-permute-done.20
  278.4 2.1 add_convert_fusion
  280.5 1.8 copy.71
  282.3 14.8 %all-to-all-done.4 = bf16[64,4,1536]{2,1,0:T(4,128)(2,1)S(1)} async-done(((bf16[64,4,1536]{2,1,0:T(4,128)(2,1)}), bf16[64,4,1536]{2,1,0:T(4,128)(2,1)S(1)}, u32[]{:S(2)}, u32[]{:S(2)}) %all-to-all-start.4) | async-done | bytes 786464 | tf_op jit(solution)/shard_map/return_slots/all_to_all | solution.py:298
  297.1 6.2 %all-to-all-start.5 = ((bf16[64,4,2048]{2,1,0:T(4,128)(2,1)}), bf16[64,4,2048]{2,1,0:T(4,128)(2,1)S(1)}, u32[]{:S(2)}, u32[]{:S(2)}) async-start(bf16[64,4,2048]{2,1,0:T(4,128)(2,1)} %bitcast.34), calls=%async_computation.5 | async-start | bytes 2097152 | tf_op jit(solution)/shard_map/return_slots/all_to_all | solution.py:298
  303.9 28.0 %all-to-all-done.5 = bf16[64,4,2048]{2,1,0:T(4,128)(2,1)S(1)} async-done(((bf16[64,4,2048]{2,1,0:T(4,128)(2,1)}), bf16[64,4,2048]{2,1,0:T(4,128)(2,1)S(1)}, u32[]{:S(2)}, u32[]{:S(2)}) %all-to-all-start.5) | async-done | bytes 1048608 | tf_op jit(solution)/shard_map/return_slots/all_to_all | solution.py:298
  (106 shorter events, 15.1 us)
Async XLA Ops:
  6.5 28.4 %copy-start = (bf16[16,3584]{1,0:T(8,128)(2,1)S(1)}, bf16[16,3584]{1,0:T(8,128)(2,1)}, u32[]{:S(2)}) copy-start(bf16[16,3584]{1,0:T(8,128)(2,1)} %param.8) | copy-start | bytes 344068
  6.5 139.1 %all-gather.2.cloned.1.call-start = ((), (), s32[]{:S(2)}) async-start(), calls=%async_computation.6 | async-start | bytes 15974400 | tf_op jit(solution)/shard_map/gather_tokens/all_gather | solution.py:229
  8.2 25.9 %copy-start.19 = (s32[16,8]{0,1:T(8,128)S(1)}, s32[16,8]{0,1:T(8,128)}, u32[]{:S(2)}) copy-start(s32[16,8]{0,1:T(8,128)} %param.9) | copy-start | bytes 1540
  8.2 25.9 %copy-start.20 = (f32[16,8]{0,1:T(8,128)S(1)}, f32[16,8]{0,1:T(8,128)}, u32[]{:S(2)}) copy-start(f32[16,8]{0,1:T(8,128)} %param.10) | copy-start | bytes 1540
  8.2 5.7 %collective-permute-start.9 = (bf16[16,1920]{1,0:T(8,128)(2,1)S(1)}, bf16[16,1920]{1,0:T(8,128)(2,1)S(1)}, u32[]{:S(2)}, u32[]{:S(2)}) collective-permute-start(bf16[16,1920]{1,0:T(8,128)(2,1)S(1)} %pad_maximum_fusion.2), channel_id=1, source_target_pairs={{0,64},{64,128},{128,192},{192,0},{1,65},{65,129},{129,193},{193,1... | collective-permute-start | bytes 184328 | tf_op jit(solution)/shard_map/gather_tokens/ppermute | solution.py:228
  10.3 4.9 %collective-permute-start.8 = (bf16[16,1920]{1,0:T(8,128)(2,1)S(1)}, bf16[16,1920]{1,0:T(8,128)(2,1)S(1)}, u32[]{:S(2)}, u32[]{:S(2)}) collective-permute-start(bf16[16,1920]{1,0:T(8,128)(2,1)S(1)} %pad_maximum_fusion.2), channel_id=1, source_target_pairs={{0,128},{64,192},{128,0},{192,64},{1,129},{65,193},{129,1},{193,65... | collective-permute-start | bytes 184328 | tf_op jit(solution)/shard_map/gather_tokens/ppermute | solution.py:228
  12.8 3.4 collective-permute-start.7
  20.4 34.1 %all-to-all-start = ((bf16[64,2,1792]{2,1,0:T(2,128)(2,1)}), bf16[64,2,1792]{2,1,0:T(2,128)(2,1)S(1)}, u32[]{:S(2)}, u32[]{:S(2)}) async-start(bf16[64,2,1792]{2,1,0:T(2,128)(2,1)} %reshape.132), calls=%async_computation | async-start | bytes 917504 | tf_op jit(solution)/shard_map/send_slots/all_to_all | solution.py:252
  54.6 10.9 %copy-start.4 = (bf16[2,64,1792]{2,1,0:T(8,128)(2,1)}, bf16[2,64,1792]{2,1,0:T(8,128)(2,1)S(1)}, u32[]{:S(2)}) copy-start(bf16[2,64,1792]{2,1,0:T(8,128)(2,1)S(1)} %copy.52) | copy-start | bytes 1376260
  54.6 34.8 %all-to-all-start.1 = ((bf16[64,2,3584]{2,1,0:T(2,128)(2,1)}), bf16[64,2,3584]{2,1,0:T(2,128)(2,1)S(1)}, u32[]{:S(2)}, u32[]{:S(2)}) async-start(bf16[64,2,3584]{2,1,0:T(2,128)(2,1)} %reshape.135), calls=%async_computation.1 | async-start | bytes 1835008 | tf_op jit(solution)/shard_map/send_slots/all_to_all | solution.py:252
  60.9 12.9 %collective-permute-start.1 = (bf16[128,1792]{1,0:T(8,128)(2,1)S(1)}, bf16[128,1792]{1,0:T(8,128)(2,1)S(1)}, u32[]{:S(2)}, u32[]{:S(2)}) collective-permute-start(bf16[128,1792]{1,0:T(8,128)(2,1)S(1)} %bitcast.49), channel_id=1, source_target_pairs={{0,64},{64,128},{128,192},{192,0},{1,65},{65,129},{129,193},{193,1... | collective-permute-start | bytes 1376264 | tf_op jit(solution)/shard_map/ring/ppermute | solution.py:266
  61.0 12.8 %collective-permute-start = (bf16[128,1792]{1,0:T(8,128)(2,1)S(1)}, bf16[128,1792]{1,0:T(8,128)(2,1)S(1)}, u32[]{:S(2)}, u32[]{:S(2)}) collective-permute-start(bf16[128,1792]{1,0:T(8,128)(2,1)S(1)} %bitcast.50), channel_id=1, source_target_pairs={{0,192},{64,0},{128,64},{192,128},{1,193},{65,1},{129,65},{193,129... | collective-permute-start | bytes 1376264 | tf_op jit(solution)/shard_map/ring/ppermute | solution.py:265
  73.8 15.7 %copy-start.12 = (bf16[128,1792]{1,0:T(8,128)(2,1)}, bf16[128,1792]{1,0:T(8,128)(2,1)S(1)}, u32[]{:S(2)}) copy-start(bf16[128,1792]{1,0:T(8,128)(2,1)S(1)} %collective-permute-done.1.left_ref) | copy-start | bytes 1376260
  73.8 25.2 %copy-start.13 = (bf16[128,1792]{1,0:T(8,128)(2,1)}, bf16[128,1792]{1,0:T(8,128)(2,1)S(1)}, u32[]{:S(2)}) copy-start(bf16[128,1792]{1,0:T(8,128)(2,1)S(1)} %collective-permute-done.right_ref) | copy-start | bytes 1376260
  89.5 42.7 %copy-start.2 = (bf16[2,64,3584]{2,1,0:T(8,128)(2,1)}, bf16[2,64,3584]{2,1,0:T(8,128)(2,1)S(1)}, u32[]{:S(2)}) copy-start(bf16[2,64,3584]{2,1,0:T(8,128)(2,1)S(1)} %copy.57) | copy-start | bytes 2752516
  89.5 45.4 %copy-start.18 = (bf16[16,3584]{1,0:T(8,128)(2,1)S(1)}, bf16[16,3584]{1,0:T(8,128)(2,1)}, u32[]{:S(2)}) copy-start(bf16[16,3584]{1,0:T(8,128)(2,1)} %param.7) | copy-start | bytes 344068
  89.5 42.5 %all-to-all-start.2 = ((bf16[64,2,3584]{2,1,0:T(2,128)(2,1)}), bf16[64,2,3584]{2,1,0:T(2,128)(2,1)S(1)}, u32[]{:S(2)}, u32[]{:S(2)}) async-start(bf16[64,2,3584]{2,1,0:T(2,128)(2,1)} %reshape.136), calls=%async_computation.2 | async-start | bytes 1835008 | tf_op jit(solution)/shard_map/send_slots/all_to_all | solution.py:252
  96.3 31.6 %collective-permute-start.3 = (bf16[128,3584]{1,0:T(8,128)(2,1)S(1)}, bf16[128,3584]{1,0:T(8,128)(2,1)S(1)}, u32[]{:S(2)}, u32[]{:S(2)}) collective-permute-start(bf16[128,3584]{1,0:T(8,128)(2,1)S(1)} %bitcast.40), channel_id=1, source_target_pairs={{0,64},{64,128},{128,192},{192,0},{1,65},{65,129},{129,193},{193,1... | collective-permute-start | bytes 2752520 | tf_op jit(solution)/shard_map/ring/ppermute | solution.py:266
  96.4 32.5 %collective-permute-start.2 = (bf16[128,3584]{1,0:T(8,128)(2,1)S(1)}, bf16[128,3584]{1,0:T(8,128)(2,1)}, u32[]{:S(2)}, u32[]{:S(2)}) collective-permute-start(bf16[128,3584]{1,0:T(8,128)(2,1)S(1)} %bitcast.41), channel_id=1, source_target_pairs={{0,192},{64,0},{128,64},{192,128},{1,193},{65,1},{129,65},{193,129... | collective-permute-start | bytes 2752520 | tf_op jit(solution)/shard_map/ring/ppermute | solution.py:265
  99.0 28.8 %collective-permute-start.4 = (bf16[128,1792]{1,0:T(8,128)(2,1)S(1)}, bf16[128,1792]{1,0:T(8,128)(2,1)S(1)}, u32[]{:S(2)}, u32[]{:S(2)}) collective-permute-start(bf16[128,1792]{1,0:T(8,128)(2,1)S(1)} %collective-permute-done.right_ref), channel_id=1, source_target_pairs={{0,192},{64,0},{128,64},{192,128},{1,193},{65,1},{129,65},{193,129... | collective-permute-start | bytes 1376264 | tf_op jit(solution)/shard_map/ring/ppermute | solution.py:223
  127.8 31.9 %copy-start.14 = (bf16[128,1792]{1,0:T(8,128)(2,1)}, bf16[128,1792]{1,0:T(8,128)(2,1)S(1)}, u32[]{:S(2)}) copy-start(bf16[128,1792]{1,0:T(8,128)(2,1)S(1)} %collective-permute-done.4.far_ref) | copy-start | bytes 1376260
  127.8 1.0 copy-start.8
  132.1 27.6 %copy-start.3 = (bf16[2,64,3584]{2,1,0:T(8,128)(2,1)}, bf16[2,64,3584]{2,1,0:T(8,128)(2,1)S(1)}, u32[]{:S(2)}) copy-start(bf16[2,64,3584]{2,1,0:T(8,128)(2,1)S(1)} %copy.58) | copy-start | bytes 2752516
  132.1 13.4 %copy-start.9 = (bf16[128,3584]{1,0:T(8,128)(2,1)S(1)}, bf16[128,3584]{1,0:T(8,128)(2,1)}, u32[]{:S(2)}) copy-start(bf16[128,3584]{1,0:T(8,128)(2,1)} %copy-done.8) | copy-start | bytes 2752516
  132.2 29.3 %collective-permute-start.6 = (bf16[128,3584]{1,0:T(8,128)(2,1)S(1)}, bf16[128,3584]{1,0:T(8,128)(2,1)}, u32[]{:S(2)}, u32[]{:S(2)}) collective-permute-start(bf16[128,3584]{1,0:T(8,128)(2,1)S(1)} %bitcast.43), channel_id=1, source_target_pairs={{0,64},{64,128},{128,192},{192,0},{1,65},{65,129},{129,193},{193,1... | collective-permute-start | bytes 2752520 | tf_op jit(solution)/shard_map/ring/ppermute | solution.py:266
  132.2 29.2 %collective-permute-start.5 = (bf16[128,3584]{1,0:T(8,128)(2,1)S(1)}, bf16[128,3584]{1,0:T(8,128)(2,1)}, u32[]{:S(2)}, u32[]{:S(2)}) collective-permute-start(bf16[128,3584]{1,0:T(8,128)(2,1)S(1)} %bitcast.44), channel_id=1, source_target_pairs={{0,192},{64,0},{128,64},{192,128},{1,193},{65,1},{129,65},{193,129... | collective-permute-start | bytes 2752520 | tf_op jit(solution)/shard_map/ring/ppermute | solution.py:265
  136.1 25.4 %all-to-all-start.3 = ((bf16[64,2,1792]{2,1,0:T(2,128)(2,1)}), bf16[64,2,1792]{2,1,0:T(2,128)(2,1)S(1)}, u32[]{:S(2)}, u32[]{:S(2)}) async-start(bf16[64,2,1792]{2,1,0:T(2,128)(2,1)} %reshape.138), calls=%async_computation.3 | async-start | bytes 917504 | tf_op jit(solution)/shard_map/send_slots/all_to_all | solution.py:252
  145.6 29.2 %collective-permute-start.12 = (bf16[128,3584]{1,0:T(8,128)(2,1)S(1)}, bf16[128,3584]{1,0:T(8,128)(2,1)}, u32[]{:S(2)}, u32[]{:S(2)}) collective-permute-start(bf16[128,3584]{1,0:T(8,128)(2,1)S(1)} %copy-done.9), channel_id=1, source_target_pairs={{0,64},{64,128},{128,192},{192,0},{1,65},{65,129},{129,193},{193,1... | collective-permute-start | bytes 2752520 | tf_op jit(solution)/shard_map/ring/ppermute | solution.py:223
  161.5 36.6 %collective-permute-start.14 = (bf16[128,3584]{1,0:T(8,128)(2,1)}, bf16[128,3584]{1,0:T(8,128)(2,1)}, u32[]{:S(2)}, u32[]{:S(2)}) collective-permute-start(bf16[128,3584]{1,0:T(8,128)(2,1)} %collective-permute-done.5.right_ref), channel_id=1, source_target_pairs={{0,192},{64,0},{128,64},{192,128},{1,193},{65,1},{129,65},{193,129... | collective-permute-start | bytes 2752520 | tf_op jit(solution)/shard_map/ring/ppermute | solution.py:223
  163.2 15.6 %copy-start.5 = (bf16[2,64,1792]{2,1,0:T(8,128)(2,1)}, bf16[2,64,1792]{2,1,0:T(8,128)(2,1)S(1)}, u32[]{:S(2)}) copy-start(bf16[2,64,1792]{2,1,0:T(8,128)(2,1)S(1)} %copy.60) | copy-start | bytes 1376260
  163.2 21.3 %collective-permute-start.11 = (bf16[128,1792]{1,0:T(8,128)(2,1)S(1)}, bf16[128,1792]{1,0:T(8,128)(2,1)S(1)}, u32[]{:S(2)}, u32[]{:S(2)}) collective-permute-start(bf16[128,1792]{1,0:T(8,128)(2,1)S(1)} %bitcast.52), channel_id=1, source_target_pairs={{0,64},{64,128},{128,192},{192,0},{1,65},{65,129},{129,193},{193,1... | collective-permute-start | bytes 1376264 | tf_op jit(solution)/shard_map/ring/ppermute | solution.py:266
  163.3 29.8 %collective-permute-start.10 = (bf16[128,1792]{1,0:T(8,128)(2,1)S(1)}, bf16[128,1792]{1,0:T(8,128)(2,1)S(1)}, u32[]{:S(2)}, u32[]{:S(2)}) collective-permute-start(bf16[128,1792]{1,0:T(8,128)(2,1)S(1)} %bitcast.53), channel_id=1, source_target_pairs={{0,192},{64,0},{128,64},{192,128},{1,193},{65,1},{129,65},{193,129... | collective-permute-start | bytes 1376264 | tf_op jit(solution)/shard_map/ring/ppermute | solution.py:265
  184.5 13.6 %copy-start.15 = (bf16[128,1792]{1,0:T(8,128)(2,1)}, bf16[128,1792]{1,0:T(8,128)(2,1)S(1)}, u32[]{:S(2)}) copy-start(bf16[128,1792]{1,0:T(8,128)(2,1)S(1)} %collective-permute-done.11.left_ref) | copy-start | bytes 1376260
  193.1 5.0 %copy-start.16 = (bf16[128,1792]{1,0:T(8,128)(2,1)}, bf16[128,1792]{1,0:T(8,128)(2,1)S(1)}, u32[]{:S(2)}) copy-start(bf16[128,1792]{1,0:T(8,128)(2,1)S(1)} %collective-permute-done.10.right_ref) | copy-start | bytes 1376260
  193.1 12.4 %collective-permute-start.13 = (bf16[128,1792]{1,0:T(8,128)(2,1)S(1)}, bf16[128,1792]{1,0:T(8,128)(2,1)S(1)}, u32[]{:S(2)}, u32[]{:S(2)}) collective-permute-start(bf16[128,1792]{1,0:T(8,128)(2,1)S(1)} %collective-permute-done.11.left_ref), channel_id=1, source_target_pairs={{0,64},{64,128},{128,192},{192,0},{1,65},{65,129},{129,193},{193,1... | collective-permute-start | bytes 1376264 | tf_op jit(solution)/shard_map/ring/ppermute | solution.py:223
  216.7 17.4 %collective-permute-start.15 = (bf16[256,1536]{1,0:T(8,128)(2,1)}, bf16[256,1536]{1,0:T(8,128)(2,1)S(1)}, u32[]{:S(2)}, u32[]{:S(2)}) collective-permute-start(bf16[256,1536]{1,0:T(8,128)(2,1)} %get-tuple-element.56), channel_id=1, source_target_pairs={{0,192},{64,0},{128,64},{192,128},{1,193},{65,1},{129,65},{193,129... | collective-permute-start | bytes 2359304 | tf_op jit(solution)/shard_map/sum_blocks/ppermute | solution.py:282
  217.9 18.4 %copy-start.11 = (bf16[256,1536]{1,0:T(8,128)(2,1)S(1)}, bf16[256,1536]{1,0:T(8,128)(2,1)}, u32[]{:S(2)}) copy-start(bf16[256,1536]{1,0:T(8,128)(2,1)} %get-tuple-element.59) | copy-start | bytes 2359300
  217.9 18.4 %collective-permute-start.17 = (bf16[256,1536]{1,0:T(8,128)(2,1)}, bf16[256,1536]{1,0:T(8,128)(2,1)S(1)}, u32[]{:S(2)}, u32[]{:S(2)}) collective-permute-start(bf16[256,1536]{1,0:T(8,128)(2,1)} %get-tuple-element.60), channel_id=1, source_target_pairs={{0,64},{64,128},{128,192},{192,0},{1,65},{65,129},{129,193},{193,1... | collective-permute-start | bytes 2359304 | tf_op jit(solution)/shard_map/sum_blocks/ppermute | solution.py:281
  224.4 31.6 %copy-start.6 = (bf16[256,2048]{1,0:T(8,128)(2,1)S(1)}, bf16[256,2048]{1,0:T(8,128)(2,1)}, u32[]{:S(2)}) copy-start(bf16[256,2048]{1,0:T(8,128)(2,1)} %get-tuple-element.54) | copy-start | bytes 3145732
  234.0 22.1 %collective-permute-start.16 = (bf16[256,2048]{1,0:T(8,128)(2,1)}, bf16[256,2048]{1,0:T(8,128)(2,1)S(1)}, u32[]{:S(2)}, u32[]{:S(2)}) collective-permute-start(bf16[256,2048]{1,0:T(8,128)(2,1)} %get-tuple-element.57), channel_id=1, source_target_pairs={{0,192},{64,0},{128,64},{192,128},{1,193},{65,1},{129,65},{193,129... | collective-permute-start | bytes 3145736 | tf_op jit(solution)/shard_map/sum_blocks/ppermute | solution.py:285
  236.5 23.4 %copy-start.10 = (bf16[256,1536]{1,0:T(8,128)(2,1)S(1)}, bf16[256,1536]{1,0:T(8,128)(2,1)}, u32[]{:S(2)}) copy-start(bf16[256,1536]{1,0:T(8,128)(2,1)} %get-tuple-element.53) | copy-start | bytes 2359300
  236.5 17.0 %collective-permute-start.18 = (bf16[256,1536]{1,0:T(8,128)(2,1)S(1)}, bf16[256,1536]{1,0:T(8,128)(2,1)S(1)}, u32[]{:S(2)}, u32[]{:S(2)}) collective-permute-start(bf16[256,1536]{1,0:T(8,128)(2,1)S(1)} %add_convert_fusion.3), channel_id=1, source_target_pairs={{0,64},{64,128},{128,192},{192,0},{1,65},{65,129},{129,193},{193,1... | collective-permute-start | bytes 2359304 | tf_op jit(solution)/shard_map/sum_blocks/ppermute | solution.py:283
  253.5 22.0 %collective-permute-start.19 = (bf16[256,2048]{1,0:T(8,128)(2,1)}, bf16[256,2048]{1,0:T(8,128)(2,1)}, u32[]{:S(2)}, u32[]{:S(2)}) collective-permute-start(bf16[256,2048]{1,0:T(8,128)(2,1)} %get-tuple-element.65), channel_id=1, source_target_pairs={{0,64},{64,128},{128,192},{192,0},{1,65},{65,129},{129,193},{193,1... | collective-permute-start | bytes 3145736 | tf_op jit(solution)/shard_map/sum_blocks/ppermute | solution.py:287
  256.5 21.9 %collective-permute-start.20 = (bf16[256,2048]{1,0:T(8,128)(2,1)S(1)}, bf16[256,2048]{1,0:T(8,128)(2,1)}, u32[]{:S(2)}, u32[]{:S(2)}) collective-permute-start(bf16[256,2048]{1,0:T(8,128)(2,1)S(1)} %add_convert_fusion.1), channel_id=1, source_target_pairs={{0,192},{64,0},{128,64},{192,128},{1,193},{65,1},{129,65},{193,129... | collective-permute-start | bytes 3145736 | tf_op jit(solution)/shard_map/sum_blocks/ppermute | solution.py:290
  260.2 18.2 %copy-start.7 = (bf16[256,2048]{1,0:T(8,128)(2,1)S(1)}, bf16[256,2048]{1,0:T(8,128)(2,1)}, u32[]{:S(2)}) copy-start(bf16[256,2048]{1,0:T(8,128)(2,1)} %get-tuple-element.64) | copy-start | bytes 3145732
  261.7 35.4 %all-to-all-start.4 = ((bf16[64,4,1536]{2,1,0:T(4,128)(2,1)}), bf16[64,4,1536]{2,1,0:T(4,128)(2,1)S(1)}, u32[]{:S(2)}, u32[]{:S(2)}) async-start(bf16[64,4,1536]{2,1,0:T(4,128)(2,1)} %bitcast.35), calls=%async_computation.4 | async-start | bytes 1572864 | tf_op jit(solution)/shard_map/return_slots/all_to_all | solution.py:298
  297.1 34.8 %all-to-all-start.5 = ((bf16[64,4,2048]{2,1,0:T(4,128)(2,1)}), bf16[64,4,2048]{2,1,0:T(4,128)(2,1)S(1)}, u32[]{:S(2)}, u32[]{:S(2)}) async-start(bf16[64,4,2048]{2,1,0:T(4,128)(2,1)} %bitcast.34), calls=%async_computation.5 | async-start | bytes 2097152 | tf_op jit(solution)/shard_map/return_slots/all_to_all | solution.py:298
  303.6 29.5 %copy-start.1 = (bf16[16,3584]{1,0:T(8,128)(2,1)S(1)}, bf16[16,3584]{1,0:T(8,128)(2,1)}, u32[]{:S(2)}) copy-start(bf16[16,3584]{1,0:T(8,128)(2,1)} %param.8) | copy-start | bytes 344068
  (1 other events, 0.8 us)
Sparse Core Ops, SparseCore 0:
  17.0 127.9 all-gather.1

commit v5 on v4

--- a/solution.py
+++ b/solution.py
@@ -96,32 +96,38 @@
     )(first, x_all, w_gate, w_up)
 
 
-def hidden_kernel(own_ref, right_ref, far_ref, left_ref, down_ref, out_ref):
+def hidden_kernel(*refs):
+    *slot_refs, down_ref, out_ref = refs
+
     @pl.when(pl.program_id(0) == 0)
     def _():
         out_ref[...] = jnp.zeros_like(out_ref)
 
-    rows = jnp.concatenate([own_ref[...], right_ref[...], far_ref[...], left_ref[...]], axis=0)
+    rows = jnp.concatenate([ref[...] for ref in slot_refs], axis=0)
     out_ref[...] += lax.dot_general(rows, down_ref[0], NT, preferred_element_type=jnp.float32)
 
 
+def slot_specs(parts, step, skip):
+    return [pl.BlockSpec((part.shape[0], step), lambda k: (0, skip + k)) for part in parts]
+
+
 def hidden_grads(e, parts, w_down):
-    _, units, _ = w_down.shape
-    count, wide = parts[0].shape
-    slot_spec = pl.BlockSpec((count, STEP), lambda k: (0, k))
+    _, units, width = w_down.shape
+    rows = sum(part.shape[0] for part in parts)
     return pl.pallas_call(
         hidden_kernel,
-        out_shape=jax.ShapeDtypeStruct((4 * count, units), jnp.float32),
-        grid=(wide // STEP,),
-        in_specs=[slot_spec] * 4 + [pl.BlockSpec((1, units, STEP), lambda k: (e, 0, k))],
-        out_specs=pl.BlockSpec((4 * count, units), lambda k: (0, 0)),
+        out_shape=jax.ShapeDtypeStruct((rows, units), jnp.float32),
+        grid=(width // STEP,),
+        in_specs=slot_specs(parts, STEP, 0) + [pl.BlockSpec((1, units, STEP), lambda k: (e, 0, k))],
+        out_specs=pl.BlockSpec((rows, units), lambda k: (0, 0)),
         compiler_params=pltpu.CompilerParams(dimension_semantics=("arbitrary",)),
-        cost_estimate=pl.CostEstimate(flops=8 * count * units * wide, bytes_accessed=5 << 20, transcendentals=0),
+        cost_estimate=pl.CostEstimate(flops=2 * rows * units * width, bytes_accessed=5 << 20, transcendentals=0),
         name="hidden_grads",
     )(*parts, w_down)
 
 
-def late_kernel(own_ref, right_ref, far_ref, left_ref, hidden_ref, head_ref, gate_ref, up_ref, out_ref, pre):
+def late_kernel(*refs):
+    *slot_refs, hidden_ref, head_ref, gate_ref, up_ref, out_ref, pre = refs
     step = pl.program_id(0)
     units = gate_ref.shape[2]
 
@@ -129,7 +135,7 @@
     def _():
         pre[...] = head_ref[0]
 
-    rows = jnp.concatenate([own_ref[...], right_ref[...], far_ref[...], left_ref[...]], axis=0)
+    rows = jnp.concatenate([ref[...] for ref in slot_refs], axis=0)
     pre[:, :units] += jnp.dot(rows, gate_ref[0], preferred_element_type=jnp.float32)
     pre[:, units:] += jnp.dot(rows, up_ref[0], preferred_element_type=jnp.float32)
 
@@ -143,15 +149,14 @@
 
 def late_grads(e, parts, hidden, head_pre, w_gate, w_up):
     _, width, units = w_gate.shape
-    count, wide = parts[0].shape
-    rows = 4 * count
-    slot_spec = pl.BlockSpec((count, TAIL_STEP), lambda k: (0, k))
+    rows = sum(part.shape[0] for part in parts)
+    wide = width - HEAD
     w_spec = pl.BlockSpec((1, TAIL_STEP, units), lambda k: (e, HEAD // TAIL_STEP + k, 0))
     return pl.pallas_call(
         late_kernel,
         out_shape=jax.ShapeDtypeStruct((rows, 2 * units), jnp.bfloat16),
         grid=(wide // TAIL_STEP,),
-        in_specs=[slot_spec] * 4
+        in_specs=slot_specs(parts, TAIL_STEP, width // TAIL_STEP)
         + [
             pl.BlockSpec((rows, units), lambda k: (0, 0)),
             pl.BlockSpec((1, rows, 2 * units), lambda k: (e, 0, 0)),
@@ -219,9 +224,6 @@
     down_ring = [(i, (i + 3) % 4) for i in range(4)]
     far_ring = [(i, (i + 2) % 4) for i in range(4)]
 
-    def forward(parts, upward):
-        return lax.ppermute(parts[3], "dp", up_ring) if upward else lax.ppermute(parts[1], "dp", down_ring)
-
     with jax.named_scope("gather_tokens"):
         ids = jnp.pad(route_ids.astype(jnp.bfloat16), ((0, 0), (0, LANES - route_ids.shape[1])), constant_values=-1)
         mine = jnp.concatenate([tokens[:, :HEAD], ids], axis=1)
@@ -231,49 +233,52 @@
     with jax.named_scope("build_slots"):
         table, slot_scale = slot_table(route_ids, route_probs, experts)
         select = table.astype(jnp.bfloat16)
-        tiles = {}
+        tiles = []
         for e in range(2):
             choose = select.reshape(columns, local_experts, CAP, tok_count)[:, e].reshape(columns * CAP, tok_count)
             scale = slot_scale.reshape(columns, local_experts, CAP)[:, e].reshape(columns * CAP, 1)
             g_rows = jnp.dot(choose, out_grad, preferred_element_type=jnp.float32) * scale
             x_rows = jnp.dot(choose, tokens[:, HEAD:], preferred_element_type=jnp.float32)
-            tiles["g", e] = g_rows.astype(jnp.bfloat16).reshape(columns, CAP, -1)
-            tiles["x", e] = x_rows.astype(jnp.bfloat16).reshape(columns, CAP, -1)
-
-    order = (("x", 0), ("g", 0), ("g", 1), ("x", 1))
-    upward = (False, True, False, True)
-    sent = {}
-    for n, name in enumerate(order):
-        tile = tiles[name]
-        last = sent[order[n - 1]] if n else None
-        with jax.named_scope("send_slots"):
-            if n:
-                tile, _ = lax.optimization_barrier((tile, last[0]))
-            got = lax.all_to_all(tile, "expert", split_axis=0, concat_axis=0, tiled=True)
-            if n == len(order) - 1:
-                head_pre = head_products(first, x_all, w_gate, w_up)
-                got, last[1], last[3], head_pre = lax.optimization_barrier((got, last[1], last[3], head_pre))
-            elif n == 2:
-                early = sent[order[0]]
-                got, last[1], last[3], early[2] = lax.optimization_barrier((got, last[1], last[3], early[2]))
-            elif n:
-                got, last[1], last[3] = lax.optimization_barrier((got, last[1], last[3]))
-            own = got.transpose(1, 0, 2).reshape(columns * CAP, -1)
-        with jax.named_scope("ring"):
-            if n:
-                last[2] = forward(last, upward[n - 1])
-            right = lax.ppermute(own, "dp", down_ring)
-            left = lax.ppermute(own, "dp", up_ring)
-            sent[name] = [own, right, None, left]
-
-    hidden = hidden_grads(0, sent["g", 0], w_down)
-    with jax.named_scope("ring"):
-        final = sent["x", 1]
-        final[1], final[3], hidden = lax.optimization_barrier((final[1], final[3], hidden))
-        final[2] = forward(final, upward[3])
-    h = [late_grads(0, sent["x", 0], hidden, head_pre, w_gate, w_up)]
-    hidden = hidden_grads(1, sent["g", 1], w_down)
-    h.append(late_grads(1, final, hidden, head_pre, w_gate, w_up))
+            rows = jnp.concatenate([g_rows.astype(jnp.bfloat16), x_rows.astype(jnp.bfloat16)], axis=1)
+            tiles.append(rows.reshape(columns, CAP, -1))
+
+    def unpack(got):
+        got = got.transpose(1, 0, 2)
+        return [got[0], got[1]]
+
+    def send(slab):
+        return lax.all_to_all(slab, "expert", split_axis=0, concat_axis=0, tiled=True)
+
+    def ring(own):
+        right1 = lax.ppermute(own[1], "dp", down_ring)
+        left0 = lax.ppermute(own[0], "dp", up_ring)
+        right0 = lax.ppermute(own[0], "dp", down_ring)
+        left1 = lax.ppermute(own[1], "dp", up_ring)
+        return [right0, right1], [left0, left1]
+
+    def ring_on(left0, right1):
+        return [lax.ppermute(left0, "dp", up_ring), lax.ppermute(right1, "dp", down_ring)]
+
+    with jax.named_scope("first_expert"):
+        own = unpack(send(tiles[0]))
+        right, left = ring(own)
+        far = ring_on(left[0], right[1])
+    with jax.named_scope("second_expert"):
+        slab, _ = lax.optimization_barrier((tiles[1], own[0]))
+        got, right, left, far = lax.optimization_barrier((send(slab), right, left, far))
+        first_parts = own + right + far + left
+        hidden0 = hidden_grads(0, first_parts, w_down)
+        own = unpack(got)
+        right, left = ring(own)
+        left[0], right[1], hidden0 = lax.optimization_barrier((left[0], right[1], hidden0))
+        far = ring_on(left[0], right[1])
+        head_pre = head_products(first, x_all, w_gate, w_up)
+        h = [late_grads(0, first_parts, hidden0, head_pre, w_gate, w_up)]
+        far, left[1], right[0], h[0] = lax.optimization_barrier((far, left[1], right[0], h[0]))
+        second_parts = own + right + far + left
+
+    hidden1 = hidden_grads(1, second_parts, w_down)
+    h.append(late_grads(1, second_parts, hidden1, head_pre, w_gate, w_up))
 
     own_a, right_a, far_a, left_a = out_rows(h, w_gate, w_up, 0, OUT_SPLIT)
     own_b, right_b, far_b, left_b = out_rows(h, w_gate, w_up, OUT_SPLIT, width)

time: 341 us -> 323 us (0.947)
  starting transfers between devices: 81.7 us -> 64.8 us
    all_to_all x4 -> x2, starting transfers between devices: 36.3 us -> 19.8 us  [send(): lax.all_to_all(slab, 'expert', split_axis=0, concat_axis=0, tiled=True)]
    all_to_all x4 -> x2, waiting for transfers between devices: 38.3 us -> 42.5 us  [send(): lax.all_to_all(slab, 'expert', split_axis=0, concat_axis=0, tiled=True)]
    ppermute x12, waiting for transfers between devices: 62.5 us -> 58.4 us  [the longest x2 19 us: ring(): right1 = lax.ppermute(own[1], 'dp', down_ring)]
  transfers between devices with their start and end apart: 28 -> 26, of which waited for: 19 -> 18; matrix products, arithmetic and copies ran while one was open for 5% -> 5% of each run, Pallas kernels for 10% -> 9%
where the time goes in v5:
time: 323 us; the launch traced here: 322 us
  waiting for transfers between devices  180 us (56%)
  starting transfers between devices  64.8 us (20%)
  Pallas kernels  44 us (14%)
  between operations  13.8 us (4%)
  local copies, waits for them, and re-layouts  9.89 us (3%)
  other arithmetic  7.38 us (2%)
    all_to_all x2, waiting for transfers between devices, send(): lax.all_to_all(slab, 'expert', split_axis=0, concat_axis=0, tiled=True)  42.5 us
    all_to_all x2, waiting for transfers between devices, on_device(): lax.all_to_all(back, 'expert', split_axis=0, concat_axis=0, tiled=True)  39.6 us
    all_to_all x2, starting transfers between devices, send(): lax.all_to_all(slab, 'expert', split_axis=0, concat_axis=0, tiled=True)  19.8 us
    ppermute x2, waiting for transfers between devices, ring(): right1 = lax.ppermute(own[1], 'dp', down_ring)  19 us
    ppermute x1, waiting for transfers between devices, on_device(): from_left_a = lax.ppermute(total(right_a, from_far), 'dp', up_ring)  17.8 us
    all_to_all x2, starting transfers between devices, on_device(): lax.all_to_all(back, 'expert', split_axis=0, concat_axis=0, tiled=True)  16.2 us
    ppermute x2, waiting for transfers between devices, ring(): left1 = lax.ppermute(own[1], 'dp', up_ring)  14.4 us
    pallas_call x1, Pallas kernels, head_products(): pl.pallas_call(head_kernel, out_shape=jax.ShapeDtypeStruct((local_experts...  14 us
  transfers between devices with their start and end apart: 26, of which 18 were waited for; matrix products, arithmetic and copies ran while one was open for 5% of the time, Pallas kernels for 9%

profile of v5, /device:TPU:1, one launch (start us, length us, event | category | flops | bytes accessed | tf_op | source)
XLA Modules:
  0.0 322.2 jit_solution(1086145962479176627)
XLA Ops:
  7.4 0.8 slice.40
  8.2 2.1 collective-permute-start.14
  10.3 2.5 collective-permute-start.13
  12.8 1.2 collective-permute-start.12
  13.9 1.3 collective-permute-done.13
  15.2 0.9 collective-permute-done.12
  20.6 1.4 reshape.116
  22.0 13.7 %all-to-all-start = ((bf16[64,2,5376]{2,1,0:T(2,128)(2,1)}), bf16[64,2,5376]{2,1,0:T(2,128)(2,1)S(1)}, u32[]{:S(2)}, u32[]{:S(2)}) async-start(bf16[64,2,5376]{2,1,0:T(2,128)(2,1)} %reshape.116), calls=%async_computation | async-start | bytes 2752512 | tf_op jit(solution)/shard_map/first_expert/all_to_all | solution.py:250
  36.7 1.4 reshape.115
  38.1 41.2 %all-to-all-done = bf16[64,2,5376]{2,1,0:T(2,128)(2,1)S(1)} async-done(((bf16[64,2,5376]{2,1,0:T(2,128)(2,1)}), bf16[64,2,5376]{2,1,0:T(2,128)(2,1)S(1)}, u32[]{:S(2)}, u32[]{:S(2)}) %all-to-all-start) | async-done | bytes 1376288 | tf_op jit(solution)/shard_map/first_expert/all_to_all | solution.py:250
  79.6 6.1 %all-to-all-start.1 = ((bf16[64,2,5376]{2,1,0:T(2,128)(2,1)}), bf16[64,2,5376]{2,1,0:T(2,128)(2,1)S(1)}, u32[]{:S(2)}, u32[]{:S(2)}) async-start(bf16[64,2,5376]{2,1,0:T(2,128)(2,1)} %reshape.115), calls=%async_computation.1 | async-start | bytes 2752512 | tf_op jit(solution)/shard_map/second_expert/all_to_all | solution.py:250
  85.6 2.4 collective-permute-start.1
  88.3 2.4 collective-permute-start
  90.7 11.7 %collective-permute-done.1.refs_3_ = bf16[64,5376]{1,0:T(8,128)(2,1)S(1)} collective-permute-done((bf16[64,5376]{1,0:T(8,128)(2,1)S(1)}, bf16[64,5376]{1,0:T(8,128)(2,1)S(1)}, u32[]{:S(2)}, u32[]{:S(2)}) %collective-permute-start.1) | collective-permute-done | bytes 688160 | tf_op jit(solution)/shard_map/first_expert/ppermute | solution.py:253
  102.4 3.5 %collective-permute-start.5 = (bf16[64,5376]{1,0:T(8,128)(2,1)S(1)}, bf16[64,5376]{1,0:T(8,128)(2,1)S(1)}, u32[]{:S(2)}, u32[]{:S(2)}) collective-permute-start(bf16[64,5376]{1,0:T(8,128)(2,1)S(1)} %collective-permute-done.1.refs_3_), channel_id=1, source_target_pairs={{0,192},{64,0},{128,64},{192,128},{1,193},{65,1},{129,65},{193,129... | collective-permute-start | bytes 2064392 | tf_op jit(solution)/shard_map/first_expert/ppermute | solution.py:260
  105.9 14.4 %collective-permute-done.3.refs_7_ = bf16[64,5376]{1,0:T(8,128)(2,1)S(1)} collective-permute-done((bf16[64,5376]{1,0:T(8,128)(2,1)S(1)}, bf16[64,5376]{1,0:T(8,128)(2,1)S(1)}, u32[]{:S(2)}, u32[]{:S(2)}) %collective-permute-start.3) | collective-permute-done | bytes 688160 | tf_op jit(solution)/shard_map/first_expert/ppermute | solution.py:256
  120.3 11.6 %collective-permute-done.5.refs_5_ = bf16[64,5376]{1,0:T(8,128)(2,1)S(1)} collective-permute-done((bf16[64,5376]{1,0:T(8,128)(2,1)S(1)}, bf16[64,5376]{1,0:T(8,128)(2,1)S(1)}, u32[]{:S(2)}, u32[]{:S(2)}) %collective-permute-start.5) | collective-permute-done | bytes 688160 | tf_op jit(solution)/shard_map/first_expert/ppermute | solution.py:260
  131.9 0.8 copy-done.10
  132.7 2.3 collective-permute-done.4.refs_4_
  135.0 1.3 all-to-all-done.1
  136.6 2.4 collective-permute-start.7
  139.3 2.4 collective-permute-start.11
  141.7 4.4 %hidden_grads.2.refs_8_ = f32[512,256]{1,0:T(8,128)} custom-call(bf16[64,5376]{1,0:T(8,128)(2,1)} %copy-done.3, bf16[64,5376]{1,0:T(8,128)(2,1)} %copy-done.2, bf16[64,5376]{1,0:T(8,128)(2,1)} %copy-done.9, bf16[64,5376]{1,0:T(8,128)(2,1)} %copy-done.6, bf16[64,5376]{1,0:T(8,128)(2,1)} %collective-permute-done.4.refs_4_, bf16[64,5376]{1,0:T(8,128)(2,1)} %copy-done.10, ...), custom_call_target="tpu_custom_call" | custom-call | flops 939524096 | bytes 5242880 | tf_op jit(solution)/shard_map/second_expert/hidden_grads/pallas_call | solution.py:117
  146.1 7.3 %collective-permute-done.7.refs_3_ = bf16[64,5376]{1,0:T(8,128)(2,1)S(1)} collective-permute-done((bf16[64,5376]{1,0:T(8,128)(2,1)S(1)}, bf16[64,5376]{1,0:T(8,128)(2,1)S(1)}, u32[]{:S(2)}, u32[]{:S(2)}) %collective-permute-start.7) | collective-permute-done | bytes 688160 | tf_op jit(solution)/shard_map/second_expert/ppermute | solution.py:253
  153.4 3.1 collective-permute-done.6.refs_6_
  156.5 2.7 collective-permute-start.9
  159.2 14.0 %head_products.1.refs_9_ = f32[2,512,512]{2,1,0:T(8,128)} custom-call(s32[1]{0:T(128)} %bitcast.10.first_ref, bf16[64,4,16,1920]{3,2,1,0:T(8,128)(2,1)} %bitcast.42, bf16[2,3584,256]{2,1,0:T(8,128)(2,1)} %gate_ref.5, bf16[2,3584,256]{2,1,0:T(8,128)(2,1)} %up_ref.5), custom_call_target="tpu_custom_call" | custom-call | flops 2113929216 | bytes 20971520 | tf_op jit(solution)/shard_map/second_expert/head_products/pallas_call | solution.py:75
  173.2 4.8 %late_grads.2.h0_ref = bf16[512,512]{1,0:T(8,128)(2,1)} custom-call(bf16[64,5376]{1,0:T(8,128)(2,1)} %copy-done.3, bf16[64,5376]{1,0:T(8,128)(2,1)} %copy-done.2, bf16[64,5376]{1,0:T(8,128)(2,1)} %copy-done.9, bf16[64,5376]{1,0:T(8,128)(2,1)} %copy-done.6, bf16[64,5376]{1,0:T(8,128)(2,1)} %collective-permute-done.4.refs_4_, bf16[64,5376]{1,0:T(8,128)(2,1)} %copy-done.10, ...), custom_call_target="tpu_custom_call" | custom-call | flops 939524096 | bytes 6291456 | tf_op jit(solution)/shard_map/second_expert/late_grads/pallas_call | solution.py:155
  178.1 8.0 %collective-permute-done.8.refs_4_ = bf16[64,5376]{1,0:T(8,128)(2,1)} collective-permute-done((bf16[64,5376]{1,0:T(8,128)(2,1)S(1)}, bf16[64,5376]{1,0:T(8,128)(2,1)}, u32[]{:S(2)}, u32[]{:S(2)}) %collective-permute-start.8) | collective-permute-done | bytes 688160 | tf_op jit(solution)/shard_map/second_expert/ppermute | solution.py:260
  186.1 4.2 %hidden_grads.3.refs_8_ = f32[512,256]{1,0:T(8,128)} custom-call(bf16[64,5376]{1,0:T(8,128)(2,1)} %copy-done.5, bf16[64,5376]{1,0:T(8,128)(2,1)} %copy-done.4, bf16[64,5376]{1,0:T(8,128)(2,1)} %collective-permute-done.11.refs_2_, bf16[64,5376]{1,0:T(8,128)(2,1)} %copy-done.11, bf16[64,5376]{1,0:T(8,128)(2,1)} %collective-permute-done.8.refs_4_, ...), custom_call_target="tpu_custom_call" | custom-call | flops 939524096 | bytes 5242880 | tf_op jit(solution)/shard_map/hidden_grads/pallas_call | solution.py:117
  190.3 4.8 %late_grads.3.h1_ref = bf16[512,512]{1,0:T(8,128)(2,1)} custom-call(bf16[64,5376]{1,0:T(8,128)(2,1)} %copy-done.5, bf16[64,5376]{1,0:T(8,128)(2,1)} %copy-done.4, bf16[64,5376]{1,0:T(8,128)(2,1)} %collective-permute-done.11.refs_2_, bf16[64,5376]{1,0:T(8,128)(2,1)} %copy-done.11, bf16[64,5376]{1,0:T(8,128)(2,1)} %collective-permute-done.8.refs_4_, ...), custom_call_target="tpu_custom_call" | custom-call | flops 939524096 | bytes 6291456 | tf_op jit(solution)/shard_map/late_grads/pallas_call | solution.py:155
  195.2 5.4 %out_rows.2 = (bf16[256,1536]{1,0:T(8,128)(2,1)}, bf16[256,1536]{1,0:T(8,128)(2,1)}, bf16[256,1536]{1,0:T(8,128)(2,1)}, bf16[256,1536]{1,0:T(8,128)(2,1)}) custom-call(bf16[512,512]{1,0:T(8,128)(2,1)} %late_grads.2.h0_ref, bf16[512,512]{1,0:T(8,128)(2,1)} %late_grads.3.h1_ref, bf16[2,3584,256]{2,1,0:T(8,128)(2,1)} %gate_ref.5, bf16[2,3584,256]{2,1,0:T(8,128)(2,1)} %up_ref.5), custom_call_target="tpu_custom_call" | custom-call | flops 1610612736 | bytes 8388608 | tf_op jit(solution)/shard_map/out_rows/pallas_call | solution.py:193
  200.9 1.2 collective-permute-start.17
  202.1 6.3 %out_rows.3 = (bf16[256,2048]{1,0:T(8,128)(2,1)}, bf16[256,2048]{1,0:T(8,128)(2,1)}, bf16[256,2048]{1,0:T(8,128)(2,1)}, bf16[256,2048]{1,0:T(8,128)(2,1)}) custom-call(bf16[512,512]{1,0:T(8,128)(2,1)} %late_grads.2.h0_ref, bf16[512,512]{1,0:T(8,128)(2,1)} %late_grads.3.h1_ref, bf16[2,3584,256]{2,1,0:T(8,128)(2,1)} %gate_ref.5, bf16[2,3584,256]{2,1,0:T(8,128)(2,1)} %up_ref.5), custom_call_target="tpu_custom_call" | custom-call | flops 2147483648 | bytes 8388608 | tf_op jit(solution)/shard_map/out_rows/pallas_call | solution.py:193
  208.4 9.9 %collective-permute-done.15 = bf16[256,1536]{1,0:T(8,128)(2,1)S(1)} collective-permute-done((bf16[256,1536]{1,0:T(8,128)(2,1)}, bf16[256,1536]{1,0:T(8,128)(2,1)S(1)}, u32[]{:S(2)}, u32[]{:S(2)}) %collective-permute-start.15) | collective-permute-done | bytes 786464 | tf_op jit(solution)/shard_map/sum_blocks/ppermute | solution.py:287
  218.3 1.8 collective-permute-start.16
  220.4 17.8 %collective-permute-done.18 = bf16[256,1536]{1,0:T(8,128)(2,1)S(1)} collective-permute-done((bf16[256,1536]{1,0:T(8,128)(2,1)S(1)}, bf16[256,1536]{1,0:T(8,128)(2,1)S(1)}, u32[]{:S(2)}, u32[]{:S(2)}) %collective-permute-start.18) | collective-permute-done | bytes 786464 | tf_op jit(solution)/shard_map/sum_blocks/ppermute | solution.py:288
  238.2 2.5 collective-permute-done.16
  241.2 3.4 %collective-permute-start.20 = (bf16[256,2048]{1,0:T(8,128)(2,1)S(1)}, bf16[256,2048]{1,0:T(8,128)(2,1)}, u32[]{:S(2)}, u32[]{:S(2)}) collective-permute-start(bf16[256,2048]{1,0:T(8,128)(2,1)S(1)} %add_convert_fusion.1), channel_id=1, source_target_pairs={{0,192},{64,0},{128,64},{192,128},{1,193},{65,1},{129,65},{193,129... | collective-permute-start | bytes 3145736 | tf_op jit(solution)/shard_map/sum_blocks/ppermute | solution.py:295
  244.9 1.5 copy.64
  246.4 10.0 %all-to-all-start.2 = ((bf16[64,4,1536]{2,1,0:T(4,128)(2,1)}), bf16[64,4,1536]{2,1,0:T(4,128)(2,1)S(1)}, u32[]{:S(2)}, u32[]{:S(2)}) async-start(bf16[64,4,1536]{2,1,0:T(4,128)(2,1)} %bitcast.41), calls=%async_computation.2 | async-start | bytes 1572864 | tf_op jit(solution)/shard_map/return_slots/all_to_all | solution.py:303
  256.3 4.7 %collective-permute-done.19 = bf16[256,2048]{1,0:T(8,128)(2,1)} collective-permute-done((bf16[256,2048]{1,0:T(8,128)(2,1)}, bf16[256,2048]{1,0:T(8,128)(2,1)}, u32[]{:S(2)}, u32[]{:S(2)}) %collective-permute-start.19) | collective-permute-done | bytes 1048608 | tf_op jit(solution)/shard_map/sum_blocks/ppermute | solution.py:292
  261.0 2.9 collective-permute-done.20
  263.9 2.1 add_convert_fusion
  266.0 1.8 copy.63
  267.8 11.5 %all-to-all-done.2 = bf16[64,4,1536]{2,1,0:T(4,128)(2,1)S(1)} async-done(((bf16[64,4,1536]{2,1,0:T(4,128)(2,1)}), bf16[64,4,1536]{2,1,0:T(4,128)(2,1)S(1)}, u32[]{:S(2)}, u32[]{:S(2)}) %all-to-all-start.2) | async-done | bytes 786464 | tf_op jit(solution)/shard_map/return_slots/all_to_all | solution.py:303
  279.3 6.2 %all-to-all-start.3 = ((bf16[64,4,2048]{2,1,0:T(4,128)(2,1)}), bf16[64,4,2048]{2,1,0:T(4,128)(2,1)S(1)}, u32[]{:S(2)}, u32[]{:S(2)}) async-start(bf16[64,4,2048]{2,1,0:T(4,128)(2,1)} %bitcast.40), calls=%async_computation.3 | async-start | bytes 2097152 | tf_op jit(solution)/shard_map/return_slots/all_to_all | solution.py:303
  286.1 28.0 %all-to-all-done.3 = bf16[64,4,2048]{2,1,0:T(4,128)(2,1)S(1)} async-done(((bf16[64,4,2048]{2,1,0:T(4,128)(2,1)}), bf16[64,4,2048]{2,1,0:T(4,128)(2,1)S(1)}, u32[]{:S(2)}, u32[]{:S(2)}) %all-to-all-start.3) | async-done | bytes 1048608 | tf_op jit(solution)/shard_map/return_slots/all_to_all | solution.py:303
  (98 shorter events, 10.3 us)
Async XLA Ops:
  6.5 13.6 %copy-start = (bf16[16,3584]{1,0:T(8,128)(2,1)S(1)}, bf16[16,3584]{1,0:T(8,128)(2,1)}, u32[]{:S(2)}) copy-start(bf16[16,3584]{1,0:T(8,128)(2,1)} %param.8) | copy-start | bytes 344068
  6.5 13.3 %copy-start.18 = (bf16[16,3584]{1,0:T(8,128)(2,1)S(1)}, bf16[16,3584]{1,0:T(8,128)(2,1)}, u32[]{:S(2)}) copy-start(bf16[16,3584]{1,0:T(8,128)(2,1)} %param.7) | copy-start | bytes 344068
  6.5 152.6 %all-gather.2.cloned.1.call-start = ((), (), s32[]{:S(2)}) async-start(), calls=%async_computation.4 | async-start | bytes 15974400 | tf_op jit(solution)/shard_map/gather_tokens/all_gather | solution.py:231
  8.2 5.7 %collective-permute-start.14 = (bf16[16,1920]{1,0:T(8,128)(2,1)S(1)}, bf16[16,1920]{1,0:T(8,128)(2,1)S(1)}, u32[]{:S(2)}, u32[]{:S(2)}) collective-permute-start(bf16[16,1920]{1,0:T(8,128)(2,1)S(1)} %pad_maximum_fusion.4), channel_id=1, source_target_pairs={{0,64},{64,128},{128,192},{192,0},{1,65},{65,129},{129,193},{193,1... | collective-permute-start | bytes 184328 | tf_op jit(solution)/shard_map/gather_tokens/ppermute | solution.py:230
  10.3 4.9 %collective-permute-start.13 = (bf16[16,1920]{1,0:T(8,128)(2,1)S(1)}, bf16[16,1920]{1,0:T(8,128)(2,1)S(1)}, u32[]{:S(2)}, u32[]{:S(2)}) collective-permute-start(bf16[16,1920]{1,0:T(8,128)(2,1)S(1)} %pad_maximum_fusion.4), channel_id=1, source_target_pairs={{0,128},{64,192},{128,0},{192,64},{1,129},{65,193},{129,1},{193,65... | collective-permute-start | bytes 184328 | tf_op jit(solution)/shard_map/gather_tokens/ppermute | solution.py:230
  12.8 3.4 %collective-permute-start.12 = (bf16[16,1920]{1,0:T(8,128)(2,1)S(1)}, bf16[16,1920]{1,0:T(8,128)(2,1)S(1)}, u32[]{:S(2)}, u32[]{:S(2)}) collective-permute-start(bf16[16,1920]{1,0:T(8,128)(2,1)S(1)} %pad_maximum_fusion.4), channel_id=1, source_target_pairs={{0,192},{64,0},{128,64},{192,128},{1,193},{65,1},{129,65},{193,129... | collective-permute-start | bytes 184328 | tf_op jit(solution)/shard_map/gather_tokens/ppermute | solution.py:230
  22.0 57.3 %all-to-all-start = ((bf16[64,2,5376]{2,1,0:T(2,128)(2,1)}), bf16[64,2,5376]{2,1,0:T(2,128)(2,1)S(1)}, u32[]{:S(2)}, u32[]{:S(2)}) async-start(bf16[64,2,5376]{2,1,0:T(2,128)(2,1)} %reshape.116), calls=%async_computation | async-start | bytes 2752512 | tf_op jit(solution)/shard_map/first_expert/all_to_all | solution.py:250
  79.5 56.9 %copy-start.2 = (bf16[64,5376]{1,0:T(8,128)(2,1)}, bf16[64,5376]{1,0:T(8,128)(2,1)S(1)}, u32[]{:S(2)}) copy-start(bf16[64,5376]{1,0:T(8,128)(2,1)S(1)} %get-tuple-element.71.refs_1_) | copy-start | bytes 2064388
  79.5 56.9 %copy-start.3 = (bf16[64,5376]{1,0:T(8,128)(2,1)}, bf16[64,5376]{1,0:T(8,128)(2,1)S(1)}, u32[]{:S(2)}) copy-start(bf16[64,5376]{1,0:T(8,128)(2,1)S(1)} %get-tuple-element.72.refs_0_) | copy-start | bytes 2064388
  79.6 56.8 %all-to-all-start.1 = ((bf16[64,2,5376]{2,1,0:T(2,128)(2,1)}), bf16[64,2,5376]{2,1,0:T(2,128)(2,1)S(1)}, u32[]{:S(2)}, u32[]{:S(2)}) async-start(bf16[64,2,5376]{2,1,0:T(2,128)(2,1)} %reshape.115), calls=%async_computation.1 | async-start | bytes 2752512 | tf_op jit(solution)/shard_map/second_expert/all_to_all | solution.py:250
  85.6 16.7 %collective-permute-start.1 = (bf16[64,5376]{1,0:T(8,128)(2,1)S(1)}, bf16[64,5376]{1,0:T(8,128)(2,1)S(1)}, u32[]{:S(2)}, u32[]{:S(2)}) collective-permute-start(bf16[64,5376]{1,0:T(8,128)(2,1)S(1)} %get-tuple-element.71.refs_1_), channel_id=1, source_target_pairs={{0,192},{64,0},{128,64},{192,128},{1,193},{65,1},{129,65},{193,129... | collective-permute-start | bytes 2064392 | tf_op jit(solution)/shard_map/first_expert/ppermute | solution.py:253
  88.0 17.9 %collective-permute-start.2 = (bf16[64,5376]{1,0:T(8,128)(2,1)S(1)}, bf16[64,5376]{1,0:T(8,128)(2,1)S(1)}, u32[]{:S(2)}, u32[]{:S(2)}) collective-permute-start(bf16[64,5376]{1,0:T(8,128)(2,1)S(1)} %get-tuple-element.72.refs_0_), channel_id=1, source_target_pairs={{0,64},{64,128},{128,192},{192,0},{1,65},{65,129},{129,193},{193,1... | collective-permute-start | bytes 2064392 | tf_op jit(solution)/shard_map/first_expert/ppermute | solution.py:254
  88.0 32.3 %collective-permute-start.3 = (bf16[64,5376]{1,0:T(8,128)(2,1)S(1)}, bf16[64,5376]{1,0:T(8,128)(2,1)S(1)}, u32[]{:S(2)}, u32[]{:S(2)}) collective-permute-start(bf16[64,5376]{1,0:T(8,128)(2,1)S(1)} %get-tuple-element.71.refs_1_), channel_id=1, source_target_pairs={{0,64},{64,128},{128,192},{192,0},{1,65},{65,129},{129,193},{193,1... | collective-permute-start | bytes 2064392 | tf_op jit(solution)/shard_map/first_expert/ppermute | solution.py:256
  88.3 32.0 %collective-permute-start = (bf16[64,5376]{1,0:T(8,128)(2,1)S(1)}, bf16[64,5376]{1,0:T(8,128)(2,1)S(1)}, u32[]{:S(2)}, u32[]{:S(2)}) collective-permute-start(bf16[64,5376]{1,0:T(8,128)(2,1)S(1)} %get-tuple-element.72.refs_0_), channel_id=1, source_target_pairs={{0,192},{64,0},{128,64},{192,128},{1,193},{65,1},{129,65},{193,129... | collective-permute-start | bytes 2064392 | tf_op jit(solution)/shard_map/first_expert/ppermute | solution.py:255
  102.4 34.2 %copy-start.6 = (bf16[64,5376]{1,0:T(8,128)(2,1)}, bf16[64,5376]{1,0:T(8,128)(2,1)S(1)}, u32[]{:S(2)}) copy-start(bf16[64,5376]{1,0:T(8,128)(2,1)S(1)} %collective-permute-done.1.refs_3_) | copy-start | bytes 2064388
  102.4 29.5 %collective-permute-start.5 = (bf16[64,5376]{1,0:T(8,128)(2,1)S(1)}, bf16[64,5376]{1,0:T(8,128)(2,1)S(1)}, u32[]{:S(2)}, u32[]{:S(2)}) collective-permute-start(bf16[64,5376]{1,0:T(8,128)(2,1)S(1)} %collective-permute-done.1.refs_3_), channel_id=1, source_target_pairs={{0,192},{64,0},{128,64},{192,128},{1,193},{65,1},{129,65},{193,129... | collective-permute-start | bytes 2064392 | tf_op jit(solution)/shard_map/first_expert/ppermute | solution.py:260
  105.9 26.0 %copy-start.7 = (bf16[64,5376]{1,0:T(8,128)(2,1)}, bf16[64,5376]{1,0:T(8,128)(2,1)S(1)}, u32[]{:S(2)}) copy-start(bf16[64,5376]{1,0:T(8,128)(2,1)S(1)} %collective-permute-done.2.refs_6_) | copy-start | bytes 2064388
  105.9 29.2 %collective-permute-start.4 = (bf16[64,5376]{1,0:T(8,128)(2,1)S(1)}, bf16[64,5376]{1,0:T(8,128)(2,1)}, u32[]{:S(2)}, u32[]{:S(2)}) collective-permute-start(bf16[64,5376]{1,0:T(8,128)(2,1)S(1)} %collective-permute-done.2.refs_6_), channel_id=1, source_target_pairs={{0,64},{64,128},{128,192},{192,0},{1,65},{65,129},{129,193},{193,1... | collective-permute-start | bytes 2064392 | tf_op jit(solution)/shard_map/first_expert/ppermute | solution.py:260
  120.3 11.6 %copy-start.8 = (bf16[64,5376]{1,0:T(8,128)(2,1)}, bf16[64,5376]{1,0:T(8,128)(2,1)S(1)}, u32[]{:S(2)}) copy-start(bf16[64,5376]{1,0:T(8,128)(2,1)S(1)} %collective-permute-done.3.refs_7_) | copy-start | bytes 2064388
  120.3 11.6 %copy-start.9 = (bf16[64,5376]{1,0:T(8,128)(2,1)}, bf16[64,5376]{1,0:T(8,128)(2,1)S(1)}, u32[]{:S(2)}) copy-start(bf16[64,5376]{1,0:T(8,128)(2,1)S(1)} %collective-permute-done.refs_2_) | copy-start | bytes 2064388
  131.9 0.8 copy-start.10
  136.6 9.5 %copy-start.4 = (bf16[64,5376]{1,0:T(8,128)(2,1)}, bf16[64,5376]{1,0:T(8,128)(2,1)S(1)}, u32[]{:S(2)}) copy-start(bf16[64,5376]{1,0:T(8,128)(2,1)S(1)} %get-tuple-element.69.refs_1_) | copy-start | bytes 2064388
  136.6 9.5 %copy-start.5 = (bf16[64,5376]{1,0:T(8,128)(2,1)}, bf16[64,5376]{1,0:T(8,128)(2,1)S(1)}, u32[]{:S(2)}) copy-start(bf16[64,5376]{1,0:T(8,128)(2,1)S(1)} %get-tuple-element.70.refs_0_) | copy-start | bytes 2064388
  136.6 16.8 %collective-permute-start.7 = (bf16[64,5376]{1,0:T(8,128)(2,1)S(1)}, bf16[64,5376]{1,0:T(8,128)(2,1)S(1)}, u32[]{:S(2)}, u32[]{:S(2)}) collective-permute-start(bf16[64,5376]{1,0:T(8,128)(2,1)S(1)} %get-tuple-element.69.refs_1_), channel_id=1, source_target_pairs={{0,192},{64,0},{128,64},{192,128},{1,193},{65,1},{129,65},{193,129... | collective-permute-start | bytes 2064392 | tf_op jit(solution)/shard_map/second_expert/ppermute | solution.py:253
  139.0 17.5 %collective-permute-start.6 = (bf16[64,5376]{1,0:T(8,128)(2,1)S(1)}, bf16[64,5376]{1,0:T(8,128)(2,1)S(1)}, u32[]{:S(2)}, u32[]{:S(2)}) collective-permute-start(bf16[64,5376]{1,0:T(8,128)(2,1)S(1)} %get-tuple-element.70.refs_0_), channel_id=1, source_target_pairs={{0,64},{64,128},{128,192},{192,0},{1,65},{65,129},{129,193},{193,1... | collective-permute-start | bytes 2064392 | tf_op jit(solution)/shard_map/second_expert/ppermute | solution.py:254
  139.0 39.1 %collective-permute-start.10 = (bf16[64,5376]{1,0:T(8,128)(2,1)S(1)}, bf16[64,5376]{1,0:T(8,128)(2,1)S(1)}, u32[]{:S(2)}, u32[]{:S(2)}) collective-permute-start(bf16[64,5376]{1,0:T(8,128)(2,1)S(1)} %get-tuple-element.69.refs_1_), channel_id=1, source_target_pairs={{0,64},{64,128},{128,192},{192,0},{1,65},{65,129},{129,193},{193,1... | collective-permute-start | bytes 2064392 | tf_op jit(solution)/shard_map/second_expert/ppermute | solution.py:256
  139.3 38.8 %collective-permute-start.11 = (bf16[64,5376]{1,0:T(8,128)(2,1)S(1)}, bf16[64,5376]{1,0:T(8,128)(2,1)}, u32[]{:S(2)}, u32[]{:S(2)}) collective-permute-start(bf16[64,5376]{1,0:T(8,128)(2,1)S(1)} %get-tuple-element.70.refs_0_), channel_id=1, source_target_pairs={{0,192},{64,0},{128,64},{192,128},{1,193},{65,1},{129,65},{193,129... | collective-permute-start | bytes 2064392 | tf_op jit(solution)/shard_map/second_expert/ppermute | solution.py:255
  153.4 19.8 %copy-start.11 = (bf16[64,5376]{1,0:T(8,128)(2,1)}, bf16[64,5376]{1,0:T(8,128)(2,1)S(1)}, u32[]{:S(2)}) copy-start(bf16[64,5376]{1,0:T(8,128)(2,1)S(1)} %collective-permute-done.7.refs_3_) | copy-start | bytes 2064388
  156.5 16.7 %copy-start.12 = (bf16[64,5376]{1,0:T(8,128)(2,1)}, bf16[64,5376]{1,0:T(8,128)(2,1)S(1)}, u32[]{:S(2)}) copy-start(bf16[64,5376]{1,0:T(8,128)(2,1)S(1)} %collective-permute-done.6.refs_6_) | copy-start | bytes 2064388
  156.5 29.6 %collective-permute-start.8 = (bf16[64,5376]{1,0:T(8,128)(2,1)S(1)}, bf16[64,5376]{1,0:T(8,128)(2,1)}, u32[]{:S(2)}, u32[]{:S(2)}) collective-permute-start(bf16[64,5376]{1,0:T(8,128)(2,1)S(1)} %collective-permute-done.6.refs_6_), channel_id=1, source_target_pairs={{0,64},{64,128},{128,192},{192,0},{1,65},{65,129},{129,193},{193,1... | collective-permute-start | bytes 2064392 | tf_op jit(solution)/shard_map/second_expert/ppermute | solution.py:260
  156.5 29.6 %collective-permute-start.9 = (bf16[64,5376]{1,0:T(8,128)(2,1)S(1)}, bf16[64,5376]{1,0:T(8,128)(2,1)}, u32[]{:S(2)}, u32[]{:S(2)}) collective-permute-start(bf16[64,5376]{1,0:T(8,128)(2,1)S(1)} %collective-permute-done.7.refs_3_), channel_id=1, source_target_pairs={{0,192},{64,0},{128,64},{192,128},{1,193},{65,1},{129,65},{193,129... | collective-permute-start | bytes 2064392 | tf_op jit(solution)/shard_map/second_expert/ppermute | solution.py:260
  178.0 8.0 %copy-start.13 = (bf16[64,5376]{1,0:T(8,128)(2,1)}, bf16[64,5376]{1,0:T(8,128)(2,1)S(1)}, u32[]{:S(2)}) copy-start(bf16[64,5376]{1,0:T(8,128)(2,1)S(1)} %collective-permute-done.10.refs_7_) | copy-start | bytes 2064388
  200.6 17.7 %collective-permute-start.15 = (bf16[256,1536]{1,0:T(8,128)(2,1)}, bf16[256,1536]{1,0:T(8,128)(2,1)S(1)}, u32[]{:S(2)}, u32[]{:S(2)}) collective-permute-start(bf16[256,1536]{1,0:T(8,128)(2,1)} %get-tuple-element.54), channel_id=1, source_target_pairs={{0,192},{64,0},{128,64},{192,128},{1,193},{65,1},{129,65},{193,129... | collective-permute-start | bytes 2359304 | tf_op jit(solution)/shard_map/sum_blocks/ppermute | solution.py:287
  200.9 19.2 %copy-start.17 = (bf16[256,1536]{1,0:T(8,128)(2,1)S(1)}, bf16[256,1536]{1,0:T(8,128)(2,1)}, u32[]{:S(2)}) copy-start(bf16[256,1536]{1,0:T(8,128)(2,1)} %get-tuple-element.57) | copy-start | bytes 2359300
  200.9 19.2 %collective-permute-start.17 = (bf16[256,1536]{1,0:T(8,128)(2,1)}, bf16[256,1536]{1,0:T(8,128)(2,1)S(1)}, u32[]{:S(2)}, u32[]{:S(2)}) collective-permute-start(bf16[256,1536]{1,0:T(8,128)(2,1)} %get-tuple-element.58), channel_id=1, source_target_pairs={{0,64},{64,128},{128,192},{192,0},{1,65},{65,129},{129,193},{193,1... | collective-permute-start | bytes 2359304 | tf_op jit(solution)/shard_map/sum_blocks/ppermute | solution.py:286
  208.4 32.3 %copy-start.14 = (bf16[256,2048]{1,0:T(8,128)(2,1)S(1)}, bf16[256,2048]{1,0:T(8,128)(2,1)}, u32[]{:S(2)}) copy-start(bf16[256,2048]{1,0:T(8,128)(2,1)} %get-tuple-element.52) | copy-start | bytes 3145732
  218.3 22.4 %collective-permute-start.16 = (bf16[256,2048]{1,0:T(8,128)(2,1)}, bf16[256,2048]{1,0:T(8,128)(2,1)S(1)}, u32[]{:S(2)}, u32[]{:S(2)}) collective-permute-start(bf16[256,2048]{1,0:T(8,128)(2,1)} %get-tuple-element.55), channel_id=1, source_target_pairs={{0,192},{64,0},{128,64},{192,128},{1,193},{65,1},{129,65},{193,129... | collective-permute-start | bytes 3145736 | tf_op jit(solution)/shard_map/sum_blocks/ppermute | solution.py:290
  220.3 24.3 %copy-start.16 = (bf16[256,1536]{1,0:T(8,128)(2,1)S(1)}, bf16[256,1536]{1,0:T(8,128)(2,1)}, u32[]{:S(2)}) copy-start(bf16[256,1536]{1,0:T(8,128)(2,1)} %get-tuple-element.51) | copy-start | bytes 2359300
  220.3 17.9 %collective-permute-start.18 = (bf16[256,1536]{1,0:T(8,128)(2,1)S(1)}, bf16[256,1536]{1,0:T(8,128)(2,1)S(1)}, u32[]{:S(2)}, u32[]{:S(2)}) collective-permute-start(bf16[256,1536]{1,0:T(8,128)(2,1)S(1)} %add_convert_fusion.3), channel_id=1, source_target_pairs={{0,64},{64,128},{128,192},{192,0},{1,65},{65,129},{129,193},{193,1... | collective-permute-start | bytes 2359304 | tf_op jit(solution)/shard_map/sum_blocks/ppermute | solution.py:288
  238.2 22.8 %collective-permute-start.19 = (bf16[256,2048]{1,0:T(8,128)(2,1)}, bf16[256,2048]{1,0:T(8,128)(2,1)}, u32[]{:S(2)}, u32[]{:S(2)}) collective-permute-start(bf16[256,2048]{1,0:T(8,128)(2,1)} %get-tuple-element.63), channel_id=1, source_target_pairs={{0,64},{64,128},{128,192},{192,0},{1,65},{65,129},{129,193},{193,1... | collective-permute-start | bytes 3145736 | tf_op jit(solution)/shard_map/sum_blocks/ppermute | solution.py:292
  241.2 22.7 %collective-permute-start.20 = (bf16[256,2048]{1,0:T(8,128)(2,1)S(1)}, bf16[256,2048]{1,0:T(8,128)(2,1)}, u32[]{:S(2)}, u32[]{:S(2)}) collective-permute-start(bf16[256,2048]{1,0:T(8,128)(2,1)S(1)} %add_convert_fusion.1), channel_id=1, source_target_pairs={{0,192},{64,0},{128,64},{192,128},{1,193},{65,1},{129,65},{193,129... | collective-permute-start | bytes 3145736 | tf_op jit(solution)/shard_map/sum_blocks/ppermute | solution.py:295
  244.9 19.1 %copy-start.15 = (bf16[256,2048]{1,0:T(8,128)(2,1)S(1)}, bf16[256,2048]{1,0:T(8,128)(2,1)}, u32[]{:S(2)}) copy-start(bf16[256,2048]{1,0:T(8,128)(2,1)} %get-tuple-element.62) | copy-start | bytes 3145732
  246.4 33.0 %all-to-all-start.2 = ((bf16[64,4,1536]{2,1,0:T(4,128)(2,1)}), bf16[64,4,1536]{2,1,0:T(4,128)(2,1)S(1)}, u32[]{:S(2)}, u32[]{:S(2)}) async-start(bf16[64,4,1536]{2,1,0:T(4,128)(2,1)} %bitcast.41), calls=%async_computation.2 | async-start | bytes 1572864 | tf_op jit(solution)/shard_map/return_slots/all_to_all | solution.py:303
  279.3 34.8 %all-to-all-start.3 = ((bf16[64,4,2048]{2,1,0:T(4,128)(2,1)}), bf16[64,4,2048]{2,1,0:T(4,128)(2,1)S(1)}, u32[]{:S(2)}, u32[]{:S(2)}) async-start(bf16[64,4,2048]{2,1,0:T(4,128)(2,1)} %bitcast.40), calls=%async_computation.3 | async-start | bytes 2097152 | tf_op jit(solution)/shard_map/return_slots/all_to_all | solution.py:303
  285.8 29.5 %copy-start.1 = (bf16[16,3584]{1,0:T(8,128)(2,1)S(1)}, bf16[16,3584]{1,0:T(8,128)(2,1)}, u32[]{:S(2)}) copy-start(bf16[16,3584]{1,0:T(8,128)(2,1)} %param.8) | copy-start | bytes 344068
Sparse Core Ops, SparseCore 0:
  17.0 137.4 all-gather.1

commit v6 on v5

--- a/solution.py
+++ b/solution.py
@@ -11,8 +11,7 @@
 HEAD = 1792
 STEP = 1792
 TAIL_STEP = 896
-OUT_STEP = 512
-OUT_SPLIT = 1536
+OUT_SPLIT = 2304
 NT = (((1,), (1,)), ((), ()))
 
 
@@ -184,18 +183,18 @@
             out_ref[e * part : (e + 1) * part, :] = value[r * part : (r + 1) * part]
 
 
-def out_rows(h, w_gate, w_up, start, stop):
+def out_rows(h, w_gate, w_up, start, stop, step):
     rows = h[0].shape[0]
     local_experts, width, units = w_gate.shape
     count = local_experts * rows // 4
     h_spec = pl.BlockSpec((rows, 2 * units), lambda n: (0, 0))
-    w_spec = pl.BlockSpec((local_experts, OUT_STEP, units), lambda n: (0, start // OUT_STEP + n, 0))
+    w_spec = pl.BlockSpec((local_experts, step, units), lambda n: (0, start // step + n, 0))
     return pl.pallas_call(
         out_kernel,
         out_shape=[jax.ShapeDtypeStruct((count, stop - start), jnp.bfloat16)] * 4,
-        grid=((stop - start) // OUT_STEP,),
+        grid=((stop - start) // step,),
         in_specs=[h_spec, h_spec, w_spec, w_spec],
-        out_specs=[pl.BlockSpec((count, OUT_STEP), lambda n: (0, n))] * 4,
+        out_specs=[pl.BlockSpec((count, step), lambda n: (0, n))] * 4,
         compiler_params=pltpu.CompilerParams(dimension_semantics=("arbitrary",)),
         cost_estimate=pl.CostEstimate(
             flops=2 * local_experts * rows * 2 * units * (stop - start), bytes_accessed=8 << 20, transcendentals=0
@@ -227,8 +226,7 @@
     with jax.named_scope("gather_tokens"):
         ids = jnp.pad(route_ids.astype(jnp.bfloat16), ((0, 0), (0, LANES - route_ids.shape[1])), constant_values=-1)
         mine = jnp.concatenate([tokens[:, :HEAD], ids], axis=1)
-        near = jnp.concatenate([mine] + [lax.ppermute(mine, "dp", ring) for ring in (down_ring, far_ring, up_ring)])
-        x_all = lax.all_gather(near, "expert", axis=0, tiled=True).reshape(columns, 4, tok_count, HEAD + LANES)
+        pieces = [mine] + [lax.ppermute(mine, "dp", ring) for ring in (down_ring, far_ring, up_ring)]
 
     with jax.named_scope("build_slots"):
         table, slot_scale = slot_table(route_ids, route_probs, experts)
@@ -241,6 +239,11 @@
             x_rows = jnp.dot(choose, tokens[:, HEAD:], preferred_element_type=jnp.float32)
             rows = jnp.concatenate([g_rows.astype(jnp.bfloat16), x_rows.astype(jnp.bfloat16)], axis=1)
             tiles.append(rows.reshape(columns, CAP, -1))
+
+    with jax.named_scope("gather_tokens"):
+        tiles[0], pieces = lax.optimization_barrier((tiles[0], pieces))
+        near = jnp.concatenate(pieces)
+        x_all = lax.all_gather(near, "expert", axis=0, tiled=True).reshape(columns, 4, tok_count, HEAD + LANES)
 
     def unpack(got):
         got = got.transpose(1, 0, 2)
@@ -280,8 +283,8 @@
     hidden1 = hidden_grads(1, second_parts, w_down)
     h.append(late_grads(1, second_parts, hidden1, head_pre, w_gate, w_up))
 
-    own_a, right_a, far_a, left_a = out_rows(h, w_gate, w_up, 0, OUT_SPLIT)
-    own_b, right_b, far_b, left_b = out_rows(h, w_gate, w_up, OUT_SPLIT, width)
+    own_a, right_a, far_a, left_a = out_rows(h, w_gate, w_up, OUT_SPLIT, width, 256)
+    own_b, right_b, far_b, left_b = out_rows(h, w_gate, w_up, 0, OUT_SPLIT, 768)
     with jax.named_scope("sum_blocks"):
         from_far = lax.ppermute(far_a, "dp", up_ring)
         from_right_a = lax.ppermute(left_a, "dp", down_ring)
@@ -308,7 +311,7 @@
                     preferred_element_type=jnp.float32,
                 ).astype(jnp.bfloat16)
             )
-    return jnp.concatenate(results, axis=1)
+    return jnp.concatenate(results[::-1], axis=1)
 
 
 def solution(mesh):

time: 323 us -> 320 us (level)
  starting transfers between devices: 64.8 us -> 59.7 us
    ppermute x1, waiting for transfers between devices: 2.51 us -> 8.27 us  [on_device(): from_far = lax.ppermute(far_b, 'dp', down_ring)]
    ppermute x1, waiting for transfers between devices: 2.92 us -> 8.4 us  [on_device(): from_right_b = lax.ppermute(left_b, 'dp', down_ring)]
    ppermute x2, starting transfers between devices: 4.73 us -> 0.19 us  [ring(): right1 = lax.ppermute(own[1], 'dp', down_ring)]
    all_to_all x2, waiting for transfers between devices: 39.6 us -> 35.3 us  [on_device(): lax.all_to_all(back, 'expert', split_axis=0, concat_axis=0, tiled=True)]
    all_to_all x2, waiting for transfers between devices: 42.5 us -> 45.7 us  [send(): lax.all_to_all(slab, 'expert', split_axis=0, concat_axis=0, tiled=True)]
  transfers between devices with their start and end apart: 26 -> 26, of which waited for: 18 -> 16; matrix products, arithmetic and copies ran while one was open for 5% -> 4% of each run, Pallas kernels for 9% -> 9%
where the time goes in v6:
time: 320 us; the launch traced here: 319 us
  waiting for transfers between devices  182 us (57%)
  starting transfers between devices  59.7 us (19%)
  Pallas kernels  44.7 us (14%)
  between operations  13.8 us (4%)
  local copies, waits for them, and re-layouts  9.92 us (3%)
  other arithmetic  7.13 us (2%)
    all_to_all x2, waiting for transfers between devices, send(): lax.all_to_all(slab, 'expert', split_axis=0, concat_axis=0, tiled=True)  45.7 us
    all_to_all x2, waiting for transfers between devices, on_device(): lax.all_to_all(back, 'expert', split_axis=0, concat_axis=0, tiled=True)  35.3 us
    ppermute x2, waiting for transfers between devices, ring(): right1 = lax.ppermute(own[1], 'dp', down_ring)  20.8 us
    all_to_all x2, starting transfers between devices, send(): lax.all_to_all(slab, 'expert', split_axis=0, concat_axis=0, tiled=True)  19.3 us
    all_to_all x2, starting transfers between devices, on_device(): lax.all_to_all(back, 'expert', split_axis=0, concat_axis=0, tiled=True)  15.4 us
    ppermute x1, waiting for transfers between devices, on_device(): from_left_a = lax.ppermute(total(right_a, from_far), 'dp', up_ring)  15.3 us
    ppermute x2, waiting for transfers between devices, ring(): left1 = lax.ppermute(own[1], 'dp', up_ring)  14.3 us
    pallas_call x1, Pallas kernels, head_products(): pl.pallas_call(head_kernel, out_shape=jax.ShapeDtypeStruct((local_experts...  14 us
  transfers between devices with their start and end apart: 26, of which 16 were waited for; matrix products, arithmetic and copies ran while one was open for 4% of the time, Pallas kernels for 9%

profile of v6, /device:TPU:1, one launch (start us, length us, event | category | flops | bytes accessed | tf_op | source)
XLA Modules:
  0.0 318.5 jit_solution(16334041782190128650)
XLA Ops:
  6.5 0.7 convert_element_type.74
  7.4 0.8 slice.36
  8.2 2.1 collective-permute-start.2
  10.3 2.5 collective-permute-start.1
  12.8 1.2 collective-permute-start
  13.9 0.8 fusion.3
  14.9 0.8 select_reduce_fusion.1
  17.6 1.4 reshape.116
  19.8 13.2 %all-to-all-start = ((bf16[64,2,5376]{2,1,0:T(2,128)(2,1)}), bf16[64,2,5376]{2,1,0:T(2,128)(2,1)S(1)}, u32[]{:S(2)}, u32[]{:S(2)}) async-start(bf16[64,2,5376]{2,1,0:T(2,128)(2,1)} %reshape.116), calls=%async_computation | async-start | bytes 2752512 | tf_op jit(solution)/shard_map/first_expert/all_to_all | solution.py:253
  33.9 1.4 reshape.115
  35.3 42.5 %all-to-all-done = bf16[64,2,5376]{2,1,0:T(2,128)(2,1)S(1)} async-done(((bf16[64,2,5376]{2,1,0:T(2,128)(2,1)}), bf16[64,2,5376]{2,1,0:T(2,128)(2,1)S(1)}, u32[]{:S(2)}, u32[]{:S(2)}) %all-to-all-start) | async-done | bytes 1376288 | tf_op jit(solution)/shard_map/first_expert/all_to_all | solution.py:253
  78.0 6.2 %all-to-all-start.1 = ((bf16[64,2,5376]{2,1,0:T(2,128)(2,1)}), bf16[64,2,5376]{2,1,0:T(2,128)(2,1)S(1)}, u32[]{:S(2)}, u32[]{:S(2)}) async-start(bf16[64,2,5376]{2,1,0:T(2,128)(2,1)} %reshape.115), calls=%async_computation.1 | async-start | bytes 2752512 | tf_op jit(solution)/shard_map/second_expert/all_to_all | solution.py:253
  84.3 1.4 collective-permute-start.5
  86.1 2.4 collective-permute-start.3
  88.4 12.5 %collective-permute-done.4.refs_3_ = bf16[64,5376]{1,0:T(8,128)(2,1)S(1)} collective-permute-done((bf16[64,5376]{1,0:T(8,128)(2,1)S(1)}, bf16[64,5376]{1,0:T(8,128)(2,1)S(1)}, u32[]{:S(2)}, u32[]{:S(2)}) %collective-permute-start.4) | collective-permute-done | bytes 688160 | tf_op jit(solution)/shard_map/first_expert/ppermute | solution.py:256
  100.9 1.2 collective-permute-start.8
  102.4 14.3 %collective-permute-done.6.refs_7_ = bf16[64,5376]{1,0:T(8,128)(2,1)S(1)} collective-permute-done((bf16[64,5376]{1,0:T(8,128)(2,1)S(1)}, bf16[64,5376]{1,0:T(8,128)(2,1)S(1)}, u32[]{:S(2)}, u32[]{:S(2)}) %collective-permute-start.6) | collective-permute-done | bytes 688160 | tf_op jit(solution)/shard_map/first_expert/ppermute | solution.py:259
  116.7 13.7 %collective-permute-done.8.refs_5_ = bf16[64,5376]{1,0:T(8,128)(2,1)S(1)} collective-permute-done((bf16[64,5376]{1,0:T(8,128)(2,1)S(1)}, bf16[64,5376]{1,0:T(8,128)(2,1)S(1)}, u32[]{:S(2)}, u32[]{:S(2)}) %collective-permute-start.8) | collective-permute-done | bytes 688160 | tf_op jit(solution)/shard_map/first_expert/ppermute | solution.py:263
  130.5 0.8 copy-done.10
  131.5 3.3 %all-to-all-done.1 = bf16[64,2,5376]{2,1,0:T(2,128)(2,1)S(1)} async-done(((bf16[64,2,5376]{2,1,0:T(2,128)(2,1)}), bf16[64,2,5376]{2,1,0:T(2,128)(2,1)S(1)}, u32[]{:S(2)}, u32[]{:S(2)}) %all-to-all-start.1) | async-done | bytes 1376288 | tf_op jit(solution)/shard_map/second_expert/all_to_all | solution.py:253
  135.1 1.5 collective-permute-start.9
  136.7 2.6 collective-permute-start.14
  139.2 4.3 %hidden_grads.2.refs_8_ = f32[512,256]{1,0:T(8,128)} custom-call(bf16[64,5376]{1,0:T(8,128)(2,1)} %copy-done.3, bf16[64,5376]{1,0:T(8,128)(2,1)} %copy-done.2, bf16[64,5376]{1,0:T(8,128)(2,1)} %copy-done.9, bf16[64,5376]{1,0:T(8,128)(2,1)} %copy-done.6, bf16[64,5376]{1,0:T(8,128)(2,1)} %collective-permute-done.7.refs_4_, bf16[64,5376]{1,0:T(8,128)(2,1)} %copy-done.10, ...), custom_call_target="tpu_custom_call" | custom-call | flops 939524096 | bytes 5242880 | tf_op jit(solution)/shard_map/second_expert/hidden_grads/pallas_call | solution.py:116
  143.6 8.2 %collective-permute-done.10.refs_3_ = bf16[64,5376]{1,0:T(8,128)(2,1)S(1)} collective-permute-done((bf16[64,5376]{1,0:T(8,128)(2,1)S(1)}, bf16[64,5376]{1,0:T(8,128)(2,1)S(1)}, u32[]{:S(2)}, u32[]{:S(2)}) %collective-permute-start.10) | collective-permute-done | bytes 688160 | tf_op jit(solution)/shard_map/second_expert/ppermute | solution.py:256
  151.8 1.2 collective-permute-done.9.refs_6_
  153.0 2.7 collective-permute-start.12
  155.7 14.0 %head_products.1.refs_9_ = f32[2,512,512]{2,1,0:T(8,128)} custom-call(s32[1]{0:T(128)} %bitcast.10.first_ref, bf16[64,4,16,1920]{3,2,1,0:T(8,128)(2,1)} %bitcast.42, bf16[2,3584,256]{2,1,0:T(8,128)(2,1)} %gate_ref.5, bf16[2,3584,256]{2,1,0:T(8,128)(2,1)} %up_ref.5), custom_call_target="tpu_custom_call" | custom-call | flops 2113929216 | bytes 20971520 | tf_op jit(solution)/shard_map/second_expert/head_products/pallas_call | solution.py:74
  169.7 4.8 %late_grads.2.h0_ref = bf16[512,512]{1,0:T(8,128)(2,1)} custom-call(bf16[64,5376]{1,0:T(8,128)(2,1)} %copy-done.3, bf16[64,5376]{1,0:T(8,128)(2,1)} %copy-done.2, bf16[64,5376]{1,0:T(8,128)(2,1)} %copy-done.9, bf16[64,5376]{1,0:T(8,128)(2,1)} %copy-done.6, bf16[64,5376]{1,0:T(8,128)(2,1)} %collective-permute-done.7.refs_4_, bf16[64,5376]{1,0:T(8,128)(2,1)} %copy-done.10, ...), custom_call_target="tpu_custom_call" | custom-call | flops 939524096 | bytes 6291456 | tf_op jit(solution)/shard_map/second_expert/late_grads/pallas_call | solution.py:154
  174.6 8.0 %collective-permute-done.11.refs_4_ = bf16[64,5376]{1,0:T(8,128)(2,1)} collective-permute-done((bf16[64,5376]{1,0:T(8,128)(2,1)S(1)}, bf16[64,5376]{1,0:T(8,128)(2,1)}, u32[]{:S(2)}, u32[]{:S(2)}) %collective-permute-start.11) | collective-permute-done | bytes 688160 | tf_op jit(solution)/shard_map/second_expert/ppermute | solution.py:263
  182.6 4.2 %hidden_grads.3.refs_8_ = f32[512,256]{1,0:T(8,128)} custom-call(bf16[64,5376]{1,0:T(8,128)(2,1)} %copy-done.5, bf16[64,5376]{1,0:T(8,128)(2,1)} %copy-done.4, bf16[64,5376]{1,0:T(8,128)(2,1)} %collective-permute-done.14.refs_2_, bf16[64,5376]{1,0:T(8,128)(2,1)} %copy-done.11, bf16[64,5376]{1,0:T(8,128)(2,1)} %collective-permute-done.11.refs_4_, ...), custom_call_target="tpu_custom_call" | custom-call | flops 939524096 | bytes 5242880 | tf_op jit(solution)/shard_map/hidden_grads/pallas_call | solution.py:116
  186.8 4.8 %late_grads.3.h1_ref = bf16[512,512]{1,0:T(8,128)(2,1)} custom-call(bf16[64,5376]{1,0:T(8,128)(2,1)} %copy-done.5, bf16[64,5376]{1,0:T(8,128)(2,1)} %copy-done.4, bf16[64,5376]{1,0:T(8,128)(2,1)} %collective-permute-done.14.refs_2_, bf16[64,5376]{1,0:T(8,128)(2,1)} %copy-done.11, bf16[64,5376]{1,0:T(8,128)(2,1)} %collective-permute-done.11.refs_4_, ...), custom_call_target="tpu_custom_call" | custom-call | flops 939524096 | bytes 6291456 | tf_op jit(solution)/shard_map/late_grads/pallas_call | solution.py:154
  191.6 5.8 %out_rows.3 = (bf16[256,1280]{1,0:T(8,128)(2,1)}, bf16[256,1280]{1,0:T(8,128)(2,1)}, bf16[256,1280]{1,0:T(8,128)(2,1)}, bf16[256,1280]{1,0:T(8,128)(2,1)}) custom-call(bf16[512,512]{1,0:T(8,128)(2,1)} %late_grads.2.h0_ref, bf16[512,512]{1,0:T(8,128)(2,1)} %late_grads.3.h1_ref, bf16[2,3584,256]{2,1,0:T(8,128)(2,1)} %gate_ref.5, bf16[2,3584,256]{2,1,0:T(8,128)(2,1)} %up_ref.5), custom_call_target="tpu_custom_call" | custom-call | flops 1342177280 | bytes 8388608 | tf_op jit(solution)/shard_map/out_rows/pallas_call | solution.py:192
  197.7 1.2 collective-permute-start.15
  198.9 6.7 %out_rows.2 = (bf16[256,2304]{1,0:T(8,128)(2,1)}, bf16[256,2304]{1,0:T(8,128)(2,1)}, bf16[256,2304]{1,0:T(8,128)(2,1)}, bf16[256,2304]{1,0:T(8,128)(2,1)}) custom-call(bf16[512,512]{1,0:T(8,128)(2,1)} %late_grads.2.h0_ref, bf16[512,512]{1,0:T(8,128)(2,1)} %late_grads.3.h1_ref, bf16[2,3584,256]{2,1,0:T(8,128)(2,1)} %gate_ref.5, bf16[2,3584,256]{2,1,0:T(8,128)(2,1)} %up_ref.5), custom_call_target="tpu_custom_call" | custom-call | flops 2415919104 | bytes 8388608 | tf_op jit(solution)/shard_map/out_rows/pallas_call | solution.py:192
  205.6 7.0 %collective-permute-done.18 = bf16[256,1280]{1,0:T(8,128)(2,1)S(1)} collective-permute-done((bf16[256,1280]{1,0:T(8,128)(2,1)}, bf16[256,1280]{1,0:T(8,128)(2,1)S(1)}, u32[]{:S(2)}, u32[]{:S(2)}) %collective-permute-start.18) | collective-permute-done | bytes 655392 | tf_op jit(solution)/shard_map/sum_blocks/ppermute | solution.py:290
  212.6 1.8 collective-permute-start.19
  214.7 15.3 %collective-permute-done.16 = bf16[256,1280]{1,0:T(8,128)(2,1)S(1)} collective-permute-done((bf16[256,1280]{1,0:T(8,128)(2,1)S(1)}, bf16[256,1280]{1,0:T(8,128)(2,1)S(1)}, u32[]{:S(2)}, u32[]{:S(2)}) %collective-permute-start.16) | collective-permute-done | bytes 655392 | tf_op jit(solution)/shard_map/sum_blocks/ppermute | solution.py:291
  230.0 8.3 %collective-permute-done.19 = bf16[256,2304]{1,0:T(8,128)(2,1)S(1)} collective-permute-done((bf16[256,2304]{1,0:T(8,128)(2,1)}, bf16[256,2304]{1,0:T(8,128)(2,1)S(1)}, u32[]{:S(2)}, u32[]{:S(2)}) %collective-permute-start.19) | collective-permute-done | bytes 1179680 | tf_op jit(solution)/shard_map/sum_blocks/ppermute | solution.py:293
  238.5 3.3 %collective-permute-start.20 = (bf16[256,2304]{1,0:T(8,128)(2,1)S(1)}, bf16[256,2304]{1,0:T(8,128)(2,1)}, u32[]{:S(2)}, u32[]{:S(2)}) collective-permute-start(bf16[256,2304]{1,0:T(8,128)(2,1)S(1)} %add_convert_fusion.1), channel_id=1, source_target_pairs={{0,192},{64,0},{128,64},{192,128},{1,193},{65,1},{129,65},{193,129... | collective-permute-start | bytes 3538952 | tf_op jit(solution)/shard_map/sum_blocks/ppermute | solution.py:298
  242.1 1.4 copy.64
  243.5 9.1 %all-to-all-start.3 = ((bf16[64,4,1280]{2,1,0:T(4,128)(2,1)}), bf16[64,4,1280]{2,1,0:T(4,128)(2,1)S(1)}, u32[]{:S(2)}, u32[]{:S(2)}) async-start(bf16[64,4,1280]{2,1,0:T(4,128)(2,1)} %bitcast.41), calls=%async_computation.3 | async-start | bytes 1310720 | tf_op jit(solution)/shard_map/return_slots/all_to_all | solution.py:306
  252.6 3.3 %collective-permute-done.17 = bf16[256,2304]{1,0:T(8,128)(2,1)} collective-permute-done((bf16[256,2304]{1,0:T(8,128)(2,1)}, bf16[256,2304]{1,0:T(8,128)(2,1)}, u32[]{:S(2)}, u32[]{:S(2)}) %collective-permute-start.17) | collective-permute-done | bytes 1179680 | tf_op jit(solution)/shard_map/sum_blocks/ppermute | solution.py:295
  255.9 8.4 %collective-permute-done.20 = bf16[256,2304]{1,0:T(8,128)(2,1)} collective-permute-done((bf16[256,2304]{1,0:T(8,128)(2,1)S(1)}, bf16[256,2304]{1,0:T(8,128)(2,1)}, u32[]{:S(2)}, u32[]{:S(2)}) %collective-permute-start.20) | collective-permute-done | bytes 1179680 | tf_op jit(solution)/shard_map/sum_blocks/ppermute | solution.py:298
  264.4 2.0 add_convert_fusion
  266.4 2.0 copy.63
  268.4 4.4 %all-to-all-done.3 = bf16[64,4,1280]{2,1,0:T(4,128)(2,1)S(1)} async-done(((bf16[64,4,1280]{2,1,0:T(4,128)(2,1)}), bf16[64,4,1280]{2,1,0:T(4,128)(2,1)S(1)}, u32[]{:S(2)}, u32[]{:S(2)}) %all-to-all-start.3) | async-done | bytes 655392 | tf_op jit(solution)/shard_map/return_slots/all_to_all | solution.py:306
  272.7 6.3 %all-to-all-start.2 = ((bf16[64,4,2304]{2,1,0:T(4,128)(2,1)}), bf16[64,4,2304]{2,1,0:T(4,128)(2,1)S(1)}, u32[]{:S(2)}, u32[]{:S(2)}) async-start(bf16[64,4,2304]{2,1,0:T(4,128)(2,1)} %bitcast.40), calls=%async_computation.2 | async-start | bytes 2359296 | tf_op jit(solution)/shard_map/return_slots/all_to_all | solution.py:306
  279.5 30.9 %all-to-all-done.2 = bf16[64,4,2304]{2,1,0:T(4,128)(2,1)S(1)} async-done(((bf16[64,4,2304]{2,1,0:T(4,128)(2,1)}), bf16[64,4,2304]{2,1,0:T(4,128)(2,1)S(1)}, u32[]{:S(2)}, u32[]{:S(2)}) %all-to-all-start.2) | async-done | bytes 1179680 | tf_op jit(solution)/shard_map/return_slots/all_to_all | solution.py:306
  (97 shorter events, 8.1 us)
Async XLA Ops:
  6.5 10.6 %copy-start = (bf16[16,3584]{1,0:T(8,128)(2,1)S(1)}, bf16[16,3584]{1,0:T(8,128)(2,1)}, u32[]{:S(2)}) copy-start(bf16[16,3584]{1,0:T(8,128)(2,1)} %param.8) | copy-start | bytes 344068
  6.5 10.3 %copy-start.18 = (bf16[16,3584]{1,0:T(8,128)(2,1)S(1)}, bf16[16,3584]{1,0:T(8,128)(2,1)}, u32[]{:S(2)}) copy-start(bf16[16,3584]{1,0:T(8,128)(2,1)} %param.7) | copy-start | bytes 344068
  6.5 149.1 %all-gather.2.cloned.1.call-start = ((), (), s32[]{:S(2)}) async-start(), calls=%async_computation.4 | async-start | bytes 15974400 | tf_op jit(solution)/shard_map/gather_tokens/all_gather | solution.py:246
  8.2 10.8 %collective-permute-start.2 = (bf16[16,1920]{1,0:T(8,128)(2,1)S(1)}, bf16[16,1920]{1,0:T(8,128)(2,1)S(1)}, u32[]{:S(2)}, u32[]{:S(2)}) collective-permute-start(bf16[16,1920]{1,0:T(8,128)(2,1)S(1)} %fusion.4), channel_id=1, source_target_pairs={{0,64},{64,128},{128,192},{192,0},{1,65},{65,129},{129,193},{193,1... | collective-permute-start | bytes 184328 | tf_op jit(solution)/shard_map/gather_tokens/ppermute | solution.py:229
  10.3 8.7 %collective-permute-start.1 = (bf16[16,1920]{1,0:T(8,128)(2,1)S(1)}, bf16[16,1920]{1,0:T(8,128)(2,1)S(1)}, u32[]{:S(2)}, u32[]{:S(2)}) collective-permute-start(bf16[16,1920]{1,0:T(8,128)(2,1)S(1)} %fusion.4), channel_id=1, source_target_pairs={{0,128},{64,192},{128,0},{192,64},{1,129},{65,193},{129,1},{193,65... | collective-permute-start | bytes 184328 | tf_op jit(solution)/shard_map/gather_tokens/ppermute | solution.py:229
  12.8 6.3 %collective-permute-start = (bf16[16,1920]{1,0:T(8,128)(2,1)S(1)}, bf16[16,1920]{1,0:T(8,128)(2,1)S(1)}, u32[]{:S(2)}, u32[]{:S(2)}) collective-permute-start(bf16[16,1920]{1,0:T(8,128)(2,1)S(1)} %fusion.4), channel_id=1, source_target_pairs={{0,192},{64,0},{128,64},{192,128},{1,193},{65,1},{129,65},{193,129... | collective-permute-start | bytes 184328 | tf_op jit(solution)/shard_map/gather_tokens/ppermute | solution.py:229
  19.8 58.0 %all-to-all-start = ((bf16[64,2,5376]{2,1,0:T(2,128)(2,1)}), bf16[64,2,5376]{2,1,0:T(2,128)(2,1)S(1)}, u32[]{:S(2)}, u32[]{:S(2)}) async-start(bf16[64,2,5376]{2,1,0:T(2,128)(2,1)} %reshape.116), calls=%async_computation | async-start | bytes 2752512 | tf_op jit(solution)/shard_map/first_expert/all_to_all | solution.py:253
  78.0 7.7 %copy-start.2 = (bf16[64,5376]{1,0:T(8,128)(2,1)}, bf16[64,5376]{1,0:T(8,128)(2,1)S(1)}, u32[]{:S(2)}) copy-start(bf16[64,5376]{1,0:T(8,128)(2,1)S(1)} %get-tuple-element.81.refs_1_) | copy-start | bytes 2064388
  78.0 8.0 %copy-start.3 = (bf16[64,5376]{1,0:T(8,128)(2,1)}, bf16[64,5376]{1,0:T(8,128)(2,1)S(1)}, u32[]{:S(2)}) copy-start(bf16[64,5376]{1,0:T(8,128)(2,1)S(1)} %get-tuple-element.82.refs_0_) | copy-start | bytes 2064388
  78.0 56.7 %all-to-all-start.1 = ((bf16[64,2,5376]{2,1,0:T(2,128)(2,1)}), bf16[64,2,5376]{2,1,0:T(2,128)(2,1)S(1)}, u32[]{:S(2)}, u32[]{:S(2)}) async-start(bf16[64,2,5376]{2,1,0:T(2,128)(2,1)} %reshape.115), calls=%async_computation.1 | async-start | bytes 2752512 | tf_op jit(solution)/shard_map/second_expert/all_to_all | solution.py:253
  84.2 16.7 %collective-permute-start.4 = (bf16[64,5376]{1,0:T(8,128)(2,1)S(1)}, bf16[64,5376]{1,0:T(8,128)(2,1)S(1)}, u32[]{:S(2)}, u32[]{:S(2)}) collective-permute-start(bf16[64,5376]{1,0:T(8,128)(2,1)S(1)} %get-tuple-element.81.refs_1_), channel_id=1, source_target_pairs={{0,192},{64,0},{128,64},{192,128},{1,193},{65,1},{129,65},{193,129... | collective-permute-start | bytes 2064392 | tf_op jit(solution)/shard_map/first_expert/ppermute | solution.py:256
  84.3 17.9 %collective-permute-start.5 = (bf16[64,5376]{1,0:T(8,128)(2,1)S(1)}, bf16[64,5376]{1,0:T(8,128)(2,1)S(1)}, u32[]{:S(2)}, u32[]{:S(2)}) collective-permute-start(bf16[64,5376]{1,0:T(8,128)(2,1)S(1)} %get-tuple-element.82.refs_0_), channel_id=1, source_target_pairs={{0,64},{64,128},{128,192},{192,0},{1,65},{65,129},{129,193},{193,1... | collective-permute-start | bytes 2064392 | tf_op jit(solution)/shard_map/first_expert/ppermute | solution.py:257
  85.7 31.0 %collective-permute-start.6 = (bf16[64,5376]{1,0:T(8,128)(2,1)S(1)}, bf16[64,5376]{1,0:T(8,128)(2,1)S(1)}, u32[]{:S(2)}, u32[]{:S(2)}) collective-permute-start(bf16[64,5376]{1,0:T(8,128)(2,1)S(1)} %get-tuple-element.81.refs_1_), channel_id=1, source_target_pairs={{0,64},{64,128},{128,192},{192,0},{1,65},{65,129},{129,193},{193,1... | collective-permute-start | bytes 2064392 | tf_op jit(solution)/shard_map/first_expert/ppermute | solution.py:259
  86.1 30.7 %collective-permute-start.3 = (bf16[64,5376]{1,0:T(8,128)(2,1)S(1)}, bf16[64,5376]{1,0:T(8,128)(2,1)S(1)}, u32[]{:S(2)}, u32[]{:S(2)}) collective-permute-start(bf16[64,5376]{1,0:T(8,128)(2,1)S(1)} %get-tuple-element.82.refs_0_), channel_id=1, source_target_pairs={{0,192},{64,0},{128,64},{192,128},{1,193},{65,1},{129,65},{193,129... | collective-permute-start | bytes 2064392 | tf_op jit(solution)/shard_map/first_expert/ppermute | solution.py:258
  100.9 33.9 %copy-start.6 = (bf16[64,5376]{1,0:T(8,128)(2,1)}, bf16[64,5376]{1,0:T(8,128)(2,1)S(1)}, u32[]{:S(2)}) copy-start(bf16[64,5376]{1,0:T(8,128)(2,1)S(1)} %collective-permute-done.4.refs_3_) | copy-start | bytes 2064388
  100.9 29.5 %collective-permute-start.8 = (bf16[64,5376]{1,0:T(8,128)(2,1)S(1)}, bf16[64,5376]{1,0:T(8,128)(2,1)S(1)}, u32[]{:S(2)}, u32[]{:S(2)}) collective-permute-start(bf16[64,5376]{1,0:T(8,128)(2,1)S(1)} %collective-permute-done.4.refs_3_), channel_id=1, source_target_pairs={{0,192},{64,0},{128,64},{192,128},{1,193},{65,1},{129,65},{193,129... | collective-permute-start | bytes 2064392 | tf_op jit(solution)/shard_map/first_expert/ppermute | solution.py:263
  102.2 28.2 %copy-start.7 = (bf16[64,5376]{1,0:T(8,128)(2,1)}, bf16[64,5376]{1,0:T(8,128)(2,1)S(1)}, u32[]{:S(2)}) copy-start(bf16[64,5376]{1,0:T(8,128)(2,1)S(1)} %collective-permute-done.5.refs_6_) | copy-start | bytes 2064388
  102.2 29.3 %collective-permute-start.7 = (bf16[64,5376]{1,0:T(8,128)(2,1)S(1)}, bf16[64,5376]{1,0:T(8,128)(2,1)}, u32[]{:S(2)}, u32[]{:S(2)}) collective-permute-start(bf16[64,5376]{1,0:T(8,128)(2,1)S(1)} %collective-permute-done.5.refs_6_), channel_id=1, source_target_pairs={{0,64},{64,128},{128,192},{192,0},{1,65},{65,129},{129,193},{193,1... | collective-permute-start | bytes 2064392 | tf_op jit(solution)/shard_map/first_expert/ppermute | solution.py:263
  116.7 13.7 %copy-start.8 = (bf16[64,5376]{1,0:T(8,128)(2,1)}, bf16[64,5376]{1,0:T(8,128)(2,1)S(1)}, u32[]{:S(2)}) copy-start(bf16[64,5376]{1,0:T(8,128)(2,1)S(1)} %collective-permute-done.6.refs_7_) | copy-start | bytes 2064388
  116.7 13.7 %copy-start.9 = (bf16[64,5376]{1,0:T(8,128)(2,1)}, bf16[64,5376]{1,0:T(8,128)(2,1)S(1)}, u32[]{:S(2)}) copy-start(bf16[64,5376]{1,0:T(8,128)(2,1)S(1)} %collective-permute-done.3.refs_2_) | copy-start | bytes 2064388
  130.4 0.8 copy-start.10
  135.0 8.6 %copy-start.4 = (bf16[64,5376]{1,0:T(8,128)(2,1)}, bf16[64,5376]{1,0:T(8,128)(2,1)S(1)}, u32[]{:S(2)}) copy-start(bf16[64,5376]{1,0:T(8,128)(2,1)S(1)} %get-tuple-element.79.refs_1_) | copy-start | bytes 2064388
  135.0 8.6 %copy-start.5 = (bf16[64,5376]{1,0:T(8,128)(2,1)}, bf16[64,5376]{1,0:T(8,128)(2,1)S(1)}, u32[]{:S(2)}) copy-start(bf16[64,5376]{1,0:T(8,128)(2,1)S(1)} %get-tuple-element.80.refs_0_) | copy-start | bytes 2064388
  135.0 16.8 %collective-permute-start.10 = (bf16[64,5376]{1,0:T(8,128)(2,1)S(1)}, bf16[64,5376]{1,0:T(8,128)(2,1)S(1)}, u32[]{:S(2)}, u32[]{:S(2)}) collective-permute-start(bf16[64,5376]{1,0:T(8,128)(2,1)S(1)} %get-tuple-element.79.refs_1_), channel_id=1, source_target_pairs={{0,192},{64,0},{128,64},{192,128},{1,193},{65,1},{129,65},{193,129... | collective-permute-start | bytes 2064392 | tf_op jit(solution)/shard_map/second_expert/ppermute | solution.py:256
  135.1 17.9 %collective-permute-start.9 = (bf16[64,5376]{1,0:T(8,128)(2,1)S(1)}, bf16[64,5376]{1,0:T(8,128)(2,1)S(1)}, u32[]{:S(2)}, u32[]{:S(2)}) collective-permute-start(bf16[64,5376]{1,0:T(8,128)(2,1)S(1)} %get-tuple-element.80.refs_0_), channel_id=1, source_target_pairs={{0,64},{64,128},{128,192},{192,0},{1,65},{65,129},{129,193},{193,1... | collective-permute-start | bytes 2064392 | tf_op jit(solution)/shard_map/second_expert/ppermute | solution.py:257
  136.6 38.0 %collective-permute-start.13 = (bf16[64,5376]{1,0:T(8,128)(2,1)S(1)}, bf16[64,5376]{1,0:T(8,128)(2,1)S(1)}, u32[]{:S(2)}, u32[]{:S(2)}) collective-permute-start(bf16[64,5376]{1,0:T(8,128)(2,1)S(1)} %get-tuple-element.79.refs_1_), channel_id=1, source_target_pairs={{0,64},{64,128},{128,192},{192,0},{1,65},{65,129},{129,193},{193,1... | collective-permute-start | bytes 2064392 | tf_op jit(solution)/shard_map/second_expert/ppermute | solution.py:259
  136.7 37.9 %collective-permute-start.14 = (bf16[64,5376]{1,0:T(8,128)(2,1)S(1)}, bf16[64,5376]{1,0:T(8,128)(2,1)}, u32[]{:S(2)}, u32[]{:S(2)}) collective-permute-start(bf16[64,5376]{1,0:T(8,128)(2,1)S(1)} %get-tuple-element.80.refs_0_), channel_id=1, source_target_pairs={{0,192},{64,0},{128,64},{192,128},{1,193},{65,1},{129,65},{193,129... | collective-permute-start | bytes 2064392 | tf_op jit(solution)/shard_map/second_expert/ppermute | solution.py:258
  151.8 17.9 %copy-start.11 = (bf16[64,5376]{1,0:T(8,128)(2,1)}, bf16[64,5376]{1,0:T(8,128)(2,1)S(1)}, u32[]{:S(2)}) copy-start(bf16[64,5376]{1,0:T(8,128)(2,1)S(1)} %collective-permute-done.10.refs_3_) | copy-start | bytes 2064388
  153.0 16.7 %copy-start.12 = (bf16[64,5376]{1,0:T(8,128)(2,1)}, bf16[64,5376]{1,0:T(8,128)(2,1)S(1)}, u32[]{:S(2)}) copy-start(bf16[64,5376]{1,0:T(8,128)(2,1)S(1)} %collective-permute-done.9.refs_6_) | copy-start | bytes 2064388
  153.0 29.6 %collective-permute-start.11 = (bf16[64,5376]{1,0:T(8,128)(2,1)S(1)}, bf16[64,5376]{1,0:T(8,128)(2,1)}, u32[]{:S(2)}, u32[]{:S(2)}) collective-permute-start(bf16[64,5376]{1,0:T(8,128)(2,1)S(1)} %collective-permute-done.9.refs_6_), channel_id=1, source_target_pairs={{0,64},{64,128},{128,192},{192,0},{1,65},{65,129},{129,193},{193,1... | collective-permute-start | bytes 2064392 | tf_op jit(solution)/shard_map/second_expert/ppermute | solution.py:263
  153.0 29.6 %collective-permute-start.12 = (bf16[64,5376]{1,0:T(8,128)(2,1)S(1)}, bf16[64,5376]{1,0:T(8,128)(2,1)}, u32[]{:S(2)}, u32[]{:S(2)}) collective-permute-start(bf16[64,5376]{1,0:T(8,128)(2,1)S(1)} %collective-permute-done.10.refs_3_), channel_id=1, source_target_pairs={{0,192},{64,0},{128,64},{192,128},{1,193},{65,1},{129,65},{193,129... | collective-permute-start | bytes 2064392 | tf_op jit(solution)/shard_map/second_expert/ppermute | solution.py:263
  174.5 8.1 %copy-start.13 = (bf16[64,5376]{1,0:T(8,128)(2,1)}, bf16[64,5376]{1,0:T(8,128)(2,1)S(1)}, u32[]{:S(2)}) copy-start(bf16[64,5376]{1,0:T(8,128)(2,1)S(1)} %collective-permute-done.13.refs_7_) | copy-start | bytes 2064388
  197.4 15.2 %collective-permute-start.18 = (bf16[256,1280]{1,0:T(8,128)(2,1)}, bf16[256,1280]{1,0:T(8,128)(2,1)S(1)}, u32[]{:S(2)}, u32[]{:S(2)}) collective-permute-start(bf16[256,1280]{1,0:T(8,128)(2,1)} %get-tuple-element.68), channel_id=1, source_target_pairs={{0,192},{64,0},{128,64},{192,128},{1,193},{65,1},{129,65},{193,129... | collective-permute-start | bytes 1966088 | tf_op jit(solution)/shard_map/sum_blocks/ppermute | solution.py:290
  197.7 16.7 %copy-start.17 = (bf16[256,1280]{1,0:T(8,128)(2,1)S(1)}, bf16[256,1280]{1,0:T(8,128)(2,1)}, u32[]{:S(2)}) copy-start(bf16[256,1280]{1,0:T(8,128)(2,1)} %get-tuple-element.63) | copy-start | bytes 1966084
  197.7 16.7 %collective-permute-start.15 = (bf16[256,1280]{1,0:T(8,128)(2,1)}, bf16[256,1280]{1,0:T(8,128)(2,1)S(1)}, u32[]{:S(2)}, u32[]{:S(2)}) collective-permute-start(bf16[256,1280]{1,0:T(8,128)(2,1)} %get-tuple-element.64), channel_id=1, source_target_pairs={{0,64},{64,128},{128,192},{192,0},{1,65},{65,129},{129,193},{193,1... | collective-permute-start | bytes 1966088 | tf_op jit(solution)/shard_map/sum_blocks/ppermute | solution.py:289
  205.6 32.7 %copy-start.14 = (bf16[256,2304]{1,0:T(8,128)(2,1)S(1)}, bf16[256,2304]{1,0:T(8,128)(2,1)}, u32[]{:S(2)}) copy-start(bf16[256,2304]{1,0:T(8,128)(2,1)} %get-tuple-element.66) | copy-start | bytes 3538948
  212.6 25.6 %collective-permute-start.19 = (bf16[256,2304]{1,0:T(8,128)(2,1)}, bf16[256,2304]{1,0:T(8,128)(2,1)S(1)}, u32[]{:S(2)}, u32[]{:S(2)}) collective-permute-start(bf16[256,2304]{1,0:T(8,128)(2,1)} %get-tuple-element.69), channel_id=1, source_target_pairs={{0,192},{64,0},{128,64},{192,128},{1,193},{65,1},{129,65},{193,129... | collective-permute-start | bytes 3538952 | tf_op jit(solution)/shard_map/sum_blocks/ppermute | solution.py:293
  214.6 15.4 %collective-permute-start.16 = (bf16[256,1280]{1,0:T(8,128)(2,1)S(1)}, bf16[256,1280]{1,0:T(8,128)(2,1)S(1)}, u32[]{:S(2)}, u32[]{:S(2)}) collective-permute-start(bf16[256,1280]{1,0:T(8,128)(2,1)S(1)} %add_convert_fusion.3), channel_id=1, source_target_pairs={{0,64},{64,128},{128,192},{192,0},{1,65},{65,129},{129,193},{193,1... | collective-permute-start | bytes 1966088 | tf_op jit(solution)/shard_map/sum_blocks/ppermute | solution.py:291
  230.0 26.0 %collective-permute-start.17 = (bf16[256,2304]{1,0:T(8,128)(2,1)}, bf16[256,2304]{1,0:T(8,128)(2,1)}, u32[]{:S(2)}, u32[]{:S(2)}) collective-permute-start(bf16[256,2304]{1,0:T(8,128)(2,1)} %get-tuple-element.65), channel_id=1, source_target_pairs={{0,64},{64,128},{128,192},{192,0},{1,65},{65,129},{129,193},{193,1... | collective-permute-start | bytes 3538952 | tf_op jit(solution)/shard_map/sum_blocks/ppermute | solution.py:295
  238.3 3.6 %copy-start.16 = (bf16[256,1280]{1,0:T(8,128)(2,1)S(1)}, bf16[256,1280]{1,0:T(8,128)(2,1)}, u32[]{:S(2)}) copy-start(bf16[256,1280]{1,0:T(8,128)(2,1)} %get-tuple-element.72) | copy-start | bytes 1966084
  238.5 25.8 %collective-permute-start.20 = (bf16[256,2304]{1,0:T(8,128)(2,1)S(1)}, bf16[256,2304]{1,0:T(8,128)(2,1)}, u32[]{:S(2)}, u32[]{:S(2)}) collective-permute-start(bf16[256,2304]{1,0:T(8,128)(2,1)S(1)} %add_convert_fusion.1), channel_id=1, source_target_pairs={{0,192},{64,0},{128,64},{192,128},{1,193},{65,1},{129,65},{193,129... | collective-permute-start | bytes 3538952 | tf_op jit(solution)/shard_map/sum_blocks/ppermute | solution.py:298
  242.1 22.2 %copy-start.15 = (bf16[256,2304]{1,0:T(8,128)(2,1)S(1)}, bf16[256,2304]{1,0:T(8,128)(2,1)}, u32[]{:S(2)}) copy-start(bf16[256,2304]{1,0:T(8,128)(2,1)} %get-tuple-element.61) | copy-start | bytes 3538948
  243.5 29.3 %all-to-all-start.3 = ((bf16[64,4,1280]{2,1,0:T(4,128)(2,1)}), bf16[64,4,1280]{2,1,0:T(4,128)(2,1)S(1)}, u32[]{:S(2)}, u32[]{:S(2)}) async-start(bf16[64,4,1280]{2,1,0:T(4,128)(2,1)} %bitcast.41), calls=%async_computation.3 | async-start | bytes 1310720 | tf_op jit(solution)/shard_map/return_slots/all_to_all | solution.py:306
  272.7 37.7 %all-to-all-start.2 = ((bf16[64,4,2304]{2,1,0:T(4,128)(2,1)}), bf16[64,4,2304]{2,1,0:T(4,128)(2,1)S(1)}, u32[]{:S(2)}, u32[]{:S(2)}) async-start(bf16[64,4,2304]{2,1,0:T(4,128)(2,1)} %bitcast.40), calls=%async_computation.2 | async-start | bytes 2359296 | tf_op jit(solution)/shard_map/return_slots/all_to_all | solution.py:306
  279.3 32.4 %copy-start.1 = (bf16[16,3584]{1,0:T(8,128)(2,1)S(1)}, bf16[16,3584]{1,0:T(8,128)(2,1)}, u32[]{:S(2)}) copy-start(bf16[16,3584]{1,0:T(8,128)(2,1)} %param.8) | copy-start | bytes 344068
Sparse Core Ops, SparseCore 0:
  19.9 135.0 all-gather.1

commit v7 on v6

--- a/solution.py
+++ b/solution.py
@@ -8,10 +8,10 @@
 CAP = 2
 LANES = 128
 BLOCK = 256
-HEAD = 1792
+HEAD = 2048
 STEP = 1792
-TAIL_STEP = 896
-OUT_SPLIT = 2304
+TAIL_STEP = 512
+OUT_SPLIT = 1280
 NT = (((1,), (1,)), ((), ()))
 
 
@@ -28,7 +28,15 @@
     return slots.reshape(experts * CAP, tok_count), slot_scale.reshape(experts * CAP)
 
 
-def head_kernel(first_ref, x_ref, gate_ref, up_ref, out_ref, picked):
+def unit_grads(pre, grad, out_ref):
+    units = grad.shape[1]
+    gate_pre, up_pre = pre[:, :units], pre[:, units:]
+    s = jax.nn.sigmoid(gate_pre)
+    out_ref[:, :units] = (grad * up_pre * s * (1.0 + gate_pre * (1.0 - s))).astype(jnp.bfloat16)
+    out_ref[:, units:] = (grad * gate_pre * s).astype(jnp.bfloat16)
+
+
+def head_kernel(first_ref, x_ref, gate_ref, up_ref, tail_ref, hidden_ref, out_ref, pre_ref, picked):
     group = pl.program_id(0)
     head = gate_ref.shape[1]
     columns, _, tok_count, _ = x_ref.shape
@@ -61,11 +69,17 @@
     def _():
         units = gate_ref.shape[2]
         for e in range(2):
-            out_ref[e, :, :units] = jnp.dot(picked[e], gate_ref[e], preferred_element_type=jnp.float32)
-            out_ref[e, :, units:] = jnp.dot(picked[e], up_ref[e], preferred_element_type=jnp.float32)
-
-
-def head_products(first, x_all, w_gate, w_up):
+            gate_pre = jnp.dot(picked[e], gate_ref[e], preferred_element_type=jnp.float32)
+            up_pre = jnp.dot(picked[e], up_ref[e], preferred_element_type=jnp.float32)
+            if e == 0:
+                pre = tail_ref[...] + jnp.concatenate([gate_pre, up_pre], axis=1)
+                unit_grads(pre, hidden_ref[...], out_ref)
+            else:
+                pre_ref[:, :units] = gate_pre
+                pre_ref[:, units:] = up_pre
+
+
+def head_products(first, x_all, w_gate, w_up, tail, hidden):
     columns, groups, tok_count, wide = x_all.shape
     head = wide - LANES
     local_experts, _, units = w_gate.shape
@@ -73,7 +87,10 @@
     w_spec = pl.BlockSpec((local_experts, head, units), lambda i, first: (0, 0, 0))
     return pl.pallas_call(
         head_kernel,
-        out_shape=jax.ShapeDtypeStruct((local_experts, rows, 2 * units), jnp.float32),
+        out_shape=[
+            jax.ShapeDtypeStruct((rows, 2 * units), jnp.bfloat16),
+            jax.ShapeDtypeStruct((rows, 2 * units), jnp.float32),
+        ],
         grid_spec=pltpu.PrefetchScalarGridSpec(
             num_scalar_prefetch=1,
             grid=(groups,),
@@ -81,8 +98,10 @@
                 pl.BlockSpec((columns, 1, tok_count, wide), lambda i, first: (0, i, 0, 0)),
                 w_spec,
                 w_spec,
+                pl.BlockSpec((rows, 2 * units), lambda i, first: (0, 0)),
+                pl.BlockSpec((rows, units), lambda i, first: (0, 0)),
             ],
-            out_specs=pl.BlockSpec((local_experts, rows, 2 * units), lambda i, first: (0, 0, 0)),
+            out_specs=[pl.BlockSpec((rows, 2 * units), lambda i, first: (0, 0))] * 2,
             scratch_shapes=[pltpu.VMEM((local_experts, rows, head), jnp.bfloat16)],
         ),
         compiler_params=pltpu.CompilerParams(dimension_semantics=("arbitrary",)),
@@ -92,7 +111,7 @@
             transcendentals=0,
         ),
         name="head_products",
-    )(first, x_all, w_gate, w_up)
+    )(first, x_all, w_gate, w_up, tail, hidden)
 
 
 def hidden_kernel(*refs):
@@ -125,6 +144,19 @@
     )(*parts, w_down)
 
 
+def tail_kernel(*refs):
+    *slot_refs, gate_ref, up_ref, pre = refs
+    units = gate_ref.shape[2]
+
+    @pl.when(pl.program_id(0) == 0)
+    def _():
+        pre[...] = jnp.zeros_like(pre)
+
+    rows = jnp.concatenate([ref[...] for ref in slot_refs], axis=0)
+    pre[:, :units] += jnp.dot(rows, gate_ref[0], preferred_element_type=jnp.float32)
+    pre[:, units:] += jnp.dot(rows, up_ref[0], preferred_element_type=jnp.float32)
+
+
 def late_kernel(*refs):
     *slot_refs, hidden_ref, head_ref, gate_ref, up_ref, out_ref, pre = refs
     step = pl.program_id(0)
@@ -132,7 +164,7 @@
 
     @pl.when(step == 0)
     def _():
-        pre[...] = head_ref[0]
+        pre[...] = head_ref[...]
 
     rows = jnp.concatenate([ref[...] for ref in slot_refs], axis=0)
     pre[:, :units] += jnp.dot(rows, gate_ref[0], preferred_element_type=jnp.float32)
@@ -140,34 +172,45 @@
 
     @pl.when(step == pl.num_programs(0) - 1)
     def _():
-        gate_pre, up_pre, grad = pre[:, :units], pre[:, units:], hidden_ref[...]
-        s = jax.nn.sigmoid(gate_pre)
-        out_ref[:, :units] = (grad * up_pre * s * (1.0 + gate_pre * (1.0 - s))).astype(jnp.bfloat16)
-        out_ref[:, units:] = (grad * gate_pre * s).astype(jnp.bfloat16)
+        unit_grads(pre[...], hidden_ref[...], out_ref)
+
+
+def late_specs(e, parts, w_gate):
+    _, width, units = w_gate.shape
+    w_spec = pl.BlockSpec((1, TAIL_STEP, units), lambda k: (e, HEAD // TAIL_STEP + k, 0))
+    rows = sum(part.shape[0] for part in parts)
+    whole = pl.BlockSpec((rows, 2 * units), lambda k: (0, 0))
+    cost = pl.CostEstimate(
+        flops=4 * rows * units * (width - HEAD), bytes_accessed=6 << 20, transcendentals=rows * units
+    )
+    return slot_specs(parts, TAIL_STEP, width // TAIL_STEP), [w_spec, w_spec], whole, cost
+
+
+def tail_products(e, parts, w_gate, w_up):
+    slots, weights, whole, cost = late_specs(e, parts, w_gate)
+    return pl.pallas_call(
+        tail_kernel,
+        out_shape=jax.ShapeDtypeStruct(whole.block_shape, jnp.float32),
+        grid=((w_gate.shape[1] - HEAD) // TAIL_STEP,),
+        in_specs=slots + weights,
+        out_specs=whole,
+        compiler_params=pltpu.CompilerParams(dimension_semantics=("arbitrary",)),
+        cost_estimate=cost,
+        name="tail_products",
+    )(*parts, w_gate, w_up)
 
 
 def late_grads(e, parts, hidden, head_pre, w_gate, w_up):
-    _, width, units = w_gate.shape
-    rows = sum(part.shape[0] for part in parts)
-    wide = width - HEAD
-    w_spec = pl.BlockSpec((1, TAIL_STEP, units), lambda k: (e, HEAD // TAIL_STEP + k, 0))
+    slots, weights, whole, cost = late_specs(e, parts, w_gate)
     return pl.pallas_call(
         late_kernel,
-        out_shape=jax.ShapeDtypeStruct((rows, 2 * units), jnp.bfloat16),
-        grid=(wide // TAIL_STEP,),
-        in_specs=slot_specs(parts, TAIL_STEP, width // TAIL_STEP)
-        + [
-            pl.BlockSpec((rows, units), lambda k: (0, 0)),
-            pl.BlockSpec((1, rows, 2 * units), lambda k: (e, 0, 0)),
-            w_spec,
-            w_spec,
-        ],
-        out_specs=pl.BlockSpec((rows, 2 * units), lambda k: (0, 0)),
-        scratch_shapes=[pltpu.VMEM((rows, 2 * units), jnp.float32)],
-        compiler_params=pltpu.CompilerParams(dimension_semantics=("arbitrary",)),
-        cost_estimate=pl.CostEstimate(
-            flops=4 * rows * units * wide, bytes_accessed=6 << 20, transcendentals=rows * units
-        ),
+        out_shape=jax.ShapeDtypeStruct(whole.block_shape, jnp.bfloat16),
+        grid=((w_gate.shape[1] - HEAD) // TAIL_STEP,),
+        in_specs=slots + [pl.BlockSpec(hidden.shape, lambda k: (0, 0)), whole] + weights,
+        out_specs=whole,
+        scratch_shapes=[pltpu.VMEM(whole.block_shape, jnp.float32)],
+        compiler_params=pltpu.CompilerParams(dimension_semantics=("arbitrary",)),
+        cost_estimate=cost,
         name="late_grads",
     )(*parts, hidden, head_pre, w_gate, w_up)
 
@@ -271,20 +314,20 @@
         got, right, left, far = lax.optimization_barrier((send(slab), right, left, far))
         first_parts = own + right + far + left
         hidden0 = hidden_grads(0, first_parts, w_down)
+        tail0 = tail_products(0, first_parts, w_gate, w_up)
         own = unpack(got)
         right, left = ring(own)
-        left[0], right[1], hidden0 = lax.optimization_barrier((left[0], right[1], hidden0))
+        left[0], right[1], hidden0, tail0 = lax.optimization_barrier((left[0], right[1], hidden0, tail0))
         far = ring_on(left[0], right[1])
-        head_pre = head_products(first, x_all, w_gate, w_up)
-        h = [late_grads(0, first_parts, hidden0, head_pre, w_gate, w_up)]
-        far, left[1], right[0], h[0] = lax.optimization_barrier((far, left[1], right[0], h[0]))
+        h0, head_pre = head_products(first, x_all, w_gate, w_up, tail0, hidden0)
+        far, left[1], right[0], h0 = lax.optimization_barrier((far, left[1], right[0], h0))
         second_parts = own + right + far + left
 
     hidden1 = hidden_grads(1, second_parts, w_down)
-    h.append(late_grads(1, second_parts, hidden1, head_pre, w_gate, w_up))
-
-    own_a, right_a, far_a, left_a = out_rows(h, w_gate, w_up, OUT_SPLIT, width, 256)
-    own_b, right_b, far_b, left_b = out_rows(h, w_gate, w_up, 0, OUT_SPLIT, 768)
+    h = [h0, late_grads(1, second_parts, hidden1, head_pre, w_gate, w_up)]
+
+    own_a, right_a, far_a, left_a = out_rows(h, w_gate, w_up, 0, OUT_SPLIT, 640)
+    own_b, right_b, far_b, left_b = out_rows(h, w_gate, w_up, OUT_SPLIT, width, 256)
     with jax.named_scope("sum_blocks"):
         from_far = lax.ppermute(far_a, "dp", up_ring)
         from_right_a = lax.ppermute(left_a, "dp", down_ring)
@@ -311,7 +354,7 @@
                     preferred_element_type=jnp.float32,
                 ).astype(jnp.bfloat16)
             )
-    return jnp.concatenate(results[::-1], axis=1)
+    return jnp.concatenate(results, axis=1)
 
 
 def solution(mesh):

time: 320 us -> 314 us (0.981)
  waiting for transfers between devices: 182 us -> 171 us
    ppermute x2, waiting for transfers between devices: 20.8 us -> 3.46 us  [ring(): right1 = lax.ppermute(own[1], 'dp', down_ring)]
    ppermute x2, waiting for transfers between devices: 14.3 us -> 0.11 us  [ring(): left1 = lax.ppermute(own[1], 'dp', up_ring)]
    ppermute x2, waiting for transfers between devices: 13.7 us -> 0.01 us  [ring_on(): lax.ppermute(right1, 'dp', down_ring)]
    ppermute x2, waiting for transfers between devices: 1.2 us -> 14.2 us  [ring(): left0 = lax.ppermute(own[0], 'dp', up_ring)]
    ppermute x2, waiting for transfers between devices: 0.01 us -> 11.3 us  [ring(): right0 = lax.ppermute(own[0], 'dp', down_ring)]
    ppermute x2, waiting for transfers between devices: 8.22 us -> 16.6 us  [ring_on(): lax.ppermute(left0, 'dp', up_ring)]
    all_gather x1, waiting for transfers between devices: 0.01 us -> 7.3 us  [on_device(): lax.all_gather(near, 'expert', axis=0, tiled=True)]
  transfers between devices with their start and end apart: 26 -> 26, of which waited for: 16 -> 17; matrix products, arithmetic and copies ran while one was open for 4% -> 5% of each run, Pallas kernels for 9% -> 11%
where the time goes in v7:
time: 314 us; the launch traced here: 313 us
  waiting for transfers between devices  171 us (54%)
  starting transfers between devices  61.5 us (20%)
  Pallas kernels  47.6 us (15%)
  between operations  13.8 us (4%)
  local copies, waits for them, and re-layouts  10.1 us (3%)
  other arithmetic  7.18 us (2%)
    all_to_all x2, waiting for transfers between devices, send(): lax.all_to_all(slab, 'expert', split_axis=0, concat_axis=0, tiled=True)  43.5 us
    all_to_all x2, waiting for transfers between devices, on_device(): lax.all_to_all(back, 'expert', split_axis=0, concat_axis=0, tiled=True)  35.5 us
    all_to_all x2, starting transfers between devices, send(): lax.all_to_all(slab, 'expert', split_axis=0, concat_axis=0, tiled=True)  19.2 us
    ppermute x2, waiting for transfers between devices, ring_on(): lax.ppermute(left0, 'dp', up_ring)  16.6 us
    all_to_all x2, starting transfers between devices, on_device(): lax.all_to_all(back, 'expert', split_axis=0, concat_axis=0, tiled=True)  15.7 us
    pallas_call x1, Pallas kernels, head_products(): pl.pallas_call(head_kernel, out_shape=[jax.ShapeDtypeStruct((rows, 2 * un...  15.5 us
    ppermute x1, waiting for transfers between devices, on_device(): from_left_a = lax.ppermute(total(right_a, from_far), 'dp', up_ring)  15.4 us
    ppermute x2, waiting for transfers between devices, ring(): left0 = lax.ppermute(own[0], 'dp', up_ring)  14.2 us
  transfers between devices with their start and end apart: 26, of which 17 were waited for; matrix products, arithmetic and copies ran while one was open for 5% of the time, Pallas kernels for 11%

profile of v7, /device:TPU:1, one launch (start us, length us, event | category | flops | bytes accessed | tf_op | source)
XLA Modules:
  0.0 313.2 jit_solution(7203144423380107391)
XLA Ops:
  6.5 0.9 slice.36
  8.2 3.4 %collective-permute-start = (bf16[16,2176]{1,0:T(8,128)(2,1)S(1)}, bf16[16,2176]{1,0:T(8,128)(2,1)S(1)}, u32[]{:S(2)}, u32[]{:S(2)}) collective-permute-start(bf16[16,2176]{1,0:T(8,128)(2,1)S(1)} %fusion.3), channel_id=1, source_target_pairs={{0,192},{64,0},{128,64},{192,128},{1,193},{65,1},{129,65},{193,129... | collective-permute-start | bytes 208904 | tf_op jit(solution)/shard_map/gather_tokens/ppermute | solution.py:272
  12.8 0.8 fusion.4
  13.9 0.8 select_reduce_fusion.1
  16.5 1.4 reshape.116
  18.6 13.2 %all-to-all-start = ((bf16[64,2,5120]{2,1,0:T(2,128)(2,1)}), bf16[64,2,5120]{2,1,0:T(2,128)(2,1)S(1)}, u32[]{:S(2)}, u32[]{:S(2)}) async-start(bf16[64,2,5120]{2,1,0:T(2,128)(2,1)} %reshape.116), calls=%async_computation | async-start | bytes 2621440 | tf_op jit(solution)/shard_map/first_expert/all_to_all | solution.py:296
  32.8 1.4 reshape.115
  34.1 42.3 %all-to-all-done = bf16[64,2,5120]{2,1,0:T(2,128)(2,1)S(1)} async-done(((bf16[64,2,5120]{2,1,0:T(2,128)(2,1)}), bf16[64,2,5120]{2,1,0:T(2,128)(2,1)S(1)}, u32[]{:S(2)}, u32[]{:S(2)}) %all-to-all-start) | async-done | bytes 1310752 | tf_op jit(solution)/shard_map/first_expert/all_to_all | solution.py:296
  76.8 6.0 %all-to-all-start.1 = ((bf16[64,2,5120]{2,1,0:T(2,128)(2,1)}), bf16[64,2,5120]{2,1,0:T(2,128)(2,1)S(1)}, u32[]{:S(2)}, u32[]{:S(2)}) async-start(bf16[64,2,5120]{2,1,0:T(2,128)(2,1)} %reshape.115), calls=%async_computation.1 | async-start | bytes 2621440 | tf_op jit(solution)/shard_map/second_expert/all_to_all | solution.py:296
  82.8 1.5 collective-permute-start.5
  84.3 1.3 collective-permute-start.4
  86.2 0.8 collective-permute-start.6
  87.0 13.0 %collective-permute-done.5.refs_6_ = bf16[64,5120]{1,0:T(8,128)(2,1)S(1)} collective-permute-done((bf16[64,5120]{1,0:T(8,128)(2,1)S(1)}, bf16[64,5120]{1,0:T(8,128)(2,1)S(1)}, u32[]{:S(2)}, u32[]{:S(2)}) %collective-permute-start.5) | collective-permute-done | bytes 655392 | tf_op jit(solution)/shard_map/first_expert/ppermute | solution.py:300
  100.3 2.5 collective-permute-start.8
  102.8 11.2 %collective-permute-done.3.refs_2_ = bf16[64,5120]{1,0:T(8,128)(2,1)S(1)} collective-permute-done((bf16[64,5120]{1,0:T(8,128)(2,1)S(1)}, bf16[64,5120]{1,0:T(8,128)(2,1)S(1)}, u32[]{:S(2)}, u32[]{:S(2)}) %collective-permute-start.3) | collective-permute-done | bytes 655392 | tf_op jit(solution)/shard_map/first_expert/ppermute | solution.py:301
  114.1 14.0 %collective-permute-done.7.refs_4_ = bf16[64,5120]{1,0:T(8,128)(2,1)S(1)} collective-permute-done((bf16[64,5120]{1,0:T(8,128)(2,1)S(1)}, bf16[64,5120]{1,0:T(8,128)(2,1)S(1)}, u32[]{:S(2)}, u32[]{:S(2)}) %collective-permute-start.7) | collective-permute-done | bytes 655392 | tf_op jit(solution)/shard_map/first_expert/ppermute | solution.py:306
  128.2 0.8 copy-done.13
  129.0 1.2 all-to-all-done.1
  130.6 1.4 collective-permute-start.10
  132.4 1.4 collective-permute-start.13
  133.8 1.3 collective-permute-start.14
  135.1 4.5 %tail_products.1.tail_ref = f32[512,512]{1,0:T(8,128)} custom-call(bf16[64,5120]{1,0:T(8,128)(2,1)} %copy-done.5, bf16[64,5120]{1,0:T(8,128)(2,1)} %copy-done.4, bf16[64,5120]{1,0:T(8,128)(2,1)} %copy-done.11, bf16[64,5120]{1,0:T(8,128)(2,1)} %copy-done.10, bf16[64,5120]{1,0:T(8,128)(2,1)} %copy-done.13, bf16[64,5120]{1,0:T(8,128)(2,1)} %collective-permute-done.8.refs_5_, ...), custom_call_target="tpu_custom_call" | custom-call | flops 805306368 | bytes 6291456 | tf_op jit(solution)/shard_map/second_expert/tail_products/pallas_call | solution.py:191
  139.7 4.4 %hidden_grads.2.hidden_ref = f32[512,256]{1,0:T(8,128)} custom-call(bf16[64,5120]{1,0:T(8,128)(2,1)} %copy-done.5, bf16[64,5120]{1,0:T(8,128)(2,1)} %copy-done.4, bf16[64,5120]{1,0:T(8,128)(2,1)} %copy-done.11, bf16[64,5120]{1,0:T(8,128)(2,1)} %copy-done.10, bf16[64,5120]{1,0:T(8,128)(2,1)} %copy-done.13, bf16[64,5120]{1,0:T(8,128)(2,1)} %collective-permute-done.8.refs_5_, ...), custom_call_target="tpu_custom_call" | custom-call | flops 939524096 | bytes 5242880 | tf_op jit(solution)/shard_map/second_expert/hidden_grads/pallas_call | solution.py:135
  144.0 3.5 %collective-permute-done.10.refs_3_ = bf16[64,5120]{1,0:T(8,128)(2,1)S(1)} collective-permute-done((bf16[64,5120]{1,0:T(8,128)(2,1)S(1)}, bf16[64,5120]{1,0:T(8,128)(2,1)S(1)}, u32[]{:S(2)}, u32[]{:S(2)}) %collective-permute-start.10) | collective-permute-done | bytes 655392 | tf_op jit(solution)/shard_map/second_expert/ppermute | solution.py:299
  147.5 1.2 collective-permute-done.9.refs_6_
  149.2 2.2 collective-permute-start.12
  151.4 7.3 %all-gather.2.cloned.1.call-done = bf16[4096,2176]{1,0:T(8,128)(2,1)} async-done(((bf16[64,2176]{1,0:T(8,128)(2,1)}), bf16[4096,2176]{1,0:T(8,128)(2,1)}) %all-gather.2.cloned.1.call-update) | async-done | bytes 17825808 | tf_op jit(solution)/shard_map/gather_tokens/all_gather | solution.py:289
  158.7 15.5 %head_products.1 = (bf16[512,512]{1,0:T(8,128)(2,1)}, f32[512,512]{1,0:T(8,128)}) custom-call(s32[1]{0:T(128)} %bitcast.10.first_ref, bf16[64,4,16,2176]{3,2,1,0:T(8,128)(2,1)} %bitcast.42, bf16[2,3584,256]{2,1,0:T(8,128)(2,1)} %gate_ref.5, bf16[2,3584,256]{2,1,0:T(8,128)(2,1)} %up_ref.5, f32[512,512]{1,0:T(8,128)} %tail_products.1.tail_ref, ...), custom_call_target="tpu_custom_call" | custom-call | flops 2415919104 | bytes 20971520 | tf_op jit(solution)/shard_map/second_expert/head_products/pallas_call | solution.py:88
  174.2 2.5 collective-permute-done.11.refs_4_
  176.8 4.3 %hidden_grads.3.refs_8_ = f32[512,256]{1,0:T(8,128)} custom-call(bf16[64,5120]{1,0:T(8,128)(2,1)} %copy-done.3, bf16[64,5120]{1,0:T(8,128)(2,1)} %copy-done.2, bf16[64,5120]{1,0:T(8,128)(2,1)} %collective-permute-done.14.refs_2_, bf16[64,5120]{1,0:T(8,128)(2,1)} %copy-done.6, bf16[64,5120]{1,0:T(8,128)(2,1)} %collective-permute-done.11.refs_4_, ...), custom_call_target="tpu_custom_call" | custom-call | flops 939524096 | bytes 5242880 | tf_op jit(solution)/shard_map/hidden_grads/pallas_call | solution.py:135
  181.1 5.2 %late_grads.1.h1_ref = bf16[512,512]{1,0:T(8,128)(2,1)} custom-call(bf16[64,5120]{1,0:T(8,128)(2,1)} %copy-done.3, bf16[64,5120]{1,0:T(8,128)(2,1)} %copy-done.2, bf16[64,5120]{1,0:T(8,128)(2,1)} %collective-permute-done.14.refs_2_, bf16[64,5120]{1,0:T(8,128)(2,1)} %copy-done.6, bf16[64,5120]{1,0:T(8,128)(2,1)} %collective-permute-done.11.refs_4_, ...), custom_call_target="tpu_custom_call" | custom-call | flops 805306368 | bytes 6291456 | tf_op jit(solution)/shard_map/late_grads/pallas_call | solution.py:205
  186.3 4.7 %out_rows.2 = (bf16[256,1280]{1,0:T(8,128)(2,1)}, bf16[256,1280]{1,0:T(8,128)(2,1)}, bf16[256,1280]{1,0:T(8,128)(2,1)}, bf16[256,1280]{1,0:T(8,128)(2,1)}) custom-call(bf16[512,512]{1,0:T(8,128)(2,1)} %get-tuple-element.61.h0_ref, bf16[512,512]{1,0:T(8,128)(2,1)} %late_grads.1.h1_ref, bf16[2,3584,256]{2,1,0:T(8,128)(2,1)} %gate_ref.5, ...), custom_call_target="tpu_custom_call" | custom-call | flops 1342177280 | bytes 8388608 | tf_op jit(solution)/shard_map/out_rows/pallas_call | solution.py:235
  191.0 0.9 collective-permute-start.15
  192.4 9.0 %out_rows.3 = (bf16[256,2304]{1,0:T(8,128)(2,1)}, bf16[256,2304]{1,0:T(8,128)(2,1)}, bf16[256,2304]{1,0:T(8,128)(2,1)}, bf16[256,2304]{1,0:T(8,128)(2,1)}) custom-call(bf16[512,512]{1,0:T(8,128)(2,1)} %get-tuple-element.61.h0_ref, bf16[512,512]{1,0:T(8,128)(2,1)} %late_grads.1.h1_ref, bf16[2,3584,256]{2,1,0:T(8,128)(2,1)} %gate_ref.5, ...), custom_call_target="tpu_custom_call" | custom-call | flops 2415919104 | bytes 8388608 | tf_op jit(solution)/shard_map/out_rows/pallas_call | solution.py:235
  201.5 4.2 %collective-permute-done.15 = bf16[256,1280]{1,0:T(8,128)(2,1)S(1)} collective-permute-done((bf16[256,1280]{1,0:T(8,128)(2,1)}, bf16[256,1280]{1,0:T(8,128)(2,1)S(1)}, u32[]{:S(2)}, u32[]{:S(2)}) %collective-permute-start.15) | collective-permute-done | bytes 655392 | tf_op jit(solution)/shard_map/sum_blocks/ppermute | solution.py:333
  205.6 3.1 collective-permute-start.16
  209.0 15.4 %collective-permute-done.18 = bf16[256,1280]{1,0:T(8,128)(2,1)S(1)} collective-permute-done((bf16[256,1280]{1,0:T(8,128)(2,1)S(1)}, bf16[256,1280]{1,0:T(8,128)(2,1)S(1)}, u32[]{:S(2)}, u32[]{:S(2)}) %collective-permute-start.18) | collective-permute-done | bytes 655392 | tf_op jit(solution)/shard_map/sum_blocks/ppermute | solution.py:334
  224.4 8.2 %collective-permute-done.16 = bf16[256,2304]{1,0:T(8,128)(2,1)S(1)} collective-permute-done((bf16[256,2304]{1,0:T(8,128)(2,1)}, bf16[256,2304]{1,0:T(8,128)(2,1)S(1)}, u32[]{:S(2)}, u32[]{:S(2)}) %collective-permute-start.16) | collective-permute-done | bytes 1179680 | tf_op jit(solution)/shard_map/sum_blocks/ppermute | solution.py:336
  232.9 3.4 %collective-permute-start.20 = (bf16[256,2304]{1,0:T(8,128)(2,1)S(1)}, bf16[256,2304]{1,0:T(8,128)(2,1)}, u32[]{:S(2)}, u32[]{:S(2)}) collective-permute-start(bf16[256,2304]{1,0:T(8,128)(2,1)S(1)} %add_convert_fusion.1), channel_id=1, source_target_pairs={{0,192},{64,0},{128,64},{192,128},{1,193},{65,1},{129,65},{193,129... | collective-permute-start | bytes 3538952 | tf_op jit(solution)/shard_map/sum_blocks/ppermute | solution.py:341
  236.6 1.4 copy.64
  237.9 9.4 %all-to-all-start.2 = ((bf16[64,4,1280]{2,1,0:T(4,128)(2,1)}), bf16[64,4,1280]{2,1,0:T(4,128)(2,1)S(1)}, u32[]{:S(2)}, u32[]{:S(2)}) async-start(bf16[64,4,1280]{2,1,0:T(4,128)(2,1)} %bitcast.41), calls=%async_computation.2 | async-start | bytes 1310720 | tf_op jit(solution)/shard_map/return_slots/all_to_all | solution.py:349
  247.4 3.1 collective-permute-done.19
  250.5 8.4 %collective-permute-done.20 = bf16[256,2304]{1,0:T(8,128)(2,1)} collective-permute-done((bf16[256,2304]{1,0:T(8,128)(2,1)S(1)}, bf16[256,2304]{1,0:T(8,128)(2,1)}, u32[]{:S(2)}, u32[]{:S(2)}) %collective-permute-start.20) | collective-permute-done | bytes 1179680 | tf_op jit(solution)/shard_map/sum_blocks/ppermute | solution.py:341
  258.9 2.0 add_convert_fusion
  260.9 1.9 copy.63
  262.9 4.6 %all-to-all-done.2 = bf16[64,4,1280]{2,1,0:T(4,128)(2,1)S(1)} async-done(((bf16[64,4,1280]{2,1,0:T(4,128)(2,1)}), bf16[64,4,1280]{2,1,0:T(4,128)(2,1)S(1)}, u32[]{:S(2)}, u32[]{:S(2)}) %all-to-all-start.2) | async-done | bytes 655392 | tf_op jit(solution)/shard_map/return_slots/all_to_all | solution.py:349
  267.5 6.3 %all-to-all-start.3 = ((bf16[64,4,2304]{2,1,0:T(4,128)(2,1)}), bf16[64,4,2304]{2,1,0:T(4,128)(2,1)S(1)}, u32[]{:S(2)}, u32[]{:S(2)}) async-start(bf16[64,4,2304]{2,1,0:T(4,128)(2,1)} %bitcast.40), calls=%async_computation.3 | async-start | bytes 2359296 | tf_op jit(solution)/shard_map/return_slots/all_to_all | solution.py:349
  274.2 30.9 %all-to-all-done.3 = bf16[64,4,2304]{2,1,0:T(4,128)(2,1)S(1)} async-done(((bf16[64,4,2304]{2,1,0:T(4,128)(2,1)}), bf16[64,4,2304]{2,1,0:T(4,128)(2,1)S(1)}, u32[]{:S(2)}, u32[]{:S(2)}) %all-to-all-start.3) | async-done | bytes 1179680 | tf_op jit(solution)/shard_map/return_slots/all_to_all | solution.py:349
  (97 shorter events, 11.4 us)
Async XLA Ops:
  6.5 9.4 %copy-start = (bf16[16,3584]{1,0:T(8,128)(2,1)S(1)}, bf16[16,3584]{1,0:T(8,128)(2,1)}, u32[]{:S(2)}) copy-start(bf16[16,3584]{1,0:T(8,128)(2,1)} %param.8) | copy-start | bytes 344068
  6.5 9.2 %copy-start.18 = (bf16[16,3584]{1,0:T(8,128)(2,1)S(1)}, bf16[16,3584]{1,0:T(8,128)(2,1)}, u32[]{:S(2)}) copy-start(bf16[16,3584]{1,0:T(8,128)(2,1)} %param.7) | copy-start | bytes 344068
  6.5 152.1 %all-gather.2.cloned.1.call-start = ((), (), s32[]{:S(2)}) async-start(), calls=%async_computation.4 | async-start | bytes 18104320 | tf_op jit(solution)/shard_map/gather_tokens/all_gather | solution.py:289
  8.2 9.6 %collective-permute-start = (bf16[16,2176]{1,0:T(8,128)(2,1)S(1)}, bf16[16,2176]{1,0:T(8,128)(2,1)S(1)}, u32[]{:S(2)}, u32[]{:S(2)}) collective-permute-start(bf16[16,2176]{1,0:T(8,128)(2,1)S(1)} %fusion.3), channel_id=1, source_target_pairs={{0,192},{64,0},{128,64},{192,128},{1,193},{65,1},{129,65},{193,129... | collective-permute-start | bytes 208904 | tf_op jit(solution)/shard_map/gather_tokens/ppermute | solution.py:272
  11.6 6.2 %collective-permute-start.1 = (bf16[16,2176]{1,0:T(8,128)(2,1)S(1)}, bf16[16,2176]{1,0:T(8,128)(2,1)S(1)}, u32[]{:S(2)}, u32[]{:S(2)}) collective-permute-start(bf16[16,2176]{1,0:T(8,128)(2,1)S(1)} %fusion.3), channel_id=1, source_target_pairs={{0,128},{64,192},{128,0},{192,64},{1,129},{65,193},{129,1},{193,65... | collective-permute-start | bytes 208904 | tf_op jit(solution)/shard_map/gather_tokens/ppermute | solution.py:272
  12.1 5.7 %collective-permute-start.2 = (bf16[16,2176]{1,0:T(8,128)(2,1)S(1)}, bf16[16,2176]{1,0:T(8,128)(2,1)S(1)}, u32[]{:S(2)}, u32[]{:S(2)}) collective-permute-start(bf16[16,2176]{1,0:T(8,128)(2,1)S(1)} %fusion.3), channel_id=1, source_target_pairs={{0,64},{64,128},{128,192},{192,0},{1,65},{65,129},{129,193},{193,1... | collective-permute-start | bytes 208904 | tf_op jit(solution)/shard_map/gather_tokens/ppermute | solution.py:272
  18.6 57.8 %all-to-all-start = ((bf16[64,2,5120]{2,1,0:T(2,128)(2,1)}), bf16[64,2,5120]{2,1,0:T(2,128)(2,1)S(1)}, u32[]{:S(2)}, u32[]{:S(2)}) async-start(bf16[64,2,5120]{2,1,0:T(2,128)(2,1)} %reshape.116), calls=%async_computation | async-start | bytes 2621440 | tf_op jit(solution)/shard_map/first_expert/all_to_all | solution.py:296
  76.8 8.8 %copy-start.5 = (bf16[64,5120]{1,0:T(8,128)(2,1)}, bf16[64,5120]{1,0:T(8,128)(2,1)S(1)}, u32[]{:S(2)}) copy-start(bf16[64,5120]{1,0:T(8,128)(2,1)S(1)} %get-tuple-element.88.refs_0_) | copy-start | bytes 1966084
  76.8 9.4 %copy-start.4 = (bf16[64,5120]{1,0:T(8,128)(2,1)}, bf16[64,5120]{1,0:T(8,128)(2,1)S(1)}, u32[]{:S(2)}) copy-start(bf16[64,5120]{1,0:T(8,128)(2,1)S(1)} %get-tuple-element.87.refs_1_) | copy-start | bytes 1966084
  76.8 53.4 %all-to-all-start.1 = ((bf16[64,2,5120]{2,1,0:T(2,128)(2,1)}), bf16[64,2,5120]{2,1,0:T(2,128)(2,1)S(1)}, u32[]{:S(2)}, u32[]{:S(2)}) async-start(bf16[64,2,5120]{2,1,0:T(2,128)(2,1)} %reshape.115), calls=%async_computation.1 | async-start | bytes 2621440 | tf_op jit(solution)/shard_map/second_expert/all_to_all | solution.py:296
  82.8 17.2 %collective-permute-start.5 = (bf16[64,5120]{1,0:T(8,128)(2,1)S(1)}, bf16[64,5120]{1,0:T(8,128)(2,1)S(1)}, u32[]{:S(2)}, u32[]{:S(2)}) collective-permute-start(bf16[64,5120]{1,0:T(8,128)(2,1)S(1)} %get-tuple-element.88.refs_0_), channel_id=1, source_target_pairs={{0,64},{64,128},{128,192},{192,0},{1,65},{65,129},{129,193},{193,1... | collective-permute-start | bytes 1966088 | tf_op jit(solution)/shard_map/first_expert/ppermute | solution.py:300
  84.3 16.0 %collective-permute-start.4 = (bf16[64,5120]{1,0:T(8,128)(2,1)S(1)}, bf16[64,5120]{1,0:T(8,128)(2,1)S(1)}, u32[]{:S(2)}, u32[]{:S(2)}) collective-permute-start(bf16[64,5120]{1,0:T(8,128)(2,1)S(1)} %get-tuple-element.87.refs_1_), channel_id=1, source_target_pairs={{0,192},{64,0},{128,64},{192,128},{1,193},{65,1},{129,65},{193,129... | collective-permute-start | bytes 1966088 | tf_op jit(solution)/shard_map/first_expert/ppermute | solution.py:299
  85.6 28.4 %collective-permute-start.3 = (bf16[64,5120]{1,0:T(8,128)(2,1)S(1)}, bf16[64,5120]{1,0:T(8,128)(2,1)S(1)}, u32[]{:S(2)}, u32[]{:S(2)}) collective-permute-start(bf16[64,5120]{1,0:T(8,128)(2,1)S(1)} %get-tuple-element.88.refs_0_), channel_id=1, source_target_pairs={{0,192},{64,0},{128,64},{192,128},{1,193},{65,1},{129,65},{193,129... | collective-permute-start | bytes 1966088 | tf_op jit(solution)/shard_map/first_expert/ppermute | solution.py:301
  86.2 27.9 %collective-permute-start.6 = (bf16[64,5120]{1,0:T(8,128)(2,1)S(1)}, bf16[64,5120]{1,0:T(8,128)(2,1)S(1)}, u32[]{:S(2)}, u32[]{:S(2)}) collective-permute-start(bf16[64,5120]{1,0:T(8,128)(2,1)S(1)} %get-tuple-element.87.refs_1_), channel_id=1, source_target_pairs={{0,64},{64,128},{128,192},{192,0},{1,65},{65,129},{129,193},{193,1... | collective-permute-start | bytes 1966088 | tf_op jit(solution)/shard_map/first_expert/ppermute | solution.py:302
  100.1 28.1 %copy-start.9 = (bf16[64,5120]{1,0:T(8,128)(2,1)}, bf16[64,5120]{1,0:T(8,128)(2,1)S(1)}, u32[]{:S(2)}) copy-start(bf16[64,5120]{1,0:T(8,128)(2,1)S(1)} %collective-permute-done.5.refs_6_) | copy-start | bytes 1966084
  100.1 28.1 %collective-permute-start.7 = (bf16[64,5120]{1,0:T(8,128)(2,1)S(1)}, bf16[64,5120]{1,0:T(8,128)(2,1)S(1)}, u32[]{:S(2)}, u32[]{:S(2)}) collective-permute-start(bf16[64,5120]{1,0:T(8,128)(2,1)S(1)} %collective-permute-done.5.refs_6_), channel_id=1, source_target_pairs={{0,64},{64,128},{128,192},{192,0},{1,65},{65,129},{129,193},{193,1... | collective-permute-start | bytes 1966088 | tf_op jit(solution)/shard_map/first_expert/ppermute | solution.py:306
  100.3 27.9 %copy-start.10 = (bf16[64,5120]{1,0:T(8,128)(2,1)}, bf16[64,5120]{1,0:T(8,128)(2,1)S(1)}, u32[]{:S(2)}) copy-start(bf16[64,5120]{1,0:T(8,128)(2,1)S(1)} %collective-permute-done.4.refs_3_) | copy-start | bytes 1966084
  100.3 28.7 %collective-permute-start.8 = (bf16[64,5120]{1,0:T(8,128)(2,1)S(1)}, bf16[64,5120]{1,0:T(8,128)(2,1)}, u32[]{:S(2)}, u32[]{:S(2)}) collective-permute-start(bf16[64,5120]{1,0:T(8,128)(2,1)S(1)} %collective-permute-done.4.refs_3_), channel_id=1, source_target_pairs={{0,192},{64,0},{128,64},{192,128},{1,193},{65,1},{129,65},{193,129... | collective-permute-start | bytes 1966088 | tf_op jit(solution)/shard_map/first_expert/ppermute | solution.py:306
  114.0 14.2 %copy-start.11 = (bf16[64,5120]{1,0:T(8,128)(2,1)}, bf16[64,5120]{1,0:T(8,128)(2,1)S(1)}, u32[]{:S(2)}) copy-start(bf16[64,5120]{1,0:T(8,128)(2,1)S(1)} %collective-permute-done.3.refs_2_) | copy-start | bytes 1966084
  114.1 14.1 %copy-start.12 = (bf16[64,5120]{1,0:T(8,128)(2,1)}, bf16[64,5120]{1,0:T(8,128)(2,1)S(1)}, u32[]{:S(2)}) copy-start(bf16[64,5120]{1,0:T(8,128)(2,1)S(1)} %collective-permute-done.6.refs_7_) | copy-start | bytes 1966084
  128.2 0.9 copy-start.13
  130.6 9.1 %copy-start.2 = (bf16[64,5120]{1,0:T(8,128)(2,1)}, bf16[64,5120]{1,0:T(8,128)(2,1)S(1)}, u32[]{:S(2)}) copy-start(bf16[64,5120]{1,0:T(8,128)(2,1)S(1)} %get-tuple-element.85.refs_1_) | copy-start | bytes 1966084
  130.6 9.1 %copy-start.3 = (bf16[64,5120]{1,0:T(8,128)(2,1)}, bf16[64,5120]{1,0:T(8,128)(2,1)S(1)}, u32[]{:S(2)}) copy-start(bf16[64,5120]{1,0:T(8,128)(2,1)S(1)} %get-tuple-element.86.refs_0_) | copy-start | bytes 1966084
  130.6 16.9 %collective-permute-start.10 = (bf16[64,5120]{1,0:T(8,128)(2,1)S(1)}, bf16[64,5120]{1,0:T(8,128)(2,1)S(1)}, u32[]{:S(2)}, u32[]{:S(2)}) collective-permute-start(bf16[64,5120]{1,0:T(8,128)(2,1)S(1)} %get-tuple-element.85.refs_1_), channel_id=1, source_target_pairs={{0,192},{64,0},{128,64},{192,128},{1,193},{65,1},{129,65},{193,129... | collective-permute-start | bytes 1966088 | tf_op jit(solution)/shard_map/second_expert/ppermute | solution.py:299
  132.0 16.7 %collective-permute-start.9 = (bf16[64,5120]{1,0:T(8,128)(2,1)S(1)}, bf16[64,5120]{1,0:T(8,128)(2,1)S(1)}, u32[]{:S(2)}, u32[]{:S(2)}) collective-permute-start(bf16[64,5120]{1,0:T(8,128)(2,1)S(1)} %get-tuple-element.86.refs_0_), channel_id=1, source_target_pairs={{0,64},{64,128},{128,192},{192,0},{1,65},{65,129},{129,193},{193,1... | collective-permute-start | bytes 1966088 | tf_op jit(solution)/shard_map/second_expert/ppermute | solution.py:300
  132.4 41.8 %collective-permute-start.13 = (bf16[64,5120]{1,0:T(8,128)(2,1)S(1)}, bf16[64,5120]{1,0:T(8,128)(2,1)S(1)}, u32[]{:S(2)}, u32[]{:S(2)}) collective-permute-start(bf16[64,5120]{1,0:T(8,128)(2,1)S(1)} %get-tuple-element.85.refs_1_), channel_id=1, source_target_pairs={{0,64},{64,128},{128,192},{192,0},{1,65},{65,129},{129,193},{193,1... | collective-permute-start | bytes 1966088 | tf_op jit(solution)/shard_map/second_expert/ppermute | solution.py:302
  133.8 40.4 %collective-permute-start.14 = (bf16[64,5120]{1,0:T(8,128)(2,1)S(1)}, bf16[64,5120]{1,0:T(8,128)(2,1)}, u32[]{:S(2)}, u32[]{:S(2)}) collective-permute-start(bf16[64,5120]{1,0:T(8,128)(2,1)S(1)} %get-tuple-element.86.refs_0_), channel_id=1, source_target_pairs={{0,192},{64,0},{128,64},{192,128},{1,193},{65,1},{129,65},{193,129... | collective-permute-start | bytes 1966088 | tf_op jit(solution)/shard_map/second_expert/ppermute | solution.py:301
  147.5 26.7 %copy-start.6 = (bf16[64,5120]{1,0:T(8,128)(2,1)}, bf16[64,5120]{1,0:T(8,128)(2,1)S(1)}, u32[]{:S(2)}) copy-start(bf16[64,5120]{1,0:T(8,128)(2,1)S(1)} %collective-permute-done.10.refs_3_) | copy-start | bytes 1966084
  148.7 25.5 %copy-start.7 = (bf16[64,5120]{1,0:T(8,128)(2,1)}, bf16[64,5120]{1,0:T(8,128)(2,1)S(1)}, u32[]{:S(2)}) copy-start(bf16[64,5120]{1,0:T(8,128)(2,1)S(1)} %collective-permute-done.9.refs_6_) | copy-start | bytes 1966084
  148.7 28.1 %collective-permute-start.11 = (bf16[64,5120]{1,0:T(8,128)(2,1)S(1)}, bf16[64,5120]{1,0:T(8,128)(2,1)}, u32[]{:S(2)}, u32[]{:S(2)}) collective-permute-start(bf16[64,5120]{1,0:T(8,128)(2,1)S(1)} %collective-permute-done.9.refs_6_), channel_id=1, source_target_pairs={{0,64},{64,128},{128,192},{192,0},{1,65},{65,129},{129,193},{193,1... | collective-permute-start | bytes 1966088 | tf_op jit(solution)/shard_map/second_expert/ppermute | solution.py:306
  149.2 27.6 %collective-permute-start.12 = (bf16[64,5120]{1,0:T(8,128)(2,1)S(1)}, bf16[64,5120]{1,0:T(8,128)(2,1)}, u32[]{:S(2)}, u32[]{:S(2)}) collective-permute-start(bf16[64,5120]{1,0:T(8,128)(2,1)S(1)} %collective-permute-done.10.refs_3_), channel_id=1, source_target_pairs={{0,192},{64,0},{128,64},{192,128},{1,193},{65,1},{129,65},{193,129... | collective-permute-start | bytes 1966088 | tf_op jit(solution)/shard_map/second_expert/ppermute | solution.py:306
  174.2 2.6 copy-start.8
  191.0 14.7 %collective-permute-start.15 = (bf16[256,1280]{1,0:T(8,128)(2,1)}, bf16[256,1280]{1,0:T(8,128)(2,1)S(1)}, u32[]{:S(2)}, u32[]{:S(2)}) collective-permute-start(bf16[256,1280]{1,0:T(8,128)(2,1)} %get-tuple-element.70), channel_id=1, source_target_pairs={{0,192},{64,0},{128,64},{192,128},{1,193},{65,1},{129,65},{193,129... | collective-permute-start | bytes 1966088 | tf_op jit(solution)/shard_map/sum_blocks/ppermute | solution.py:333
  191.9 16.9 %copy-start.17 = (bf16[256,1280]{1,0:T(8,128)(2,1)S(1)}, bf16[256,1280]{1,0:T(8,128)(2,1)}, u32[]{:S(2)}) copy-start(bf16[256,1280]{1,0:T(8,128)(2,1)} %get-tuple-element.73) | copy-start | bytes 1966084
  191.9 16.8 %collective-permute-start.17 = (bf16[256,1280]{1,0:T(8,128)(2,1)}, bf16[256,1280]{1,0:T(8,128)(2,1)S(1)}, u32[]{:S(2)}, u32[]{:S(2)}) collective-permute-start(bf16[256,1280]{1,0:T(8,128)(2,1)} %get-tuple-element.74), channel_id=1, source_target_pairs={{0,64},{64,128},{128,192},{192,0},{1,65},{65,129},{129,193},{193,1... | collective-permute-start | bytes 1966088 | tf_op jit(solution)/shard_map/sum_blocks/ppermute | solution.py:332
  201.5 31.1 %copy-start.14 = (bf16[256,2304]{1,0:T(8,128)(2,1)S(1)}, bf16[256,2304]{1,0:T(8,128)(2,1)}, u32[]{:S(2)}) copy-start(bf16[256,2304]{1,0:T(8,128)(2,1)} %get-tuple-element.68) | copy-start | bytes 3538948
  205.6 27.0 %collective-permute-start.16 = (bf16[256,2304]{1,0:T(8,128)(2,1)}, bf16[256,2304]{1,0:T(8,128)(2,1)S(1)}, u32[]{:S(2)}, u32[]{:S(2)}) collective-permute-start(bf16[256,2304]{1,0:T(8,128)(2,1)} %get-tuple-element.71), channel_id=1, source_target_pairs={{0,192},{64,0},{128,64},{192,128},{1,193},{65,1},{129,65},{193,129... | collective-permute-start | bytes 3538952 | tf_op jit(solution)/shard_map/sum_blocks/ppermute | solution.py:336
  208.9 15.5 %collective-permute-start.18 = (bf16[256,1280]{1,0:T(8,128)(2,1)S(1)}, bf16[256,1280]{1,0:T(8,128)(2,1)S(1)}, u32[]{:S(2)}, u32[]{:S(2)}) collective-permute-start(bf16[256,1280]{1,0:T(8,128)(2,1)S(1)} %add_convert_fusion.3), channel_id=1, source_target_pairs={{0,64},{64,128},{128,192},{192,0},{1,65},{65,129},{129,193},{193,1... | collective-permute-start | bytes 1966088 | tf_op jit(solution)/shard_map/sum_blocks/ppermute | solution.py:334
  224.4 26.1 %collective-permute-start.19 = (bf16[256,2304]{1,0:T(8,128)(2,1)}, bf16[256,2304]{1,0:T(8,128)(2,1)}, u32[]{:S(2)}, u32[]{:S(2)}) collective-permute-start(bf16[256,2304]{1,0:T(8,128)(2,1)} %get-tuple-element.79), channel_id=1, source_target_pairs={{0,64},{64,128},{128,192},{192,0},{1,65},{65,129},{129,193},{193,1... | collective-permute-start | bytes 3538952 | tf_op jit(solution)/shard_map/sum_blocks/ppermute | solution.py:338
  232.6 3.7 %copy-start.16 = (bf16[256,1280]{1,0:T(8,128)(2,1)S(1)}, bf16[256,1280]{1,0:T(8,128)(2,1)}, u32[]{:S(2)}) copy-start(bf16[256,1280]{1,0:T(8,128)(2,1)} %get-tuple-element.67) | copy-start | bytes 1966084
  232.9 26.0 %collective-permute-start.20 = (bf16[256,2304]{1,0:T(8,128)(2,1)S(1)}, bf16[256,2304]{1,0:T(8,128)(2,1)}, u32[]{:S(2)}, u32[]{:S(2)}) collective-permute-start(bf16[256,2304]{1,0:T(8,128)(2,1)S(1)} %add_convert_fusion.1), channel_id=1, source_target_pairs={{0,192},{64,0},{128,64},{192,128},{1,193},{65,1},{129,65},{193,129... | collective-permute-start | bytes 3538952 | tf_op jit(solution)/shard_map/sum_blocks/ppermute | solution.py:341
  236.5 22.3 %copy-start.15 = (bf16[256,2304]{1,0:T(8,128)(2,1)S(1)}, bf16[256,2304]{1,0:T(8,128)(2,1)}, u32[]{:S(2)}) copy-start(bf16[256,2304]{1,0:T(8,128)(2,1)} %get-tuple-element.78) | copy-start | bytes 3538948
  237.9 29.6 %all-to-all-start.2 = ((bf16[64,4,1280]{2,1,0:T(4,128)(2,1)}), bf16[64,4,1280]{2,1,0:T(4,128)(2,1)S(1)}, u32[]{:S(2)}, u32[]{:S(2)}) async-start(bf16[64,4,1280]{2,1,0:T(4,128)(2,1)} %bitcast.41), calls=%async_computation.2 | async-start | bytes 1310720 | tf_op jit(solution)/shard_map/return_slots/all_to_all | solution.py:349
  267.5 37.6 %all-to-all-start.3 = ((bf16[64,4,2304]{2,1,0:T(4,128)(2,1)}), bf16[64,4,2304]{2,1,0:T(4,128)(2,1)S(1)}, u32[]{:S(2)}, u32[]{:S(2)}) async-start(bf16[64,4,2304]{2,1,0:T(4,128)(2,1)} %bitcast.40), calls=%async_computation.3 | async-start | bytes 2359296 | tf_op jit(solution)/shard_map/return_slots/all_to_all | solution.py:349
  305.1 1.3 copy-start.1
Sparse Core Ops, SparseCore 0:
  18.7 139.8 all-gather.1

commit v8 on v7

--- a/solution.py
+++ b/solution.py
@@ -222,22 +222,29 @@
         value = value + lax.dot_general(h_ref[:, units:], up_ref[e], NT, preferred_element_type=jnp.float32)
         value = value.astype(jnp.bfloat16)
         part = value.shape[0] // 4
-        for r, out_ref in enumerate(out_refs):
-            out_ref[e * part : (e + 1) * part, :] = value[r * part : (r + 1) * part]
-
-
-def out_rows(h, w_gate, w_up, start, stop, step):
+        first = 0
+        for out_ref in out_refs:
+            last = first + out_ref.shape[0]
+            group = first // (2 * part)
+            start, stop = first - group * 2 * part, last - group * 2 * part
+            low, high = max(start, e * part), min(stop, (e + 1) * part)
+            if low < high:
+                at = group * part - e * part
+                out_ref[low - start : high - start, :] = value[at + low : at + high]
+            first = last
+
+
+def out_rows(h, w_gate, w_up, start, stop, step, counts):
     rows = h[0].shape[0]
     local_experts, width, units = w_gate.shape
-    count = local_experts * rows // 4
     h_spec = pl.BlockSpec((rows, 2 * units), lambda n: (0, 0))
     w_spec = pl.BlockSpec((local_experts, step, units), lambda n: (0, start // step + n, 0))
     return pl.pallas_call(
         out_kernel,
-        out_shape=[jax.ShapeDtypeStruct((count, stop - start), jnp.bfloat16)] * 4,
+        out_shape=[jax.ShapeDtypeStruct((count, stop - start), jnp.bfloat16) for count in counts],
         grid=((stop - start) // step,),
         in_specs=[h_spec, h_spec, w_spec, w_spec],
-        out_specs=[pl.BlockSpec((count, step), lambda n: (0, n))] * 4,
+        out_specs=[pl.BlockSpec((count, step), lambda n: (0, n)) for count in counts],
         compiler_params=pltpu.CompilerParams(dimension_semantics=("arbitrary",)),
         cost_estimate=pl.CostEstimate(
             flops=2 * local_experts * rows * 2 * units * (stop - start), bytes_accessed=8 << 20, transcendentals=0
@@ -326,24 +333,32 @@
     hidden1 = hidden_grads(1, second_parts, w_down)
     h = [h0, late_grads(1, second_parts, hidden1, head_pre, w_gate, w_up)]
 
-    own_a, right_a, far_a, left_a = out_rows(h, w_gate, w_up, 0, OUT_SPLIT, 640)
-    own_b, right_b, far_b, left_b = out_rows(h, w_gate, w_up, OUT_SPLIT, width, 256)
+    few, many = slots // 4, slots - slots // 4
+    own_a, right_a, far_a, left_a = out_rows(h, w_gate, w_up, 0, OUT_SPLIT, 640, [slots] * 4)
+    own_b0, own_b1, right_b0, right_b1, far_b0, far_b1, left_b0, left_b1 = out_rows(
+        h, w_gate, w_up, OUT_SPLIT, width, 256, [few, many] * 4
+    )
     with jax.named_scope("sum_blocks"):
         from_far = lax.ppermute(far_a, "dp", up_ring)
         from_right_a = lax.ppermute(left_a, "dp", down_ring)
         from_left_a = lax.ppermute(total(right_a, from_far), "dp", up_ring)
-        far_b, from_right_a = lax.optimization_barrier((far_b, from_right_a))
-        from_far = lax.ppermute(far_b, "dp", down_ring)
-        right_b, from_left_a = lax.optimization_barrier((right_b, from_left_a))
-        from_left_b = lax.ppermute(right_b, "dp", up_ring)
-        left_b = total(left_b, from_far)
-        left_b, from_left_a = lax.optimization_barrier((left_b, from_left_a))
-        from_right_b = lax.ppermute(left_b, "dp", down_ring)
-
+        far_b1, left_b0, from_right_a = lax.optimization_barrier((far_b1, left_b0, from_right_a))
+        from_far1 = lax.ppermute(far_b1, "dp", down_ring)
+        from_right_b0 = lax.ppermute(left_b0, "dp", down_ring)
+        far_b0, right_b1, from_left_a = lax.optimization_barrier((far_b0, right_b1, from_left_a))
+        from_far0 = lax.ppermute(far_b0, "dp", up_ring)
+        from_left_b1 = lax.ppermute(right_b1, "dp", up_ring)
+        left_b1, from_left_a = lax.optimization_barrier((total(left_b1, from_far1), from_left_a))
+        from_right_b1 = lax.ppermute(left_b1, "dp", down_ring)
+        from_left_b0 = lax.ppermute(total(right_b0, from_far0), "dp", up_ring)
+
+    sums_a = total(own_a, from_left_a, from_right_a)
+    sums_b = jnp.concatenate(
+        [total(own_b0, from_left_b0, from_right_b0), total(own_b1, from_left_b1, from_right_b1)], axis=0
+    )
     results = []
-    for terms in ((own_a, from_left_a, from_right_a), (own_b, from_left_b, from_right_b)):
+    for summed in (sums_a, sums_b):
         with jax.named_scope("return_slots"):
-            summed = total(*terms)
             cols = summed.shape[1]
             back = summed.reshape(per_dest, columns, cols).transpose(1, 0, 2)
             returned = lax.all_to_all(back, "expert", split_axis=0, concat_axis=0, tiled=True)

time: 314 us -> 314 us (level)
  waiting for transfers between devices: 171 us -> 162 us
  starting transfers between devices: 61.5 us -> 68.4 us
    ppermute x3 -> x6, waiting for transfers between devices: 19.7 us -> 12.5 us  [the longest x1 10.2 us: on_device(): from_left_b0 = lax.ppermute(total(right_b0, from_far0), 'dp', up_ring)]
    all_to_all x2, starting transfers between devices: 15.7 us -> 19.7 us  [on_device(): lax.all_to_all(back, 'expert', split_axis=0, concat_axis=0, tiled=True)]
    ppermute x3 -> x6, starting transfers between devices: 6.49 us -> 9.26 us  [the longest x1 3.31 us: on_device(): from_right_b1 = lax.ppermute(left_b1, 'dp', down_ring)]
  transfers between devices with their start and end apart: 26 -> 29, of which waited for: 17 -> 16; matrix products, arithmetic and copies ran while one was open for 5% -> 5% of each run, Pallas kernels for 11% -> 11%
where the time goes in v8:
time: 314 us; the launch traced here: 313 us
  waiting for transfers between devices  162 us (52%)
  starting transfers between devices  68.4 us (22%)
  Pallas kernels  47.7 us (15%)
  between operations  13.9 us (4%)
  local copies, waits for them, and re-layouts  10.1 us (3%)
  other arithmetic  8.72 us (3%)
    all_to_all x2, waiting for transfers between devices, send(): lax.all_to_all(slab, 'expert', split_axis=0, concat_axis=0, tiled=True)  43.5 us
    all_to_all x2, waiting for transfers between devices, on_device(): lax.all_to_all(back, 'expert', split_axis=0, concat_axis=0, tiled=True)  36.2 us
    all_to_all x2, starting transfers between devices, on_device(): lax.all_to_all(back, 'expert', split_axis=0, concat_axis=0, tiled=True)  19.7 us
    all_to_all x2, starting transfers between devices, send(): lax.all_to_all(slab, 'expert', split_axis=0, concat_axis=0, tiled=True)  19.1 us
    ppermute x2, waiting for transfers between devices, ring_on(): lax.ppermute(left0, 'dp', up_ring)  16.8 us
    pallas_call x1, Pallas kernels, head_products(): pl.pallas_call(head_kernel, out_shape=[jax.ShapeDtypeStruct((rows, 2 * un...  15.5 us
    ppermute x2, waiting for transfers between devices, ring(): left0 = lax.ppermute(own[0], 'dp', up_ring)  14.2 us
    pallas_call x2, Pallas kernels, out_rows(): pl.pallas_call(out_kernel, out_shape=[jax.ShapeDtypeStruct((count, stop -...  13.8 us
  transfers between devices with their start and end apart: 29, of which 16 were waited for; matrix products, arithmetic and copies ran while one was open for 5% of the time, Pallas kernels for 11%

profile of v8, /device:TPU:1, one launch (start us, length us, event | category | flops | bytes accessed | tf_op | source)
XLA Modules:
  0.0 312.9 jit_solution(2270751530392909323)
XLA Ops:
  6.5 0.9 slice.36
  8.2 3.4 %collective-permute-start = (bf16[16,2176]{1,0:T(8,128)(2,1)S(1)}, bf16[16,2176]{1,0:T(8,128)(2,1)S(1)}, u32[]{:S(2)}, u32[]{:S(2)}) collective-permute-start(bf16[16,2176]{1,0:T(8,128)(2,1)S(1)} %fusion.3), channel_id=1, source_target_pairs={{0,192},{64,0},{128,64},{192,128},{1,193},{65,1},{129,65},{193,129... | collective-permute-start | bytes 208904 | tf_op jit(solution)/shard_map/gather_tokens/ppermute | solution.py:279
  13.9 0.8 select_reduce_fusion.1
  16.5 1.4 reshape.116
  18.6 13.2 %all-to-all-start = ((bf16[64,2,5120]{2,1,0:T(2,128)(2,1)}), bf16[64,2,5120]{2,1,0:T(2,128)(2,1)S(1)}, u32[]{:S(2)}, u32[]{:S(2)}) async-start(bf16[64,2,5120]{2,1,0:T(2,128)(2,1)} %reshape.116), calls=%async_computation | async-start | bytes 2621440 | tf_op jit(solution)/shard_map/first_expert/all_to_all | solution.py:303
  32.7 1.4 reshape.115
  34.1 42.3 %all-to-all-done = bf16[64,2,5120]{2,1,0:T(2,128)(2,1)S(1)} async-done(((bf16[64,2,5120]{2,1,0:T(2,128)(2,1)}), bf16[64,2,5120]{2,1,0:T(2,128)(2,1)S(1)}, u32[]{:S(2)}, u32[]{:S(2)}) %all-to-all-start) | async-done | bytes 1310752 | tf_op jit(solution)/shard_map/first_expert/all_to_all | solution.py:303
  76.8 5.9 %all-to-all-start.1 = ((bf16[64,2,5120]{2,1,0:T(2,128)(2,1)}), bf16[64,2,5120]{2,1,0:T(2,128)(2,1)S(1)}, u32[]{:S(2)}, u32[]{:S(2)}) async-start(bf16[64,2,5120]{2,1,0:T(2,128)(2,1)} %reshape.115), calls=%async_computation.1 | async-start | bytes 2621440 | tf_op jit(solution)/shard_map/second_expert/all_to_all | solution.py:303
  82.7 1.6 collective-permute-start.5
  84.3 1.2 collective-permute-start.4
  87.0 13.0 %collective-permute-done.5.refs_6_ = bf16[64,5120]{1,0:T(8,128)(2,1)S(1)} collective-permute-done((bf16[64,5120]{1,0:T(8,128)(2,1)S(1)}, bf16[64,5120]{1,0:T(8,128)(2,1)S(1)}, u32[]{:S(2)}, u32[]{:S(2)}) %collective-permute-start.5) | collective-permute-done | bytes 655392 | tf_op jit(solution)/shard_map/first_expert/ppermute | solution.py:307
  100.3 2.4 collective-permute-start.8
  102.7 11.3 %collective-permute-done.3.refs_2_ = bf16[64,5120]{1,0:T(8,128)(2,1)S(1)} collective-permute-done((bf16[64,5120]{1,0:T(8,128)(2,1)S(1)}, bf16[64,5120]{1,0:T(8,128)(2,1)S(1)}, u32[]{:S(2)}, u32[]{:S(2)}) %collective-permute-start.3) | collective-permute-done | bytes 655392 | tf_op jit(solution)/shard_map/first_expert/ppermute | solution.py:308
  114.0 14.0 %collective-permute-done.7.refs_4_ = bf16[64,5120]{1,0:T(8,128)(2,1)S(1)} collective-permute-done((bf16[64,5120]{1,0:T(8,128)(2,1)S(1)}, bf16[64,5120]{1,0:T(8,128)(2,1)S(1)}, u32[]{:S(2)}, u32[]{:S(2)}) %collective-permute-start.7) | collective-permute-done | bytes 655392 | tf_op jit(solution)/shard_map/first_expert/ppermute | solution.py:313
  128.1 0.9 copy-done.13
  129.0 1.2 all-to-all-done.1
  130.5 1.5 collective-permute-start.10
  132.5 1.4 collective-permute-start.13
  133.9 1.3 collective-permute-start.14
  135.2 4.6 %tail_products.1.tail_ref = f32[512,512]{1,0:T(8,128)} custom-call(bf16[64,5120]{1,0:T(8,128)(2,1)} %copy-done.5, bf16[64,5120]{1,0:T(8,128)(2,1)} %copy-done.4, bf16[64,5120]{1,0:T(8,128)(2,1)} %copy-done.11, bf16[64,5120]{1,0:T(8,128)(2,1)} %copy-done.10, bf16[64,5120]{1,0:T(8,128)(2,1)} %copy-done.13, bf16[64,5120]{1,0:T(8,128)(2,1)} %collective-permute-done.8.refs_5_, ...), custom_call_target="tpu_custom_call" | custom-call | flops 805306368 | bytes 6291456 | tf_op jit(solution)/shard_map/second_expert/tail_products/pallas_call | solution.py:191
  139.8 4.3 %hidden_grads.2.hidden_ref = f32[512,256]{1,0:T(8,128)} custom-call(bf16[64,5120]{1,0:T(8,128)(2,1)} %copy-done.5, bf16[64,5120]{1,0:T(8,128)(2,1)} %copy-done.4, bf16[64,5120]{1,0:T(8,128)(2,1)} %copy-done.11, bf16[64,5120]{1,0:T(8,128)(2,1)} %copy-done.10, bf16[64,5120]{1,0:T(8,128)(2,1)} %copy-done.13, bf16[64,5120]{1,0:T(8,128)(2,1)} %collective-permute-done.8.refs_5_, ...), custom_call_target="tpu_custom_call" | custom-call | flops 939524096 | bytes 5242880 | tf_op jit(solution)/shard_map/second_expert/hidden_grads/pallas_call | solution.py:135
  144.1 3.5 %collective-permute-done.10.refs_3_ = bf16[64,5120]{1,0:T(8,128)(2,1)S(1)} collective-permute-done((bf16[64,5120]{1,0:T(8,128)(2,1)S(1)}, bf16[64,5120]{1,0:T(8,128)(2,1)S(1)}, u32[]{:S(2)}, u32[]{:S(2)}) %collective-permute-start.10) | collective-permute-done | bytes 655392 | tf_op jit(solution)/shard_map/second_expert/ppermute | solution.py:306
  147.6 1.2 collective-permute-done.9.refs_6_
  149.3 2.3 collective-permute-start.12
  151.5 7.1 %all-gather.2.cloned.1.call-done = bf16[4096,2176]{1,0:T(8,128)(2,1)} async-done(((bf16[64,2176]{1,0:T(8,128)(2,1)}), bf16[4096,2176]{1,0:T(8,128)(2,1)}) %all-gather.2.cloned.1.call-update) | async-done | bytes 17825808 | tf_op jit(solution)/shard_map/gather_tokens/all_gather | solution.py:296
  158.6 15.5 %head_products.1 = (bf16[512,512]{1,0:T(8,128)(2,1)}, f32[512,512]{1,0:T(8,128)}) custom-call(s32[1]{0:T(128)} %bitcast.10.first_ref, bf16[64,4,16,2176]{3,2,1,0:T(8,128)(2,1)} %bitcast.42, bf16[2,3584,256]{2,1,0:T(8,128)(2,1)} %gate_ref.5, bf16[2,3584,256]{2,1,0:T(8,128)(2,1)} %up_ref.5, f32[512,512]{1,0:T(8,128)} %tail_products.1.tail_ref, ...), custom_call_target="tpu_custom_call" | custom-call | flops 2415919104 | bytes 20971520 | tf_op jit(solution)/shard_map/second_expert/head_products/pallas_call | solution.py:88
  174.2 2.8 collective-permute-done.11.refs_4_
  176.9 4.2 %hidden_grads.3.refs_8_ = f32[512,256]{1,0:T(8,128)} custom-call(bf16[64,5120]{1,0:T(8,128)(2,1)} %copy-done.3, bf16[64,5120]{1,0:T(8,128)(2,1)} %copy-done.2, bf16[64,5120]{1,0:T(8,128)(2,1)} %collective-permute-done.14.refs_2_, bf16[64,5120]{1,0:T(8,128)(2,1)} %copy-done.6, bf16[64,5120]{1,0:T(8,128)(2,1)} %collective-permute-done.11.refs_4_, ...), custom_call_target="tpu_custom_call" | custom-call | flops 939524096 | bytes 5242880 | tf_op jit(solution)/shard_map/hidden_grads/pallas_call | solution.py:135
  181.2 5.2 %late_grads.1.h1_ref = bf16[512,512]{1,0:T(8,128)(2,1)} custom-call(bf16[64,5120]{1,0:T(8,128)(2,1)} %copy-done.3, bf16[64,5120]{1,0:T(8,128)(2,1)} %copy-done.2, bf16[64,5120]{1,0:T(8,128)(2,1)} %collective-permute-done.14.refs_2_, bf16[64,5120]{1,0:T(8,128)(2,1)} %copy-done.6, bf16[64,5120]{1,0:T(8,128)(2,1)} %collective-permute-done.11.refs_4_, ...), custom_call_target="tpu_custom_call" | custom-call | flops 805306368 | bytes 6291456 | tf_op jit(solution)/shard_map/late_grads/pallas_call | solution.py:205
  186.4 4.7 %out_rows.2 = (bf16[256,1280]{1,0:T(8,128)(2,1)}, bf16[256,1280]{1,0:T(8,128)(2,1)}, bf16[256,1280]{1,0:T(8,128)(2,1)}, bf16[256,1280]{1,0:T(8,128)(2,1)}) custom-call(bf16[512,512]{1,0:T(8,128)(2,1)} %get-tuple-element.67.h0_ref, bf16[512,512]{1,0:T(8,128)(2,1)} %late_grads.1.h1_ref, bf16[2,3584,256]{2,1,0:T(8,128)(2,1)} %gate_ref.5, ...), custom_call_target="tpu_custom_call" | custom-call | flops 1342177280 | bytes 8388608 | tf_op jit(solution)/shard_map/out_rows/pallas_call | solution.py:242
  191.1 1.0 collective-permute-start.15
  192.5 9.1 %out_rows.3 = (bf16[64,2304]{1,0:T(8,128)(2,1)}, bf16[192,2304]{1,0:T(8,128)(2,1)}, bf16[64,2304]{1,0:T(8,128)(2,1)}, bf16[192,2304]{1,0:T(8,128)(2,1)}, bf16[64...) custom-call(bf16[512,512]{1,0:T(8,128)(2,1)} %get-tuple-element.67.h0_ref, ...), custom_call_target="tpu_custom_call" | custom-call | flops 2415919104 | bytes 8388608 | tf_op jit(solution)/shard_map/out_rows/pallas_call | solution.py:242
  201.6 4.2 %collective-permute-done.15 = bf16[256,1280]{1,0:T(8,128)(2,1)S(1)} collective-permute-done((bf16[256,1280]{1,0:T(8,128)(2,1)}, bf16[256,1280]{1,0:T(8,128)(2,1)S(1)}, u32[]{:S(2)}, u32[]{:S(2)}) %collective-permute-start.15) | collective-permute-done | bytes 655392 | tf_op jit(solution)/shard_map/sum_blocks/ppermute | solution.py:343
  205.9 3.2 %collective-permute-start.16 = (bf16[192,2304]{1,0:T(8,128)(2,1)}, bf16[192,2304]{1,0:T(8,128)(2,1)S(1)}, u32[]{:S(2)}, u32[]{:S(2)}) collective-permute-start(bf16[192,2304]{1,0:T(8,128)(2,1)} %get-tuple-element.78), channel_id=1, source_target_pairs={{0,192},{64,0},{128,64},{192,128},{1,193},{65,1},{129,65},{193,129... | collective-permute-start | bytes 2654216 | tf_op jit(solution)/shard_map/sum_blocks/ppermute | solution.py:346
  209.3 2.7 collective-permute-start.21
  212.0 12.9 %collective-permute-done.18 = bf16[256,1280]{1,0:T(8,128)(2,1)S(1)} collective-permute-done((bf16[256,1280]{1,0:T(8,128)(2,1)S(1)}, bf16[256,1280]{1,0:T(8,128)(2,1)S(1)}, u32[]{:S(2)}, u32[]{:S(2)}) %collective-permute-start.18) | collective-permute-done | bytes 655392 | tf_op jit(solution)/shard_map/sum_blocks/ppermute | solution.py:344
  224.9 1.8 collective-permute-done.16
  226.8 1.2 add_convert_fusion.1
  228.0 3.3 %collective-permute-start.23 = (bf16[192,2304]{1,0:T(8,128)(2,1)}, bf16[192,2304]{1,0:T(8,128)(2,1)}, u32[]{:S(2)}, u32[]{:S(2)}) collective-permute-start(bf16[192,2304]{1,0:T(8,128)(2,1)} %add_convert_fusion.1), channel_id=1, source_target_pairs={{0,192},{64,0},{128,64},{192,128},{1,193},{65,1},{129,65},{193,129... | collective-permute-start | bytes 2654216 | tf_op jit(solution)/shard_map/sum_blocks/ppermute | solution.py:352
  232.2 1.3 copy.64
  233.5 13.5 %all-to-all-start.2 = ((bf16[64,4,1280]{2,1,0:T(4,128)(2,1)}), bf16[64,4,1280]{2,1,0:T(4,128)(2,1)S(1)}, u32[]{:S(2)}, u32[]{:S(2)}) async-start(bf16[64,4,1280]{2,1,0:T(4,128)(2,1)} %bitcast.41), calls=%async_computation.2 | async-start | bytes 1310720 | tf_op jit(solution)/shard_map/return_slots/all_to_all | solution.py:364
  247.0 10.2 %collective-permute-done.20 = bf16[64,2304]{1,0:T(8,128)(2,1)} collective-permute-done((bf16[64,2304]{1,0:T(8,128)(2,1)S(1)}, bf16[64,2304]{1,0:T(8,128)(2,1)}, u32[]{:S(2)}, u32[]{:S(2)}) %collective-permute-start.20) | collective-permute-done | bytes 294944 | tf_op jit(solution)/shard_map/sum_blocks/ppermute | solution.py:353
  257.2 1.1 add_convert_fusion.4
  258.3 1.5 add_convert_fusion
  259.9 1.9 copy.63
  261.8 5.3 %all-to-all-done.2 = bf16[64,4,1280]{2,1,0:T(4,128)(2,1)S(1)} async-done(((bf16[64,4,1280]{2,1,0:T(4,128)(2,1)}), bf16[64,4,1280]{2,1,0:T(4,128)(2,1)S(1)}, u32[]{:S(2)}, u32[]{:S(2)}) %all-to-all-start.2) | async-done | bytes 655392 | tf_op jit(solution)/shard_map/return_slots/all_to_all | solution.py:364
  267.1 6.3 %all-to-all-start.3 = ((bf16[64,4,2304]{2,1,0:T(4,128)(2,1)}), bf16[64,4,2304]{2,1,0:T(4,128)(2,1)S(1)}, u32[]{:S(2)}, u32[]{:S(2)}) async-start(bf16[64,4,2304]{2,1,0:T(4,128)(2,1)} %bitcast.40), calls=%async_computation.3 | async-start | bytes 2359296 | tf_op jit(solution)/shard_map/return_slots/all_to_all | solution.py:364
  273.9 30.9 %all-to-all-done.3 = bf16[64,4,2304]{2,1,0:T(4,128)(2,1)S(1)} async-done(((bf16[64,4,2304]{2,1,0:T(4,128)(2,1)}), bf16[64,4,2304]{2,1,0:T(4,128)(2,1)S(1)}, u32[]{:S(2)}, u32[]{:S(2)}) %all-to-all-start.3) | async-done | bytes 1179680 | tf_op jit(solution)/shard_map/return_slots/all_to_all | solution.py:364
  (112 shorter events, 13.3 us)
Async XLA Ops:
  6.5 9.4 %copy-start = (bf16[16,3584]{1,0:T(8,128)(2,1)S(1)}, bf16[16,3584]{1,0:T(8,128)(2,1)}, u32[]{:S(2)}) copy-start(bf16[16,3584]{1,0:T(8,128)(2,1)} %param.8) | copy-start | bytes 344068
  6.5 9.2 %copy-start.20 = (bf16[16,3584]{1,0:T(8,128)(2,1)S(1)}, bf16[16,3584]{1,0:T(8,128)(2,1)}, u32[]{:S(2)}) copy-start(bf16[16,3584]{1,0:T(8,128)(2,1)} %param.7) | copy-start | bytes 344068
  6.5 152.1 %all-gather.2.cloned.1.call-start = ((), (), s32[]{:S(2)}) async-start(), calls=%async_computation.4 | async-start | bytes 18104320 | tf_op jit(solution)/shard_map/gather_tokens/all_gather | solution.py:296
  8.2 9.6 %collective-permute-start = (bf16[16,2176]{1,0:T(8,128)(2,1)S(1)}, bf16[16,2176]{1,0:T(8,128)(2,1)S(1)}, u32[]{:S(2)}, u32[]{:S(2)}) collective-permute-start(bf16[16,2176]{1,0:T(8,128)(2,1)S(1)} %fusion.3), channel_id=1, source_target_pairs={{0,192},{64,0},{128,64},{192,128},{1,193},{65,1},{129,65},{193,129... | collective-permute-start | bytes 208904 | tf_op jit(solution)/shard_map/gather_tokens/ppermute | solution.py:279
  11.6 6.2 %collective-permute-start.1 = (bf16[16,2176]{1,0:T(8,128)(2,1)S(1)}, bf16[16,2176]{1,0:T(8,128)(2,1)S(1)}, u32[]{:S(2)}, u32[]{:S(2)}) collective-permute-start(bf16[16,2176]{1,0:T(8,128)(2,1)S(1)} %fusion.3), channel_id=1, source_target_pairs={{0,128},{64,192},{128,0},{192,64},{1,129},{65,193},{129,1},{193,65... | collective-permute-start | bytes 208904 | tf_op jit(solution)/shard_map/gather_tokens/ppermute | solution.py:279
  12.1 5.7 %collective-permute-start.2 = (bf16[16,2176]{1,0:T(8,128)(2,1)S(1)}, bf16[16,2176]{1,0:T(8,128)(2,1)S(1)}, u32[]{:S(2)}, u32[]{:S(2)}) collective-permute-start(bf16[16,2176]{1,0:T(8,128)(2,1)S(1)} %fusion.3), channel_id=1, source_target_pairs={{0,64},{64,128},{128,192},{192,0},{1,65},{65,129},{129,193},{193,1... | collective-permute-start | bytes 208904 | tf_op jit(solution)/shard_map/gather_tokens/ppermute | solution.py:279
  18.6 57.8 %all-to-all-start = ((bf16[64,2,5120]{2,1,0:T(2,128)(2,1)}), bf16[64,2,5120]{2,1,0:T(2,128)(2,1)S(1)}, u32[]{:S(2)}, u32[]{:S(2)}) async-start(bf16[64,2,5120]{2,1,0:T(2,128)(2,1)} %reshape.116), calls=%async_computation | async-start | bytes 2621440 | tf_op jit(solution)/shard_map/first_expert/all_to_all | solution.py:303
  76.8 8.7 %copy-start.5 = (bf16[64,5120]{1,0:T(8,128)(2,1)}, bf16[64,5120]{1,0:T(8,128)(2,1)S(1)}, u32[]{:S(2)}) copy-start(bf16[64,5120]{1,0:T(8,128)(2,1)S(1)} %get-tuple-element.100.refs_0_) | copy-start | bytes 1966084
  76.8 9.4 %copy-start.4 = (bf16[64,5120]{1,0:T(8,128)(2,1)}, bf16[64,5120]{1,0:T(8,128)(2,1)S(1)}, u32[]{:S(2)}) copy-start(bf16[64,5120]{1,0:T(8,128)(2,1)S(1)} %get-tuple-element.99.refs_1_) | copy-start | bytes 1966084
  76.8 53.3 %all-to-all-start.1 = ((bf16[64,2,5120]{2,1,0:T(2,128)(2,1)}), bf16[64,2,5120]{2,1,0:T(2,128)(2,1)S(1)}, u32[]{:S(2)}, u32[]{:S(2)}) async-start(bf16[64,2,5120]{2,1,0:T(2,128)(2,1)} %reshape.115), calls=%async_computation.1 | async-start | bytes 2621440 | tf_op jit(solution)/shard_map/second_expert/all_to_all | solution.py:303
  82.7 17.2 %collective-permute-start.5 = (bf16[64,5120]{1,0:T(8,128)(2,1)S(1)}, bf16[64,5120]{1,0:T(8,128)(2,1)S(1)}, u32[]{:S(2)}, u32[]{:S(2)}) collective-permute-start(bf16[64,5120]{1,0:T(8,128)(2,1)S(1)} %get-tuple-element.100.refs_0_), channel_id=1, source_target_pairs={{0,64},{64,128},{128,192},{192,0},{1,65},{65,129},{129,193},{193,1... | collective-permute-start | bytes 1966088 | tf_op jit(solution)/shard_map/first_expert/ppermute | solution.py:307
  84.3 16.0 %collective-permute-start.4 = (bf16[64,5120]{1,0:T(8,128)(2,1)S(1)}, bf16[64,5120]{1,0:T(8,128)(2,1)S(1)}, u32[]{:S(2)}, u32[]{:S(2)}) collective-permute-start(bf16[64,5120]{1,0:T(8,128)(2,1)S(1)} %get-tuple-element.99.refs_1_), channel_id=1, source_target_pairs={{0,192},{64,0},{128,64},{192,128},{1,193},{65,1},{129,65},{193,129... | collective-permute-start | bytes 1966088 | tf_op jit(solution)/shard_map/first_expert/ppermute | solution.py:306
  85.5 28.5 %collective-permute-start.3 = (bf16[64,5120]{1,0:T(8,128)(2,1)S(1)}, bf16[64,5120]{1,0:T(8,128)(2,1)S(1)}, u32[]{:S(2)}, u32[]{:S(2)}) collective-permute-start(bf16[64,5120]{1,0:T(8,128)(2,1)S(1)} %get-tuple-element.100.refs_0_), channel_id=1, source_target_pairs={{0,192},{64,0},{128,64},{192,128},{1,193},{65,1},{129,65},{193,129... | collective-permute-start | bytes 1966088 | tf_op jit(solution)/shard_map/first_expert/ppermute | solution.py:308
  86.2 27.8 %collective-permute-start.6 = (bf16[64,5120]{1,0:T(8,128)(2,1)S(1)}, bf16[64,5120]{1,0:T(8,128)(2,1)S(1)}, u32[]{:S(2)}, u32[]{:S(2)}) collective-permute-start(bf16[64,5120]{1,0:T(8,128)(2,1)S(1)} %get-tuple-element.99.refs_1_), channel_id=1, source_target_pairs={{0,64},{64,128},{128,192},{192,0},{1,65},{65,129},{129,193},{193,1... | collective-permute-start | bytes 1966088 | tf_op jit(solution)/shard_map/first_expert/ppermute | solution.py:309
  100.0 28.1 %copy-start.9 = (bf16[64,5120]{1,0:T(8,128)(2,1)}, bf16[64,5120]{1,0:T(8,128)(2,1)S(1)}, u32[]{:S(2)}) copy-start(bf16[64,5120]{1,0:T(8,128)(2,1)S(1)} %collective-permute-done.5.refs_6_) | copy-start | bytes 1966084
  100.0 28.1 %collective-permute-start.7 = (bf16[64,5120]{1,0:T(8,128)(2,1)S(1)}, bf16[64,5120]{1,0:T(8,128)(2,1)S(1)}, u32[]{:S(2)}, u32[]{:S(2)}) collective-permute-start(bf16[64,5120]{1,0:T(8,128)(2,1)S(1)} %collective-permute-done.5.refs_6_), channel_id=1, source_target_pairs={{0,64},{64,128},{128,192},{192,0},{1,65},{65,129},{129,193},{193,1... | collective-permute-start | bytes 1966088 | tf_op jit(solution)/shard_map/first_expert/ppermute | solution.py:313
  100.3 27.8 %copy-start.10 = (bf16[64,5120]{1,0:T(8,128)(2,1)}, bf16[64,5120]{1,0:T(8,128)(2,1)S(1)}, u32[]{:S(2)}) copy-start(bf16[64,5120]{1,0:T(8,128)(2,1)S(1)} %collective-permute-done.4.refs_3_) | copy-start | bytes 1966084
  100.3 28.7 %collective-permute-start.8 = (bf16[64,5120]{1,0:T(8,128)(2,1)S(1)}, bf16[64,5120]{1,0:T(8,128)(2,1)}, u32[]{:S(2)}, u32[]{:S(2)}) collective-permute-start(bf16[64,5120]{1,0:T(8,128)(2,1)S(1)} %collective-permute-done.4.refs_3_), channel_id=1, source_target_pairs={{0,192},{64,0},{128,64},{192,128},{1,193},{65,1},{129,65},{193,129... | collective-permute-start | bytes 1966088 | tf_op jit(solution)/shard_map/first_expert/ppermute | solution.py:313
  114.0 14.1 %copy-start.11 = (bf16[64,5120]{1,0:T(8,128)(2,1)}, bf16[64,5120]{1,0:T(8,128)(2,1)S(1)}, u32[]{:S(2)}) copy-start(bf16[64,5120]{1,0:T(8,128)(2,1)S(1)} %collective-permute-done.3.refs_2_) | copy-start | bytes 1966084
  114.0 14.1 %copy-start.12 = (bf16[64,5120]{1,0:T(8,128)(2,1)}, bf16[64,5120]{1,0:T(8,128)(2,1)S(1)}, u32[]{:S(2)}) copy-start(bf16[64,5120]{1,0:T(8,128)(2,1)S(1)} %collective-permute-done.6.refs_7_) | copy-start | bytes 1966084
  130.5 9.3 %copy-start.2 = (bf16[64,5120]{1,0:T(8,128)(2,1)}, bf16[64,5120]{1,0:T(8,128)(2,1)S(1)}, u32[]{:S(2)}) copy-start(bf16[64,5120]{1,0:T(8,128)(2,1)S(1)} %get-tuple-element.97.refs_1_) | copy-start | bytes 1966084
  130.5 9.3 %copy-start.3 = (bf16[64,5120]{1,0:T(8,128)(2,1)}, bf16[64,5120]{1,0:T(8,128)(2,1)S(1)}, u32[]{:S(2)}) copy-start(bf16[64,5120]{1,0:T(8,128)(2,1)S(1)} %get-tuple-element.98.refs_0_) | copy-start | bytes 1966084
  130.5 17.1 %collective-permute-start.10 = (bf16[64,5120]{1,0:T(8,128)(2,1)S(1)}, bf16[64,5120]{1,0:T(8,128)(2,1)S(1)}, u32[]{:S(2)}, u32[]{:S(2)}) collective-permute-start(bf16[64,5120]{1,0:T(8,128)(2,1)S(1)} %get-tuple-element.97.refs_1_), channel_id=1, source_target_pairs={{0,192},{64,0},{128,64},{192,128},{1,193},{65,1},{129,65},{193,129... | collective-permute-start | bytes 1966088 | tf_op jit(solution)/shard_map/second_expert/ppermute | solution.py:306
  132.0 16.8 %collective-permute-start.9 = (bf16[64,5120]{1,0:T(8,128)(2,1)S(1)}, bf16[64,5120]{1,0:T(8,128)(2,1)S(1)}, u32[]{:S(2)}, u32[]{:S(2)}) collective-permute-start(bf16[64,5120]{1,0:T(8,128)(2,1)S(1)} %get-tuple-element.98.refs_0_), channel_id=1, source_target_pairs={{0,64},{64,128},{128,192},{192,0},{1,65},{65,129},{129,193},{193,1... | collective-permute-start | bytes 1966088 | tf_op jit(solution)/shard_map/second_expert/ppermute | solution.py:307
  132.5 41.7 %collective-permute-start.13 = (bf16[64,5120]{1,0:T(8,128)(2,1)S(1)}, bf16[64,5120]{1,0:T(8,128)(2,1)S(1)}, u32[]{:S(2)}, u32[]{:S(2)}) collective-permute-start(bf16[64,5120]{1,0:T(8,128)(2,1)S(1)} %get-tuple-element.97.refs_1_), channel_id=1, source_target_pairs={{0,64},{64,128},{128,192},{192,0},{1,65},{65,129},{129,193},{193,1... | collective-permute-start | bytes 1966088 | tf_op jit(solution)/shard_map/second_expert/ppermute | solution.py:309
  133.9 40.3 %collective-permute-start.14 = (bf16[64,5120]{1,0:T(8,128)(2,1)S(1)}, bf16[64,5120]{1,0:T(8,128)(2,1)}, u32[]{:S(2)}, u32[]{:S(2)}) collective-permute-start(bf16[64,5120]{1,0:T(8,128)(2,1)S(1)} %get-tuple-element.98.refs_0_), channel_id=1, source_target_pairs={{0,192},{64,0},{128,64},{192,128},{1,193},{65,1},{129,65},{193,129... | collective-permute-start | bytes 1966088 | tf_op jit(solution)/shard_map/second_expert/ppermute | solution.py:308
  147.6 26.5 %copy-start.6 = (bf16[64,5120]{1,0:T(8,128)(2,1)}, bf16[64,5120]{1,0:T(8,128)(2,1)S(1)}, u32[]{:S(2)}) copy-start(bf16[64,5120]{1,0:T(8,128)(2,1)S(1)} %collective-permute-done.10.refs_3_) | copy-start | bytes 1966084
  148.9 25.3 %copy-start.7 = (bf16[64,5120]{1,0:T(8,128)(2,1)}, bf16[64,5120]{1,0:T(8,128)(2,1)S(1)}, u32[]{:S(2)}) copy-start(bf16[64,5120]{1,0:T(8,128)(2,1)S(1)} %collective-permute-done.9.refs_6_) | copy-start | bytes 1966084
  148.9 28.1 %collective-permute-start.11 = (bf16[64,5120]{1,0:T(8,128)(2,1)S(1)}, bf16[64,5120]{1,0:T(8,128)(2,1)}, u32[]{:S(2)}, u32[]{:S(2)}) collective-permute-start(bf16[64,5120]{1,0:T(8,128)(2,1)S(1)} %collective-permute-done.9.refs_6_), channel_id=1, source_target_pairs={{0,64},{64,128},{128,192},{192,0},{1,65},{65,129},{129,193},{193,1... | collective-permute-start | bytes 1966088 | tf_op jit(solution)/shard_map/second_expert/ppermute | solution.py:313
  149.3 27.7 %collective-permute-start.12 = (bf16[64,5120]{1,0:T(8,128)(2,1)S(1)}, bf16[64,5120]{1,0:T(8,128)(2,1)}, u32[]{:S(2)}, u32[]{:S(2)}) collective-permute-start(bf16[64,5120]{1,0:T(8,128)(2,1)S(1)} %collective-permute-done.10.refs_3_), channel_id=1, source_target_pairs={{0,192},{64,0},{128,64},{192,128},{1,193},{65,1},{129,65},{193,129... | collective-permute-start | bytes 1966088 | tf_op jit(solution)/shard_map/second_expert/ppermute | solution.py:313
  191.1 14.8 %collective-permute-start.15 = (bf16[256,1280]{1,0:T(8,128)(2,1)}, bf16[256,1280]{1,0:T(8,128)(2,1)S(1)}, u32[]{:S(2)}, u32[]{:S(2)}) collective-permute-start(bf16[256,1280]{1,0:T(8,128)(2,1)} %get-tuple-element.77), channel_id=1, source_target_pairs={{0,192},{64,0},{128,64},{192,128},{1,193},{65,1},{129,65},{193,129... | collective-permute-start | bytes 1966088 | tf_op jit(solution)/shard_map/sum_blocks/ppermute | solution.py:343
  192.0 17.0 %copy-start.17 = (bf16[256,1280]{1,0:T(8,128)(2,1)S(1)}, bf16[256,1280]{1,0:T(8,128)(2,1)}, u32[]{:S(2)}) copy-start(bf16[256,1280]{1,0:T(8,128)(2,1)} %get-tuple-element.81) | copy-start | bytes 1966084
  192.1 17.0 %collective-permute-start.17 = (bf16[256,1280]{1,0:T(8,128)(2,1)}, bf16[256,1280]{1,0:T(8,128)(2,1)S(1)}, u32[]{:S(2)}, u32[]{:S(2)}) collective-permute-start(bf16[256,1280]{1,0:T(8,128)(2,1)} %get-tuple-element.82), channel_id=1, source_target_pairs={{0,64},{64,128},{128,192},{192,0},{1,65},{65,129},{129,193},{193,1... | collective-permute-start | bytes 1966088 | tf_op jit(solution)/shard_map/sum_blocks/ppermute | solution.py:342
  201.6 23.3 %copy-start.21 = (bf16[64,2304]{1,0:T(8,128)(2,1)S(1)}, bf16[64,2304]{1,0:T(8,128)(2,1)}, u32[]{:S(2)}) copy-start(bf16[64,2304]{1,0:T(8,128)(2,1)} %get-tuple-element.88) | copy-start | bytes 884740
  201.6 25.2 %copy-start.15 = (bf16[192,2304]{1,0:T(8,128)(2,1)S(1)}, bf16[192,2304]{1,0:T(8,128)(2,1)}, u32[]{:S(2)}) copy-start(bf16[192,2304]{1,0:T(8,128)(2,1)} %get-tuple-element.74) | copy-start | bytes 2654212
  205.9 20.9 %collective-permute-start.16 = (bf16[192,2304]{1,0:T(8,128)(2,1)}, bf16[192,2304]{1,0:T(8,128)(2,1)S(1)}, u32[]{:S(2)}, u32[]{:S(2)}) collective-permute-start(bf16[192,2304]{1,0:T(8,128)(2,1)} %get-tuple-element.78), channel_id=1, source_target_pairs={{0,192},{64,0},{128,64},{192,128},{1,193},{65,1},{129,65},{193,129... | collective-permute-start | bytes 2654216 | tf_op jit(solution)/shard_map/sum_blocks/ppermute | solution.py:346
  209.2 15.7 %collective-permute-start.18 = (bf16[256,1280]{1,0:T(8,128)(2,1)S(1)}, bf16[256,1280]{1,0:T(8,128)(2,1)S(1)}, u32[]{:S(2)}, u32[]{:S(2)}) collective-permute-start(bf16[256,1280]{1,0:T(8,128)(2,1)S(1)} %add_convert_fusion.3), channel_id=1, source_target_pairs={{0,64},{64,128},{128,192},{192,0},{1,65},{65,129},{129,193},{193,1... | collective-permute-start | bytes 1966088 | tf_op jit(solution)/shard_map/sum_blocks/ppermute | solution.py:344
  209.3 37.7 %collective-permute-start.21 = (bf16[64,2304]{1,0:T(8,128)(2,1)}, bf16[64,2304]{1,0:T(8,128)(2,1)S(1)}, u32[]{:S(2)}, u32[]{:S(2)}) collective-permute-start(bf16[64,2304]{1,0:T(8,128)(2,1)} %get-tuple-element.89), channel_id=1, source_target_pairs={{0,192},{64,0},{128,64},{192,128},{1,193},{65,1},{129,65},{193,129... | collective-permute-start | bytes 884744 | tf_op jit(solution)/shard_map/sum_blocks/ppermute | solution.py:347
  224.9 6.8 %collective-permute-start.19 = (bf16[64,2304]{1,0:T(8,128)(2,1)S(1)}, bf16[64,2304]{1,0:T(8,128)(2,1)S(1)}, u32[]{:S(2)}, u32[]{:S(2)}) collective-permute-start(bf16[64,2304]{1,0:T(8,128)(2,1)S(1)} %copy-done.21), channel_id=1, source_target_pairs={{0,64},{64,128},{128,192},{192,0},{1,65},{65,129},{129,193},{193,1... | collective-permute-start | bytes 884744 | tf_op jit(solution)/shard_map/sum_blocks/ppermute | solution.py:349
  224.9 33.3 %collective-permute-start.22 = (bf16[192,2304]{1,0:T(8,128)(2,1)}, bf16[192,2304]{1,0:T(8,128)(2,1)S(1)}, u32[]{:S(2)}, u32[]{:S(2)}) collective-permute-start(bf16[192,2304]{1,0:T(8,128)(2,1)} %get-tuple-element.91), channel_id=1, source_target_pairs={{0,64},{64,128},{128,192},{192,0},{1,65},{65,129},{129,193},{193,1... | collective-permute-start | bytes 2654216 | tf_op jit(solution)/shard_map/sum_blocks/ppermute | solution.py:350
  226.8 4.9 %copy-start.18 = (bf16[64,2304]{1,0:T(8,128)(2,1)S(1)}, bf16[64,2304]{1,0:T(8,128)(2,1)}, u32[]{:S(2)}) copy-start(bf16[64,2304]{1,0:T(8,128)(2,1)} %get-tuple-element.87) | copy-start | bytes 884740
  226.8 5.1 %copy-start.16 = (bf16[256,1280]{1,0:T(8,128)(2,1)S(1)}, bf16[256,1280]{1,0:T(8,128)(2,1)}, u32[]{:S(2)}) copy-start(bf16[256,1280]{1,0:T(8,128)(2,1)} %get-tuple-element.73) | copy-start | bytes 1966084
  228.0 30.3 %collective-permute-start.23 = (bf16[192,2304]{1,0:T(8,128)(2,1)}, bf16[192,2304]{1,0:T(8,128)(2,1)}, u32[]{:S(2)}, u32[]{:S(2)}) collective-permute-start(bf16[192,2304]{1,0:T(8,128)(2,1)} %add_convert_fusion.1), channel_id=1, source_target_pairs={{0,192},{64,0},{128,64},{192,128},{1,193},{65,1},{129,65},{193,129... | collective-permute-start | bytes 2654216 | tf_op jit(solution)/shard_map/sum_blocks/ppermute | solution.py:352
  231.8 25.4 %collective-permute-start.20 = (bf16[64,2304]{1,0:T(8,128)(2,1)S(1)}, bf16[64,2304]{1,0:T(8,128)(2,1)}, u32[]{:S(2)}, u32[]{:S(2)}) collective-permute-start(bf16[64,2304]{1,0:T(8,128)(2,1)S(1)} %add_convert_fusion.5), channel_id=1, source_target_pairs={{0,64},{64,128},{128,192},{192,0},{1,65},{65,129},{129,193},{193,1... | collective-permute-start | bytes 884744 | tf_op jit(solution)/shard_map/sum_blocks/ppermute | solution.py:353
  232.2 25.0 %copy-start.19 = (bf16[64,2304]{1,0:T(8,128)(2,1)S(1)}, bf16[64,2304]{1,0:T(8,128)(2,1)}, u32[]{:S(2)}) copy-start(bf16[64,2304]{1,0:T(8,128)(2,1)} %get-tuple-element.86) | copy-start | bytes 884740
  233.5 24.7 %copy-start.14 = (bf16[192,2304]{1,0:T(8,128)(2,1)S(1)}, bf16[192,2304]{1,0:T(8,128)(2,1)}, u32[]{:S(2)}) copy-start(bf16[192,2304]{1,0:T(8,128)(2,1)} %get-tuple-element.90) | copy-start | bytes 2654212
  233.5 33.6 %all-to-all-start.2 = ((bf16[64,4,1280]{2,1,0:T(4,128)(2,1)}), bf16[64,4,1280]{2,1,0:T(4,128)(2,1)S(1)}, u32[]{:S(2)}, u32[]{:S(2)}) async-start(bf16[64,4,1280]{2,1,0:T(4,128)(2,1)} %bitcast.41), calls=%async_computation.2 | async-start | bytes 1310720 | tf_op jit(solution)/shard_map/return_slots/all_to_all | solution.py:364
  267.1 37.6 %all-to-all-start.3 = ((bf16[64,4,2304]{2,1,0:T(4,128)(2,1)}), bf16[64,4,2304]{2,1,0:T(4,128)(2,1)S(1)}, u32[]{:S(2)}, u32[]{:S(2)}) async-start(bf16[64,4,2304]{2,1,0:T(4,128)(2,1)} %bitcast.40), calls=%async_computation.3 | async-start | bytes 2359296 | tf_op jit(solution)/shard_map/return_slots/all_to_all | solution.py:364
  (3 other events, 5.0 us)
Sparse Core Ops, SparseCore 0:
  18.7 139.8 all-gather.1
